TPU v7x, 32 devices: a whole 2x2x4 slice. The times are simulated.
32 devices in a mesh: replica: 4 (over x, core), fsdp: 8 (over z, y).
Axes of the slice: x: 2, y: 2, z: 4, core: 2. Of those that a mesh axis runs over, the one named last changes fastest.
Arguments:
- tokens: bfloat16 [8192, 768], P(('replica', 'fsdp')), may hold values from -6 to 6
- cotangent: bfloat16 [8192, 768], P(('replica', 'fsdp')), may hold values from -6 to 6
- lengths: int32 [64], P(('replica', 'fsdp')), may hold values from 32 to 128, as said below
- routes: int32 [8192, 2], P(('replica', 'fsdp')), may hold values from 0 to 3, as said below
- slots: int32 [8192, 2], P(('replica', 'fsdp')), may hold values from 0 to 63, as said below
- gain_attn: bfloat16 [768], P('fsdp'), may hold values from 0.5 to 1.5
- w_qkv: bfloat16 [768, 2304], P('fsdp'), may hold values from -0.21875 to 0.21875
- w_proj: bfloat16 [768, 768], P('fsdp'), may hold values from -0.875 to 0.875
- rel_table: bfloat16 [128, 12], P('fsdp'), may hold values from -4 to 4
- gain_moe: bfloat16 [768], P('fsdp'), may hold values from 0.5 to 1.5
- w_router: bfloat16 [768, 4], P('fsdp'), may hold values from -0.21875 to 0.21875
- w_up: bfloat16 [8, 768, 1536], P('fsdp'), may hold values from -0.21875 to 0.21875
- w_down: bfloat16 [8, 1536, 768], P('fsdp'), may hold values from -0.109375 to 0.109375
Outputs:
- mixed: bfloat16 [8192, 768], P(('replica', 'fsdp'))
- grad_tokens: float32 [8192, 768], P(('replica', 'fsdp'))
- grad_gain_attn: float32 [768], P('fsdp')
- grad_w_qkv: float32 [768, 2304], P('fsdp')
- grad_w_proj: float32 [768, 768], P('fsdp')
- grad_rel_table: float32 [128, 12], P('fsdp')
- grad_gain_moe: float32 [768], P('fsdp')
- grad_w_router: float32 [768, 4], P('fsdp')
- grad_w_up: float32 [8, 768, 1536], P('fsdp')
- grad_w_down: float32 [8, 1536, 768], P('fsdp')
Inputs may be any that keep to these rules, and one draw needn't show every extreme that they name: `lengths`: each sequence's live slots come first; one sequence has all 128 slots live. Each slot names two different experts. Within one sequence's 128 slots, padded ones included, every expert is named by exactly 64 routes. Routes of slots that are not live are ignored. Within one sequence, the routes to one expert have distinct slots; a first route's slot is below 32, a second route's slot is 32 or more.
All inputs are finite; a program needn't handle non-finite values.
Results may differ from a plain program's by a relative error of at most 0.012.
Values may be sent and summed in bfloat16 or wider, within the bound.
A program may use at most 192 MiB of HBM per device.

v0:
```python
import jax
import jax.numpy as jnp
from jax import lax
from jax.sharding import PartitionSpec as P

D = 768
HEADS = 12
HEAD = 64
FF = 3072
SEQ = 128
MB = 2


epsilon = 1e-06
exact_precision = lax.Precision.HIGHEST


def rms_norm(values, gain):
    factor = lax.rsqrt(jnp.mean(values * values, axis=-1, keepdims=True) + epsilon)
    return values * factor * gain


def bias_matrix(table):
    length = table.shape[0]
    places = jnp.arange(length, dtype=jnp.int32)
    distance = jnp.clip(places[:, None] - places[None, :], 0, length - 1)
    return jnp.transpose(table[distance], (2, 0, 1))


def exact_gelu(values):
    return jax.nn.gelu(values, approximate=False)


def masked_scores(qkv_rows, table, allowed, factor):
    raw = jnp.einsum(
        "qhd,khd->hqk", qkv_rows[:, 0], qkv_rows[:, 1], preferred_element_type=jnp.float32
    )
    return jnp.where(allowed[None], raw * factor + bias_matrix(table), -1e30)


def fetch_weights(gain_attn, w_qkv, w_proj, rel_table, gain_moe, w_router):
    return (
        lax.all_gather(gain_attn, "fsdp", axis=0, tiled=True),
        lax.all_gather(w_qkv, "fsdp", axis=0, tiled=True),
        lax.all_gather(w_proj, "fsdp", axis=0, tiled=True),
        lax.all_gather(rel_table, "fsdp", axis=0, tiled=True),
        lax.all_gather(gain_moe, "fsdp", axis=0, tiled=True),
        lax.all_gather(w_router, "fsdp", axis=0, tiled=True),
    )


def body(
    tokens,
    cotangent,
    lengths,
    routes,
    slots,
    gain_attn,
    w_qkv,
    w_proj,
    rel_table,
    gain_moe,
    w_router,
    w_up,
    w_down,
):
    groups = lax.axis_size("fsdp")
    experts = groups // 2
    capacity = 2 * SEQ // experts
    factor = HEAD ** (-0.5)
    up_weight = w_up[0]
    down_weight = w_down[0]
    places = jnp.arange(SEQ, dtype=jnp.int32)
    causal = places[:, None] >= places[None, :]
    expert_ids = jnp.arange(experts, dtype=jnp.int32)
    saved = []
    mixed_parts = []
    for batch in range(MB):
        weights = fetch_weights(gain_attn, w_qkv, w_proj, rel_table, gain_moe, w_router)
        gain_a = weights[0].astype(jnp.float32)
        table = weights[3].astype(jnp.float32)
        gain_m = weights[4].astype(jnp.float32)
        x_float = tokens[batch * SEQ : (batch + 1) * SEQ].astype(jnp.float32)
        live_keys = places < lengths[batch]
        live_col = live_keys.astype(jnp.float32)[:, None]
        allowed = causal & live_keys[None, :]
        normed = rms_norm(x_float, gain_a).astype(jnp.bfloat16)
        qkv_rows = (
            jnp.dot(normed, weights[1], preferred_element_type=jnp.float32)
            .astype(jnp.bfloat16)
            .reshape(SEQ, 3, HEADS, HEAD)
        )
        scores = masked_scores(qkv_rows, table, allowed, factor)
        row_peak = jnp.max(scores, axis=-1, keepdims=True)
        exp_scores = jnp.exp(scores - row_peak)
        row_total = jnp.sum(exp_scores, axis=-1, keepdims=True)
        log_total = row_peak + jnp.log(row_total)
        probs_low = (exp_scores / row_total).astype(jnp.bfloat16)
        attended = jnp.einsum(
            "hqk,khd->qhd", probs_low, qkv_rows[:, 2], preferred_element_type=jnp.float32
        )
        attended = attended.astype(jnp.bfloat16).reshape(SEQ, D)
        branch = jnp.dot(attended, weights[2], preferred_element_type=jnp.float32)
        hidden = x_float + live_col * branch
        normed2 = rms_norm(hidden, gain_m).astype(jnp.bfloat16)
        logits = jnp.dot(normed2, weights[5], preferred_element_type=jnp.float32)
        route_rows = routes[batch * SEQ : (batch + 1) * SEQ]
        slot_rows = slots[batch * SEQ : (batch + 1) * SEQ]
        hot_first = (route_rows[:, 0:1] == expert_ids[None, :]).astype(jnp.float32)
        hot_second = (route_rows[:, 1:2] == expert_ids[None, :]).astype(jnp.float32)
        gate_first = jax.nn.sigmoid(
            jnp.sum(logits * hot_first, axis=-1) - jnp.sum(logits * hot_second, axis=-1)
        )
        row_place = route_rows * capacity + slot_rows
        target = jnp.where(live_keys[:, None], row_place, experts * capacity)
        outgoing = jnp.zeros((experts * capacity, D), jnp.bfloat16)
        outgoing = (
            outgoing.at[target[:, 0]]
            .set(normed2, mode="drop")
            .at[target[:, 1]]
            .set(normed2, mode="drop")
        )
        outgoing = jnp.repeat(outgoing.reshape(experts, capacity, D), 2, axis=0)
        expert_received = lax.all_to_all(outgoing, "fsdp", split_axis=0, concat_axis=0, tiled=True)
        expert_before = jnp.einsum(
            "scd,df->scf", expert_received, up_weight, preferred_element_type=jnp.float32
        )
        expert_active = exact_gelu(expert_before).astype(jnp.bfloat16)
        partial_value = jnp.einsum(
            "scf,fd->scd", expert_active, down_weight, preferred_element_type=jnp.float32
        ).astype(jnp.bfloat16)
        returned = lax.all_to_all(partial_value, "fsdp", split_axis=0, concat_axis=0, tiled=True)
        results = (returned, expert_received, expert_before)
        combined = (
            results[0]
            .astype(jnp.float32)
            .reshape(experts, 2, capacity, D)
            .sum(axis=1)
            .reshape(experts * capacity, D)
        )
        first_out = combined[row_place[:, 0]]
        second_out = combined[row_place[:, 1]]
        moe = live_col * (
            gate_first[:, None] * first_out + (1.0 - gate_first)[:, None] * second_out
        )
        mixed_parts.append((hidden + moe).astype(jnp.bfloat16))
        saved.append(
            {
                "normed": normed,
                "qkv_rows": qkv_rows,
                "log_total": log_total,
                "attended": attended,
                "hidden": hidden,
                "normed2": normed2,
                "gate_first": gate_first,
                "first_out": first_out,
                "second_out": second_out,
                "results": results,
                "target": target,
                "row_place": row_place,
                "hot_first": hot_first,
                "hot_second": hot_second,
            }
        )
    grad_qkv_w = jnp.zeros((D, 3 * D), jnp.float32)
    grad_proj_w = jnp.zeros((D, D), jnp.float32)
    grad_table = jnp.zeros((SEQ, HEADS), jnp.float32)
    grad_gain_a = jnp.zeros((D,), jnp.float32)
    grad_gain_m = jnp.zeros((D,), jnp.float32)
    grad_router = jnp.zeros((D, experts), jnp.float32)
    grad_up = jnp.zeros((D, FF // 2), jnp.float32)
    grad_down = jnp.zeros((FF // 2, D), jnp.float32)
    grad_parts = [None] * MB
    for batch in reversed(range(MB)):
        kept = saved[batch]
        weights = fetch_weights(gain_attn, w_qkv, w_proj, rel_table, gain_moe, w_router)
        gain_a = weights[0].astype(jnp.float32)
        table = weights[3].astype(jnp.float32)
        gain_m = weights[4].astype(jnp.float32)
        router_float = weights[5].astype(jnp.float32)
        x_float = tokens[batch * SEQ : (batch + 1) * SEQ].astype(jnp.float32)
        live_keys = places < lengths[batch]
        live_col = live_keys.astype(jnp.float32)[:, None]
        allowed = causal & live_keys[None, :]
        grad_out = cotangent[batch * SEQ : (batch + 1) * SEQ].astype(jnp.float32)
        grad_moe = live_col * grad_out
        gate_first = kept["gate_first"]
        gate_second = 1.0 - gate_first
        grad_gate_first = jnp.sum(grad_moe * kept["first_out"], axis=-1)
        grad_gate_second = jnp.sum(grad_moe * kept["second_out"], axis=-1)
        grad_first = (gate_first[:, None] * grad_moe).astype(jnp.bfloat16)
        grad_second = (gate_second[:, None] * grad_moe).astype(jnp.bfloat16)
        target = kept["target"]
        grad_send = jnp.zeros((experts * capacity, D), jnp.bfloat16)
        grad_send = (
            grad_send.at[target[:, 0]]
            .set(grad_first, mode="drop")
            .at[target[:, 1]]
            .set(grad_second, mode="drop")
        )
        grad_send = jnp.repeat(grad_send.reshape(experts, capacity, D), 2, axis=0)
        grad_recv = lax.all_to_all(grad_send, "fsdp", split_axis=0, concat_axis=0, tiled=True)
        received = kept["results"][1]
        before = kept["results"][2]
        active, gelu_back = jax.vjp(exact_gelu, before)
        active_low = active.astype(jnp.bfloat16)
        grad_active = jnp.einsum(
            "scd,fd->scf", grad_recv, down_weight, preferred_element_type=jnp.float32
        )
        grad_before = gelu_back(grad_active)[0].astype(jnp.bfloat16)
        grad_down = grad_down + jnp.einsum(
            "scf,scd->fd", active_low, grad_recv, preferred_element_type=jnp.float32
        )
        grad_up = grad_up + jnp.einsum(
            "scd,scf->df", received, grad_before, preferred_element_type=jnp.float32
        )
        grad_part = jnp.einsum(
            "scf,df->scd", grad_before, up_weight, preferred_element_type=jnp.float32
        ).astype(jnp.bfloat16)
        grad_back = lax.all_to_all(grad_part, "fsdp", split_axis=0, concat_axis=0, tiled=True)
        grad_rows = (
            grad_back.astype(jnp.float32)
            .reshape(experts, 2, capacity, D)
            .sum(axis=1)
            .reshape(experts * capacity, D)
        )
        row_place = kept["row_place"]
        grad_diff = (grad_gate_first - grad_gate_second) * gate_first * gate_second
        grad_logits = grad_diff[:, None] * (kept["hot_first"] - kept["hot_second"])
        normed2_float = kept["normed2"].astype(jnp.float32)
        grad_router = grad_router + jnp.dot(normed2_float.T, grad_logits, precision=exact_precision)
        grad_normed2 = live_col * (grad_rows[row_place[:, 0]] + grad_rows[row_place[:, 1]])
        grad_normed2 = grad_normed2 + jnp.dot(
            grad_logits, router_float.T, precision=exact_precision
        )
        _, norm_back_moe = jax.vjp(rms_norm, kept["hidden"], gain_m)
        grad_hidden_norm, grad_gain_part = norm_back_moe(grad_normed2)
        grad_gain_m = grad_gain_m + grad_gain_part
        grad_hidden = grad_out + grad_hidden_norm
        grad_branch = (live_col * grad_hidden).astype(jnp.bfloat16)
        grad_proj_w = grad_proj_w + jnp.einsum(
            "sd,se->de", kept["attended"], grad_branch, preferred_element_type=jnp.float32
        )
        grad_attended = jnp.einsum(
            "se,de->sd", grad_branch, weights[2], preferred_element_type=jnp.float32
        )
        grad_attended = grad_attended.astype(jnp.bfloat16).reshape(SEQ, HEADS, HEAD)
        qkv_rows = kept["qkv_rows"]
        scores = masked_scores(qkv_rows, table, allowed, factor)
        probs = jnp.exp(scores - kept["log_total"])
        probs_low = probs.astype(jnp.bfloat16)
        grad_probs = jnp.einsum(
            "qhd,khd->hqk", grad_attended, qkv_rows[:, 2], preferred_element_type=jnp.float32
        )
        row_dot = jnp.sum(probs * grad_probs, axis=-1, keepdims=True)
        grad_scores = (probs * (grad_probs - row_dot)).astype(jnp.bfloat16)
        _, bias_back = jax.vjp(bias_matrix, table)
        grad_table = grad_table + bias_back(grad_scores.astype(jnp.float32))[0]
        grad_queries = (
            jnp.einsum(
                "hqk,khd->qhd", grad_scores, qkv_rows[:, 1], preferred_element_type=jnp.float32
            )
            * factor
        )
        grad_keys = (
            jnp.einsum(
                "hqk,qhd->khd", grad_scores, qkv_rows[:, 0], preferred_element_type=jnp.float32
            )
            * factor
        )
        grad_values = jnp.einsum(
            "hqk,qhd->khd", probs_low, grad_attended, preferred_element_type=jnp.float32
        )
        grad_qkv = (
            jnp.stack([grad_queries, grad_keys, grad_values], axis=1)
            .astype(jnp.bfloat16)
            .reshape(SEQ, 3 * D)
        )
        grad_qkv_w = grad_qkv_w + jnp.einsum(
            "sd,se->de", kept["normed"], grad_qkv, preferred_element_type=jnp.float32
        )
        grad_normed = jnp.einsum(
            "se,de->sd", grad_qkv, weights[1], preferred_element_type=jnp.float32
        )
        _, norm_back_attn = jax.vjp(rms_norm, x_float, gain_a)
        grad_x_norm, grad_gain_piece = norm_back_attn(grad_normed)
        grad_gain_a = grad_gain_a + grad_gain_piece
        grad_parts[batch] = grad_hidden + grad_x_norm
    shards = (
        lax.psum_scatter(grad_gain_a, "fsdp", scatter_dimension=0, tiled=True),
        lax.psum_scatter(grad_qkv_w, "fsdp", scatter_dimension=0, tiled=True),
        lax.psum_scatter(grad_proj_w, "fsdp", scatter_dimension=0, tiled=True),
        lax.psum_scatter(grad_table, "fsdp", scatter_dimension=0, tiled=True),
        lax.psum_scatter(grad_gain_m, "fsdp", scatter_dimension=0, tiled=True),
        lax.psum_scatter(grad_router, "fsdp", scatter_dimension=0, tiled=True),
    )
    totals = lax.psum(
        (
            shards[0],
            shards[1],
            shards[2],
            shards[3],
            shards[4],
            shards[5],
            grad_up[None],
            grad_down[None],
        ),
        "replica",
    )
    mixed = jnp.concatenate(mixed_parts, axis=0)
    grad_tokens = jnp.concatenate(grad_parts, axis=0)
    return (
        mixed,
        grad_tokens,
        totals[0],
        totals[1],
        totals[2],
        totals[3],
        totals[4],
        totals[5],
        totals[6],
        totals[7],
    )


def solution(mesh):
    in_specs = (
        P(("replica", "fsdp"), None),
        P(("replica", "fsdp"), None),
        P(("replica", "fsdp")),
        P(("replica", "fsdp"), None),
        P(("replica", "fsdp"), None),
        P("fsdp"),
        P("fsdp", None),
        P("fsdp", None),
        P("fsdp", None),
        P("fsdp"),
        P("fsdp", None),
        P("fsdp", None, None),
        P("fsdp", None, None),
    )
    out_specs = (
        P(("replica", "fsdp"), None),
        P(("replica", "fsdp"), None),
        P("fsdp"),
        P("fsdp", None),
        P("fsdp", None),
        P("fsdp", None),
        P("fsdp"),
        P("fsdp", None),
        P("fsdp", None, None),
        P("fsdp", None, None),
    )
    return jax.shard_map(body, mesh=mesh, in_specs=in_specs, out_specs=out_specs, check_vma=False)
```

profile of v0, /device:TPU:0, one launch (start us, length us, event | category | flops | bytes accessed | tf_op | source)
XLA Modules:
  0.0 918.5 jit_solution(17957541413443993401)
XLA Ops:
  13.8 33.2 %all_gather.14 = bf16[128,12]{1,0:T(8,128)(2,1)S(1)} all-gather(bf16[16,12]{1,0:T(8,128)(2,1)} %param.21), channel_id=1, replica_groups=mesh['replica'=4,'fsdp'=8] {'fsdp'}, dimensions={0}, use_global_device_ids=true | all-gather | bytes 3456 | tf_op jit(solution)/shard_map/all_gather | solution.py:46
  47.0 54.8 %gather_fusion = f32[16384,12]{1,0:T(8,128)} fusion(f32[128,12]{1,0:T(8,128)S(1)} %convert_element_type.201, s32[16384]{0:T(1024)S(1)} %broadcast_clamp_fusion), kind=kCustom, calls=%fused_computation | custom fusion | bytes 1638400 | tf_op jit(solution)/shard_map/gather | solution.py:27
  101.8 7.5 copy.64
  111.9 21.3 %all-reduce.7 = (bf16[768]{0:T(1024)(128)(2,1)S(1)}, bf16[768]{0:T(1024)(128)(2,1)S(1)}) all-reduce(bf16[768]{0:T(1024)(128)(2,1)S(1)} %dynamic-update-slice, bf16[768]{0:T(1024)(128)(2,1)S(1)} %dynamic-update-slice.1), channel_id=1, replica_groups=mesh['replica'=4,'fsdp'=8] {'fsdp'}, use_global_device_ids=true, to_apply=%add | all-reduce | flops 1536 | bytes 6144
  135.1 3.5 convolution_convert_fusion
  139.9 3.7 convolution_convert_fusion.1
  147.0 2.6 fusion.177
  161.7 4.2 all-to-all-start
  165.9 22.4 %all-gather = bf16[8,96,4]{1,2,0:T(4,128)(2,1)S(1)} all-gather(bf16[1,96,4]{1,2,0:T(4,128)(2,1)} %bitcast.327), channel_id=1, replica_groups=mesh['replica'=4,'fsdp'=8] {'fsdp'}, dimensions={0}, use_global_device_ids=true | all-gather | bytes 6912 | tf_op jit(solution)/shard_map/all_gather | solution.py:48
  192.7 4.6 all-to-all-start.2
  197.4 3.2 fusion.66
  200.6 7.9 multiply_convert_fusion.1
  213.6 7.6 all-to-all-start.1
  221.2 3.2 fusion.67
  224.4 7.9 multiply_convert_fusion
  235.8 5.3 all-to-all-done.1
  241.0 5.3 all-to-all-start.3
  267.5 2.8 scatter_custom_fusion.6
  270.2 3.3 scatter_custom_fusion.7
  275.5 4.8 all-to-all-start.6
  285.6 15.1 %all-to-all-done.6 = bf16[8,64,768]{2,1,0:T(8,128)(2,1)} async-done(((bf16[8,64,768]{2,1,0:T(8,128)(2,1)}), bf16[8,64,768]{2,1,0:T(8,128)(2,1)}, u32[]{:S(2)}, u32[]{:S(2)}) %all-to-all-start.6) | async-done | bytes 786464 | tf_op jit(solution)/shard_map/all_to_all | solution.py:202
  301.8 4.2 all-to-all-start.4
  306.0 5.9 add_convert_fusion
  315.3 9.6 %all-to-all-done.4 = bf16[8,64,768]{2,1,0:T(8,128)(2,1)} async-done(((bf16[8,64,768]{2,1,0:T(8,128)(2,1)}), bf16[8,64,768]{2,1,0:T(8,128)(2,1)}, u32[]{:S(2)}, u32[]{:S(2)}) %all-to-all-start.4) | async-done | bytes 786464 | tf_op jit(solution)/shard_map/all_to_all | solution.py:202
  324.9 4.2 all-to-all-start.7
  329.1 5.9 add_convert_fusion.1
  336.1 2.3 fusion.28
  338.4 10.0 %all-to-all-done.7 = bf16[8,64,768]{2,1,0:T(8,128)(2,1)} async-done(((bf16[8,64,768]{2,1,0:T(8,128)(2,1)}), bf16[8,64,768]{2,1,0:T(8,128)(2,1)}, u32[]{:S(2)}, u32[]{:S(2)}) %all-to-all-start.7) | async-done | bytes 786464 | tf_op jit(solution)/shard_map/all_to_all | solution.py:220
  348.5 3.5 all-to-all-start.5
  356.8 8.5 all-to-all-done.5
  370.6 3.1 multiply_reduce_fusion.2
  387.6 4.0 convolution_add_fusion
  394.1 3.2 fusion.185
  397.3 4.9 fusion.186
  402.2 4.9 fusion.1
  408.8 8.7 copy.94
  417.5 7.7 copy.96
  425.2 98.3 %scatter_custom_fusion.8 = f32[128,12]{1,0:T(8,128)S(1)} fusion(s32[16384]{0:T(1024)} %fusion.136, f32[16384,12]{1,0:T(8,128)} %bitcast.292, f32[]{:T(128)} %constant.43.clone.1), kind=kCustom, calls=%fused_computation.259 | custom fusion | flops 196608 | bytes 6656 | tf_op jit(solution)/shard_map/transpose(jvp())/scatter-add | solution.py:27
  523.6 98.3 %scatter_custom_fusion.9 = f32[128,12]{1,0:T(8,128)S(1)} fusion(s32[16384]{0:T(1024)} %fusion.136, f32[16384,12]{1,0:T(8,128)} %bitcast.291, f32[]{:T(128)} %constant.43.clone.1), kind=kCustom, calls=%fused_computation.257 | custom fusion | flops 196608 | bytes 6656 | tf_op jit(solution)/shard_map/transpose(jvp())/scatter-add | solution.py:27
  622.8 6.2 fusion
  629.8 13.6 %reduce-scatter.13.cloned.1.call-done = f32[96,4]{1,0:T(8,128)} async-done(((f32[768,4]{1,0:T(8,128)}), f32[96,4]{1,0:T(8,128)}) %reduce-scatter.13.cloned.1.call-update) | async-done | bytes 1552
  644.3 3.3 fusion.184
  647.7 3.5 fusion.85
  651.3 19.7 %all-reduce.4 = (f32[768]{0:T(1024)S(1)}, f32[768]{0:T(1024)S(1)}) all-reduce(f32[768]{0:T(1024)S(1)} %add.306, f32[768]{0:T(1024)S(1)} %add.314), channel_id=2, replica_groups=mesh['replica'=4,'fsdp'=8] {'fsdp'}, use_global_device_ids=true, to_apply=%region_36.37.clone | all-reduce | flops 1536 | bytes 12288
  673.1 35.7 %reduce-scatter.11.cloned.1.call-done = f32[16,12]{1,0:T(8,128)} async-done(((f32[128,12]{1,0:T(8,128)}), f32[16,12]{1,0:T(8,128)}) %reduce-scatter.11.cloned.1.call-update) | async-done | bytes 784 | tf_op jit(solution)/shard_map/reduce_scatter | solution.py:293
  708.8 10.7 %all-reduce.5 = (f32[96]{0:T(128)}, f32[16,12]{1,0:T(8,128)}, f32[96]{0:T(128)}, f32[96,4]{0,1:T(4,128)}) all-reduce(f32[96]{0:T(128)S(1)} %dynamic-slice.3, f32[16,12]{1,0:T(8,128)} %reduce-scatter.11.cloned.1.call-done, f32[96]{0:T(128)S(1)} %dynamic-slice.5, f32[96,4]{0,1:T(4,128)S(1)} %copy.98), channel_id=1, replica_groups=mesh['replica'=4,'fsdp'=8] {'replica'}, use_global_device_ids=true, to_apply=%region_37.38 | all-reduce | flops 768 | bytes 6144 | tf_op jit(solution)/shard_map/psum | solution.py:297
  719.5 180.7 %all-reduce.10.cloned.1.call-done = (f32[96,2304]{1,0:T(8,128)}, f32[96,768]{1,0:T(8,128)}, f32[1,768,1536]{2,1,0:T(8,128)}, f32[1,1536,768]{2,1,0:T(8,128)}) async-done(((f32[96,2304]{1,0:T(8,128)}, f32[96,768]{1,0:T(8,128)}, f32[1,768,1536]{2,1,0:T(8,128)}, f32[1,1536,768]{2,1,0:T(8,128)}), (f32[96,2304]{1,0:T(8,128)}, f32[96,768]{1,0:T(8,128)}, f32[1,768,1536]{2,1,0:T(8,128)}, ...) | async-done | bytes 10616848 | tf_op jit(solution)/shard_map/psum | solution.py:297
  904.2 5.0 copy.117
  (384 shorter events, 111.5 us)
Async XLA Ops:
  7.2 190.2 %copy-start = (bf16[1,768,1536]{2,1,0:T(8,128)(2,1)S(1)}, bf16[1,768,1536]{2,1,0:T(8,128)(2,1)}, u32[]{:S(2)}) copy-start(bf16[1,768,1536]{2,1,0:T(8,128)(2,1)} %param.24) | copy-start | bytes 7077892
  7.2 127.9 %all-gather.4.cloned.1.call-start = ((), (), s32[]{:S(2)}) async-start(), calls=%async_computation.12 | async-start | bytes 3981312 | tf_op jit(solution)/shard_map/all_gather | solution.py:44
  7.9 145.1 %all-gather.6.cloned.1.call-start = ((), (), s32[]{:S(2)}) async-start(), calls=%async_computation.13 | async-start | bytes 1327104 | tf_op jit(solution)/shard_map/all_gather | solution.py:45
  101.8 8.2 copy-start.8
  101.8 8.4 copy-start.104
  101.8 9.7 %copy-start.115 = (bf16[96]{0:T(256)(128)(2,1)S(1)}, bf16[96]{0:T(256)(128)(2,1)}, u32[]{:S(2)}) copy-start(bf16[96]{0:T(256)(128)(2,1)} %param.18) | copy-start | bytes 580
  101.8 9.9 %copy-start.116 = (bf16[96]{0:T(256)(128)(2,1)S(1)}, bf16[96]{0:T(256)(128)(2,1)}, u32[]{:S(2)}) copy-start(bf16[96]{0:T(256)(128)(2,1)} %param.22) | copy-start | bytes 580
  101.8 31.5 %copy-start.85 = (s32[256,2]{0,1:T(2,128)S(1)}, s32[256,2]{0,1:T(2,128)}, u32[]{:S(2)}) copy-start(s32[256,2]{0,1:T(2,128)} %param.16) | copy-start | bytes 6148
  101.8 31.5 %copy-start.105 = (s32[256,2]{0,1:T(2,128)S(1)}, s32[256,2]{0,1:T(2,128)}, u32[]{:S(2)}) copy-start(s32[256,2]{0,1:T(2,128)} %param.17) | copy-start | bytes 6148
  110.1 24.9 %copy-start.100 = (f32[128]{0:T(128)}, f32[128]{0:T(128)S(1)}, u32[]{:S(2)}) copy-start(f32[128]{0:T(128)S(1)} %get-tuple-element.30) | copy-start | bytes 1540
  110.1 24.9 %copy-start.102 = (f32[128]{0:T(128)}, f32[128]{0:T(128)S(1)}, u32[]{:S(2)}) copy-start(f32[128]{0:T(128)S(1)} %get-tuple-element.31) | copy-start | bytes 1540
  110.2 33.5 %copy-start.76 = (f32[128]{0:T(128)}, f32[128]{0:T(128)S(1)}, u32[]{:S(2)}) copy-start(f32[128]{0:T(128)S(1)} %fusion.171) | copy-start | bytes 1540
  134.4 9.3 %copy-start.78 = (f32[128]{0:T(128)}, f32[128]{0:T(128)S(1)}, u32[]{:S(2)}) copy-start(f32[128]{0:T(128)S(1)} %fusion.169) | copy-start | bytes 1540
  157.5 32.9 %copy-start.36 = (bf16[128,768]{1,0:T(8,128)(2,1)}, bf16[128,768]{1,0:T(8,128)(2,1)S(1)}, u32[]{:S(2)}) copy-start(bf16[128,768]{1,0:T(8,128)(2,1)S(1)} %get-tuple-element.77) | copy-start | bytes 589828
  161.7 30.1 %all-to-all-start = ((bf16[8,64,768]{2,1,0:T(8,128)(2,1)}), bf16[8,64,768]{2,1,0:T(8,128)(2,1)}, u32[]{:S(2)}, u32[]{:S(2)}) async-start(bf16[8,64,768]{2,1,0:T(8,128)(2,1)} %bitcast.310), calls=%async_computation | async-start | bytes 1572864 | tf_op jit(solution)/shard_map/all_to_all | solution.py:124
  192.7 20.0 %all-to-all-start.2 = ((bf16[8,64,768]{2,1,0:T(8,128)(2,1)}), bf16[8,64,768]{2,1,0:T(8,128)(2,1)S(1)}, u32[]{:S(2)}, u32[]{:S(2)}) async-start(bf16[8,64,768]{2,1,0:T(8,128)(2,1)} %bitcast.311), calls=%async_computation.2 | async-start | bytes 1572864 | tf_op jit(solution)/shard_map/all_to_all | solution.py:124
  200.5 7.9 copy-start.38
  200.5 9.1 copy-start.113
  213.6 27.4 %all-to-all-start.1 = ((bf16[8,64,768]{2,1,0:T(8,128)(2,1)}), bf16[8,64,768]{2,1,0:T(8,128)(2,1)S(1)}, u32[]{:S(2)}, u32[]{:S(2)}) async-start(bf16[8,64,768]{2,1,0:T(8,128)(2,1)} %fusion.34), calls=%async_computation.1 | async-start | bytes 1572864 | tf_op jit(solution)/shard_map/all_to_all | solution.py:132
  224.4 9.1 copy-start.114
  241.0 10.5 %copy-start.32 = (bf16[8,64,768]{2,1,0:T(8,128)(2,1)}, bf16[8,64,768]{2,1,0:T(8,128)(2,1)S(1)}, u32[]{:S(2)}) copy-start(bf16[8,64,768]{2,1,0:T(8,128)(2,1)S(1)} %all-to-all-done.1) | copy-start | bytes 2359300
  241.0 18.6 %all-to-all-start.3 = ((bf16[8,64,768]{2,1,0:T(8,128)(2,1)}), bf16[8,64,768]{2,1,0:T(8,128)(2,1)}, u32[]{:S(2)}, u32[]{:S(2)}) async-start(bf16[8,64,768]{2,1,0:T(8,128)(2,1)} %fusion.37), calls=%async_computation.3 | async-start | bytes 1572864 | tf_op jit(solution)/shard_map/all_to_all | solution.py:132
  264.4 15.9 %copy-start.34 = (bf16[128,768]{1,0:T(8,128)(2,1)S(1)}, bf16[128,768]{1,0:T(8,128)(2,1)}, u32[]{:S(2)}) copy-start(bf16[128,768]{1,0:T(8,128)(2,1)} %copy-done.33) | copy-start | bytes 589828
  264.4 15.9 %copy-start.86 = (s32[128]{0:T(128)S(1)}, s32[128]{0:T(128)}, u32[]{:S(2)}) copy-start(s32[128]{0:T(128)} %get-tuple-element.80) | copy-start | bytes 1540
  264.4 15.9 %copy-start.88 = (s32[128]{0:T(128)S(1)}, s32[128]{0:T(128)}, u32[]{:S(2)}) copy-start(s32[128]{0:T(128)} %get-tuple-element.82) | copy-start | bytes 1540
  264.4 16.7 %copy-start.12 = (bf16[256,768]{1,0:T(8,128)(2,1)S(1)}, bf16[256,768]{1,0:T(8,128)(2,1)}, u32[]{:S(2)}) copy-start(bf16[256,768]{1,0:T(8,128)(2,1)} %param.14) | copy-start | bytes 1179652
  267.5 13.6 %copy-start.91 = (f32[128]{0:T(128)}, f32[128]{0:T(128)S(1)}, u32[]{:S(2)}) copy-start(f32[128]{0:T(128)S(1)} %get-tuple-element.51) | copy-start | bytes 1540
  267.5 13.6 %copy-start.98 = (f32[128]{0:T(128)}, f32[128]{0:T(128)S(1)}, u32[]{:S(2)}) copy-start(f32[128]{0:T(128)S(1)} %broadcast_subtract_fusion) | copy-start | bytes 1540
  275.5 25.3 %all-to-all-start.6 = ((bf16[8,64,768]{2,1,0:T(8,128)(2,1)}), bf16[8,64,768]{2,1,0:T(8,128)(2,1)}, u32[]{:S(2)}, u32[]{:S(2)}) async-start(bf16[8,64,768]{2,1,0:T(8,128)(2,1)} %bitcast.309), calls=%async_computation.6 | async-start | bytes 1572864 | tf_op jit(solution)/shard_map/all_to_all | solution.py:202
  301.8 23.1 %all-to-all-start.4 = ((bf16[8,64,768]{2,1,0:T(8,128)(2,1)}), bf16[8,64,768]{2,1,0:T(8,128)(2,1)}, u32[]{:S(2)}, u32[]{:S(2)}) async-start(bf16[8,64,768]{2,1,0:T(8,128)(2,1)} %bitcast.312), calls=%async_computation.4 | async-start | bytes 1572864 | tf_op jit(solution)/shard_map/all_to_all | solution.py:202
  324.9 23.6 %all-to-all-start.7 = ((bf16[8,64,768]{2,1,0:T(8,128)(2,1)}), bf16[8,64,768]{2,1,0:T(8,128)(2,1)}, u32[]{:S(2)}, u32[]{:S(2)}) async-start(bf16[8,64,768]{2,1,0:T(8,128)(2,1)} %fusion.31), calls=%async_computation.7 | async-start | bytes 1572864 | tf_op jit(solution)/shard_map/all_to_all | solution.py:220
  348.5 16.8 %all-to-all-start.5 = ((bf16[8,64,768]{2,1,0:T(8,128)(2,1)}), bf16[8,64,768]{2,1,0:T(8,128)(2,1)S(1)}, u32[]{:S(2)}, u32[]{:S(2)}) async-start(bf16[8,64,768]{2,1,0:T(8,128)(2,1)} %fusion.28), calls=%async_computation.5 | async-start | bytes 1572864 | tf_op jit(solution)/shard_map/all_to_all | solution.py:220
  352.0 277.0 %reduce-scatter.9.cloned.1.call-start = ((), (), s32[]{:S(2)}) async-start(), calls=%async_computation.15 | async-start | bytes 2654208 | tf_op jit(solution)/shard_map/reduce_scatter | solution.py:292
  377.5 251.6 %reduce-scatter.7.cloned.1.call-start = ((), (), s32[]{:S(2)}) async-start(), calls=%async_computation.14 | async-start | bytes 7962624 | tf_op jit(solution)/shard_map/reduce_scatter | solution.py:291
  391.7 251.7 %reduce-scatter.13.cloned.1.call-start = ((), (), s32[]{:S(2)}) async-start(), calls=%async_computation.17 | async-start | bytes 442368
  394.0 314.8 %reduce-scatter.11.cloned.1.call-start = ((), (), s32[]{:S(2)}) async-start(), calls=%async_computation.16 | async-start | bytes 73728 | tf_op jit(solution)/shard_map/reduce_scatter | solution.py:293
  408.8 8.7 copy-start.40
  417.5 205.3 %copy-start.44 = (bf16[8,64,1536]{2,1,0:T(8,128)(2,1)S(1)}, bf16[8,64,1536]{2,1,0:T(8,128)(2,1)}, u32[]{:S(2)}) copy-start(bf16[8,64,1536]{2,1,0:T(8,128)(2,1)} %copy-done.43) | copy-start | bytes 4718596
  622.6 277.7 %all-reduce.10.cloned.1.call-start = ((), (), s32[]{:S(2)}) async-start(), calls=%async_computation.18 | async-start | bytes 21233664 | tf_op jit(solution)/shard_map/psum | solution.py:297
  629.1 15.2 %copy-start.22 = (bf16[128,3,12,64]{0,3,2,1:T(8,128)(2,1)S(1)}, bf16[128,3,12,64]{0,3,2,1:T(8,128)(2,1)}, u32[]{:S(2)}) copy-start(bf16[128,3,12,64]{0,3,2,1:T(8,128)(2,1)} %copy-done.21) | copy-start | bytes 1769476
  629.1 18.5 %copy-start.24 = (bf16[128,3,12,64]{0,3,2,1:T(8,128)(2,1)S(1)}, bf16[128,3,12,64]{0,3,2,1:T(8,128)(2,1)}, u32[]{:S(2)}) copy-start(bf16[128,3,12,64]{0,3,2,1:T(8,128)(2,1)} %copy-done.23) | copy-start | bytes 1769476
  629.1 18.5 %copy-start.80 = (f32[128]{0:T(128)S(1)}, f32[128]{0:T(128)}, u32[]{:S(2)}) copy-start(f32[128]{0:T(128)} %copy-done.78) | copy-start | bytes 1540
  647.6 23.5 %copy-start.48 = (bf16[128,768]{1,0:T(8,128)(2,1)S(1)}, bf16[128,768]{1,0:T(8,128)(2,1)}, u32[]{:S(2)}) copy-start(bf16[128,768]{1,0:T(8,128)(2,1)} %get-tuple-element.72) | copy-start | bytes 589828
  647.6 23.5 %copy-start.52 = (bf16[128,768]{1,0:T(8,128)(2,1)S(1)}, bf16[128,768]{1,0:T(8,128)(2,1)}, u32[]{:S(2)}) copy-start(bf16[128,768]{1,0:T(8,128)(2,1)} %get-tuple-element.73) | copy-start | bytes 589828
  647.6 24.2 %copy-start.101 = (f32[128]{0:T(128)S(1)}, f32[128]{0:T(128)}, u32[]{:S(2)}) copy-start(f32[128]{0:T(128)} %copy-done.100) | copy-start | bytes 1540
  647.7 24.2 %copy-start.103 = (f32[128]{0:T(128)S(1)}, f32[128]{0:T(128)}, u32[]{:S(2)}) copy-start(f32[128]{0:T(128)} %copy-done.102) | copy-start | bytes 1540
  647.7 24.2 %copy-start.14 = (f32[128,768]{1,0:T(8,128)S(1)}, f32[128,768]{1,0:T(8,128)}, u32[]{:S(2)}) copy-start(f32[128,768]{1,0:T(8,128)} %copy-done.13) | copy-start | bytes 1179652
  647.7 24.2 %copy-start.20 = (f32[128,768]{1,0:T(8,128)S(1)}, f32[128,768]{1,0:T(8,128)}, u32[]{:S(2)}) copy-start(f32[128,768]{1,0:T(8,128)} %copy-done.19) | copy-start | bytes 1179652
  (89 other events, 266.2 us)
Sparse Core Ops, SparseCore 0:
  10.2 67.5 all-gather.3
  79.9 39.9 all-gather.5
  377.6 68.6 reduce-scatter.8
  449.9 128.3 reduce-scatter.6
  582.0 61.3 reduce-scatter.12
  647.2 61.5 reduce-scatter.10
  712.2 187.9 all-reduce.9
where the time goes:
time: 928 us; the launch traced here: 918 us
  waiting for transfers between devices  282 us (30%)
  other arithmetic  249 us (27%)
  local copies, waits for them, and re-layouts  135 us (15%)
  blocking collectives  107 us (12%)
  matrix products  88.8 us (10%)
  starting transfers between devices  39.2 us (4%)
  between operations  17.4 us (2%)
    scatter-add x2, other arithmetic, bias_matrix(): return jnp.transpose(table[distance], (2, 0, 1))  197 us
    psum x1, waiting for transfers between devices, body(): lax.psum((shards[0], shards[1], shards[2], shards[3], shards[4], shards[5...  181 us
    gather x2, local copies, waits for them, and re-layouts, bias_matrix(): return jnp.transpose(table[distance], (2, 0, 1))  62.2 us
    unnamed x2, blocking collectives  41 us
    reduce_scatter x1, waiting for transfers between devices, body(): lax.psum_scatter(grad_table, 'fsdp', scatter_dimension=0, tiled=True)  35.7 us
    all_gather x1, blocking collectives, fetch_weights(): lax.all_gather(rel_table, 'fsdp', axis=0, tiled=True)  33.2 us
    all_to_all x2, waiting for transfers between devices, body(): lax.all_to_all(grad_send, 'fsdp', split_axis=0, concat_axis=0, tiled=True)  24.7 us
    unnamed x258, local copies, waits for them, and re-layouts  24.3 us
  transfers between devices with their start and end apart: 15, of which 10 were waited for; matrix products, arithmetic and copies ran while one was open for 45% of the time, Pallas kernels for 0%

commit v1 on v0

--- a/solution.py
+++ b/solution.py
@@ -20,32 +20,44 @@
     return values * factor * gain
 
 
-def bias_matrix(table):
-    length = table.shape[0]
-    places = jnp.arange(length, dtype=jnp.int32)
-    distance = jnp.clip(places[:, None] - places[None, :], 0, length - 1)
-    return jnp.transpose(table[distance], (2, 0, 1))
+def distance_hot():
+    places = jnp.arange(SEQ, dtype=jnp.int32)
+    distance = jnp.clip(places[:, None] - places[None, :], 0, SEQ - 1).reshape(1, SEQ * SEQ)
+    return (distance == places[:, None]).astype(jnp.bfloat16)
+
+
+def bias_matrix(table, hot):
+    flat = jnp.einsum("dh,dp->hp", table, hot, preferred_element_type=jnp.float32)
+    return flat.reshape(table.shape[1], SEQ, SEQ)
 
 
 def exact_gelu(values):
     return jax.nn.gelu(values, approximate=False)
 
 
-def masked_scores(qkv_rows, table, allowed, factor):
+def masked_scores(qkv_rows, bias, allowed, factor):
     raw = jnp.einsum(
         "qhd,khd->hqk", qkv_rows[:, 0], qkv_rows[:, 1], preferred_element_type=jnp.float32
     )
-    return jnp.where(allowed[None], raw * factor + bias_matrix(table), -1e30)
+    return jnp.where(allowed[None], raw * factor + bias, -1e30)
 
 
 def fetch_weights(gain_attn, w_qkv, w_proj, rel_table, gain_moe, w_router):
+    rows, experts = w_router.shape
+    spread = rel_table.shape[0]
+    packed = jnp.concatenate(
+        [gain_attn, gain_moe, w_router.reshape(-1), rel_table.reshape(-1)]
+    )
+    small = lax.all_gather(packed, "fsdp", axis=0, tiled=False)
+    groups = small.shape[0]
+    edge = 2 * rows + rows * experts
     return (
-        lax.all_gather(gain_attn, "fsdp", axis=0, tiled=True),
+        small[:, :rows].reshape(-1),
         lax.all_gather(w_qkv, "fsdp", axis=0, tiled=True),
         lax.all_gather(w_proj, "fsdp", axis=0, tiled=True),
-        lax.all_gather(rel_table, "fsdp", axis=0, tiled=True),
-        lax.all_gather(gain_moe, "fsdp", axis=0, tiled=True),
-        lax.all_gather(w_router, "fsdp", axis=0, tiled=True),
+        small[:, edge:].reshape(groups * spread, HEADS),
+        small[:, rows : 2 * rows].reshape(-1),
+        small[:, 2 * rows : edge].reshape(groups * rows, experts),
     )
 
 
@@ -75,11 +87,13 @@
     expert_ids = jnp.arange(experts, dtype=jnp.int32)
     saved = []
     mixed_parts = []
+    weights = fetch_weights(gain_attn, w_qkv, w_proj, rel_table, gain_moe, w_router)
+    gain_a = weights[0].astype(jnp.float32)
+    gain_m = weights[4].astype(jnp.float32)
+    router_float = weights[5].astype(jnp.float32)
+    hot = distance_hot()
+    bias = bias_matrix(weights[3], hot)
     for batch in range(MB):
-        weights = fetch_weights(gain_attn, w_qkv, w_proj, rel_table, gain_moe, w_router)
-        gain_a = weights[0].astype(jnp.float32)
-        table = weights[3].astype(jnp.float32)
-        gain_m = weights[4].astype(jnp.float32)
         x_float = tokens[batch * SEQ : (batch + 1) * SEQ].astype(jnp.float32)
         live_keys = places < lengths[batch]
         live_col = live_keys.astype(jnp.float32)[:, None]
@@ -90,7 +104,7 @@
             .astype(jnp.bfloat16)
             .reshape(SEQ, 3, HEADS, HEAD)
         )
-        scores = masked_scores(qkv_rows, table, allowed, factor)
+        scores = masked_scores(qkv_rows, bias, allowed, factor)
         row_peak = jnp.max(scores, axis=-1, keepdims=True)
         exp_scores = jnp.exp(scores - row_peak)
         row_total = jnp.sum(exp_scores, axis=-1, keepdims=True)
@@ -173,11 +187,6 @@
     grad_parts = [None] * MB
     for batch in reversed(range(MB)):
         kept = saved[batch]
-        weights = fetch_weights(gain_attn, w_qkv, w_proj, rel_table, gain_moe, w_router)
-        gain_a = weights[0].astype(jnp.float32)
-        table = weights[3].astype(jnp.float32)
-        gain_m = weights[4].astype(jnp.float32)
-        router_float = weights[5].astype(jnp.float32)
         x_float = tokens[batch * SEQ : (batch + 1) * SEQ].astype(jnp.float32)
         live_keys = places < lengths[batch]
         live_col = live_keys.astype(jnp.float32)[:, None]
@@ -246,7 +255,7 @@
         )
         grad_attended = grad_attended.astype(jnp.bfloat16).reshape(SEQ, HEADS, HEAD)
         qkv_rows = kept["qkv_rows"]
-        scores = masked_scores(qkv_rows, table, allowed, factor)
+        scores = masked_scores(qkv_rows, bias, allowed, factor)
         probs = jnp.exp(scores - kept["log_total"])
         probs_low = probs.astype(jnp.bfloat16)
         grad_probs = jnp.einsum(
@@ -254,8 +263,12 @@
         )
         row_dot = jnp.sum(probs * grad_probs, axis=-1, keepdims=True)
         grad_scores = (probs * (grad_probs - row_dot)).astype(jnp.bfloat16)
-        _, bias_back = jax.vjp(bias_matrix, table)
-        grad_table = grad_table + bias_back(grad_scores.astype(jnp.float32))[0]
+        grad_table = grad_table + jnp.einsum(
+            "dp,hp->dh",
+            hot,
+            jnp.where(allowed[None], grad_scores, 0).reshape(HEADS, SEQ * SEQ),
+            preferred_element_type=jnp.float32,
+        )
         grad_queries = (
             jnp.einsum(
                 "hqk,khd->qhd", grad_scores, qkv_rows[:, 1], preferred_element_type=jnp.float32
@@ -286,26 +299,33 @@
         grad_x_norm, grad_gain_piece = norm_back_attn(grad_normed)
         grad_gain_a = grad_gain_a + grad_gain_piece
         grad_parts[batch] = grad_hidden + grad_x_norm
+    small = jnp.concatenate(
+        [
+            grad_gain_a.reshape(groups, -1),
+            grad_gain_m.reshape(groups, -1),
+            grad_router.reshape(groups, -1),
+            grad_table.reshape(groups, -1),
+        ],
+        axis=1,
+    )
+    small = lax.psum_scatter(small, "fsdp", scatter_dimension=0, tiled=True)
     shards = (
-        lax.psum_scatter(grad_gain_a, "fsdp", scatter_dimension=0, tiled=True),
+        small,
         lax.psum_scatter(grad_qkv_w, "fsdp", scatter_dimension=0, tiled=True),
         lax.psum_scatter(grad_proj_w, "fsdp", scatter_dimension=0, tiled=True),
-        lax.psum_scatter(grad_table, "fsdp", scatter_dimension=0, tiled=True),
-        lax.psum_scatter(grad_gain_m, "fsdp", scatter_dimension=0, tiled=True),
-        lax.psum_scatter(grad_router, "fsdp", scatter_dimension=0, tiled=True),
-    )
-    totals = lax.psum(
-        (
-            shards[0],
-            shards[1],
-            shards[2],
-            shards[3],
-            shards[4],
-            shards[5],
-            grad_up[None],
-            grad_down[None],
-        ),
-        "replica",
+    )
+    sums = lax.psum((shards[0], shards[1], shards[2], grad_up[None], grad_down[None]), "replica")
+    rows = D // groups
+    edge = 2 * rows + rows * experts
+    totals = (
+        sums[0][0, :rows],
+        sums[1],
+        sums[2],
+        sums[0][0, edge:].reshape(SEQ // groups, HEADS),
+        sums[0][0, rows : 2 * rows],
+        sums[0][0, 2 * rows : edge].reshape(rows, experts),
+        sums[3],
+        sums[4],
     )
     mixed = jnp.concatenate(mixed_parts, axis=0)
     grad_tokens = jnp.concatenate(grad_parts, axis=0)

time: 928 us -> 778 us (0.84)
  other arithmetic: 249 us -> 55.4 us
  waiting for transfers between devices: 282 us -> 436 us
  local copies, waits for them, and re-layouts: 135 us -> 60.6 us
  blocking collectives: 107 us -> 74.1 us
    scatter-add x2 -> x0, other arithmetic: 197 us -> none  [bias_matrix(): return jnp.transpose(table[distance], (2, 0, 1))]
    reduce_scatter x1, waiting for transfers between devices: 0.01 us -> 132 us  [body(): lax.psum_scatter(grad_qkv_w, 'fsdp', scatter_dimension=0, tiled=True)]
    gather x2 -> x0, local copies, waits for them, and re-layouts: 62.2 us -> none  [bias_matrix(): return jnp.transpose(table[distance], (2, 0, 1))]
    psum x1, waiting for transfers between devices: 181 us -> 130 us  [body(): lax.psum((shards[0], shards[1], shards[2], grad_up[None], grad_down[None]...]
    reduce_scatter x1, waiting for transfers between devices: 0.01 us -> 40.3 us  [body(): lax.psum_scatter(grad_proj_w, 'fsdp', scatter_dimension=0, tiled=True)]
    reduce_scatter x1 -> x0, waiting for transfers between devices: 35.7 us -> none  [body(): lax.psum_scatter(grad_table, 'fsdp', scatter_dimension=0, tiled=True)]
    all_gather x1, waiting for transfers between devices: 0.01 us -> 31.7 us  [fetch_weights(): lax.all_gather(w_proj, 'fsdp', axis=0, tiled=True)]
    all_gather x2 -> x1, blocking collectives: 55.5 us -> 32.6 us  [fetch_weights(): small = lax.all_gather(packed, 'fsdp', axis=0, tiled=False)]
  transfers between devices with their start and end apart: 15 -> 13, of which waited for: 10 -> 13; matrix products, arithmetic and copies ran while one was open for 45% -> 19% of each run, Pallas kernels for 0% -> 0%
where the time goes in v1:
time: 778 us; the launch traced here: 770 us
  waiting for transfers between devices  436 us (56%)
  matrix products  93.8 us (12%)
  blocking collectives  74.1 us (10%)
  local copies, waits for them, and re-layouts  60.6 us (8%)
  other arithmetic  55.4 us (7%)
  starting transfers between devices  33.6 us (4%)
  between operations  15.9 us (2%)
    reduce_scatter x1, waiting for transfers between devices, body(): lax.psum_scatter(grad_qkv_w, 'fsdp', scatter_dimension=0, tiled=True)  132 us
    psum x1, waiting for transfers between devices, body(): lax.psum((shards[0], shards[1], shards[2], grad_up[None], grad_down[None]...  130 us
    reduce_scatter x1, waiting for transfers between devices, body(): lax.psum_scatter(grad_proj_w, 'fsdp', scatter_dimension=0, tiled=True)  40.3 us
    unnamed x1, blocking collectives  35 us
    all_gather x1, blocking collectives, fetch_weights(): small = lax.all_gather(packed, 'fsdp', axis=0, tiled=False)  32.6 us
    all_gather x1, waiting for transfers between devices, fetch_weights(): lax.all_gather(w_proj, 'fsdp', axis=0, tiled=True)  31.7 us
    all_to_all x2, waiting for transfers between devices, body(): lax.all_to_all(grad_send, 'fsdp', split_axis=0, concat_axis=0, tiled=True)  25.5 us
    all_to_all x2, waiting for transfers between devices, body(): lax.all_to_all(grad_part, 'fsdp', split_axis=0, concat_axis=0, tiled=True)  25.3 us
  transfers between devices with their start and end apart: 13, of which 13 were waited for; matrix products, arithmetic and copies ran while one was open for 19% of the time, Pallas kernels for 0%

profile of v1, /device:TPU:0, one launch (start us, length us, event | category | flops | bytes accessed | tf_op | source)
XLA Modules:
  0.0 769.5 jit_solution(10012427860163569329)
XLA Ops:
  11.2 32.6 %all-gather.1 = bf16[8,1,768]{2,1,0:T(2,128)(2,1)S(1)} all-gather(bf16[1,1,768]{2,1,0:T(2,128)(2,1)S(1)} %reshape.583), channel_id=2, replica_groups=mesh['replica'=4,'fsdp'=8] {'fsdp'}, dimensions={0}, use_global_device_ids=true | all-gather | bytes 13824 | tf_op jit(solution)/shard_map/all_gather | solution.py:51
  49.9 5.2 fusion.3
  63.8 13.9 %all-gather.5.cloned.1.call-done = bf16[768,2304]{1,0:T(8,128)(2,1)} async-done(((bf16[96,2304]{1,0:T(8,128)(2,1)}), bf16[768,2304]{1,0:T(8,128)(2,1)}) %all-gather.5.cloned.1.call-update) | async-done | bytes 3538960 | tf_op jit(solution)/shard_map/all_gather | solution.py:56
  77.7 3.5 convolution_convert_fusion.1
  88.1 31.7 %all-gather.7.cloned.1.call-done = bf16[768,768]{1,0:T(8,128)(2,1)} async-done(((bf16[96,768]{1,0:T(8,128)(2,1)}), bf16[768,768]{1,0:T(8,128)(2,1)}) %all-gather.7.cloned.1.call-update) | async-done | bytes 1179664 | tf_op jit(solution)/shard_map/all_gather | solution.py:57
  119.8 2.4 multiply_reduce_fusion.7
  123.3 3.5 convolution_convert_fusion
  137.1 4.2 all-to-all-start
  144.5 16.1 %all-to-all-done = bf16[8,64,768]{2,1,0:T(8,128)(2,1)} async-done(((bf16[8,64,768]{2,1,0:T(8,128)(2,1)}), bf16[8,64,768]{2,1,0:T(8,128)(2,1)}, u32[]{:S(2)}, u32[]{:S(2)}) %all-to-all-start) | async-done | bytes 786464 | tf_op jit(solution)/shard_map/all_to_all | solution.py:138
  161.5 4.0 all-to-all-start.2
  165.6 3.2 fusion.67
  168.8 7.9 %multiply_convert_fusion.1 = (bf16[8,64,1536]{2,1,0:T(8,128)(2,1)S(1)}, f32[8,64,1536]{2,1,0:T(8,128)}) fusion(f32[8,64,1536]{2,1,0:T(8,128)S(1)} %get-tuple-element.114, u8[64,1536]{1,0:T(8,128)(4,1)S(1)} %get-tuple-element.31, u8[64,1536]{1,0:T(8,128)(4,1)S(1)} %get-tuple-element.30), kind=kLoop, calls=%fused_computation.60 | loop fusion | flops 55050240 | bytes 8060928 | tf_op jit(solution)/shard_map/convert_element_type | solution.py:142
  177.8 2.3 fusion.42
  180.1 5.6 all-to-all-done.2
  186.6 3.6 all-to-all-start.1
  190.2 3.2 fusion.68
  193.4 7.9 %multiply_convert_fusion = (bf16[8,64,1536]{2,1,0:T(8,128)(2,1)S(1)}, f32[8,64,1536]{2,1,0:T(8,128)}) fusion(f32[8,64,1536]{2,1,0:T(8,128)S(1)} %get-tuple-element.115, u8[64,1536]{1,0:T(8,128)(4,1)S(1)} %get-tuple-element.33, u8[64,1536]{1,0:T(8,128)(4,1)S(1)} %get-tuple-element.32), kind=kLoop, calls=%fused_computation.47 | loop fusion | flops 55050240 | bytes 8060928 | tf_op jit(solution)/shard_map/convert_element_type | solution.py:142
  202.4 2.3 fusion.45
  204.7 5.8 all-to-all-done.1
  210.6 4.2 all-to-all-start.3
  226.0 8.6 %all-to-all-done.3 = bf16[8,64,768]{2,1,0:T(8,128)(2,1)} async-done(((bf16[8,64,768]{2,1,0:T(8,128)(2,1)}), bf16[8,64,768]{2,1,0:T(8,128)(2,1)}, u32[]{:S(2)}, u32[]{:S(2)}) %all-to-all-start.3) | async-done | bytes 786464 | tf_op jit(solution)/shard_map/all_to_all | solution.py:146
  239.5 2.2 fusion.92
  248.5 4.2 all-to-all-start.6
  257.5 15.1 %all-to-all-done.6 = bf16[8,64,768]{2,1,0:T(8,128)(2,1)} async-done(((bf16[8,64,768]{2,1,0:T(8,128)(2,1)}), bf16[8,64,768]{2,1,0:T(8,128)(2,1)}, u32[]{:S(2)}, u32[]{:S(2)}) %all-to-all-start.6) | async-done | bytes 786464 | tf_op jit(solution)/shard_map/all_to_all | solution.py:211
  273.5 4.2 all-to-all-start.4
  277.7 5.9 add_convert_fusion
  284.8 2.3 fusion.39
  287.1 10.5 %all-to-all-done.4 = bf16[8,64,768]{2,1,0:T(8,128)(2,1)} async-done(((bf16[8,64,768]{2,1,0:T(8,128)(2,1)}), bf16[8,64,768]{2,1,0:T(8,128)(2,1)}, u32[]{:S(2)}, u32[]{:S(2)}) %all-to-all-start.4) | async-done | bytes 786464 | tf_op jit(solution)/shard_map/all_to_all | solution.py:211
  297.5 4.2 all-to-all-start.7
  301.8 5.9 add_convert_fusion.1
  308.8 2.3 fusion.36
  311.1 10.5 %all-to-all-done.7 = bf16[8,64,768]{2,1,0:T(8,128)(2,1)} async-done(((bf16[8,64,768]{2,1,0:T(8,128)(2,1)}), bf16[8,64,768]{2,1,0:T(8,128)(2,1)}, u32[]{:S(2)}, u32[]{:S(2)}) %all-to-all-start.7) | async-done | bytes 786464 | tf_op jit(solution)/shard_map/all_to_all | solution.py:229
  321.6 4.2 all-to-all-start.5
  330.7 14.8 %all-to-all-done.5 = bf16[8,64,768]{2,1,0:T(8,128)(2,1)} async-done(((bf16[8,64,768]{2,1,0:T(8,128)(2,1)}), bf16[8,64,768]{2,1,0:T(8,128)(2,1)}, u32[]{:S(2)}, u32[]{:S(2)}) %all-to-all-start.5) | async-done | bytes 786464 | tf_op jit(solution)/shard_map/all_to_all | solution.py:229
  352.3 3.1 multiply_reduce_fusion.2
  367.5 4.0 convolution_add_fusion
  371.8 3.2 fusion.178
  375.0 2.7 fusion.179
  377.8 5.0 fusion.6
  382.8 4.9 fusion.5
  387.6 40.3 %reduce-scatter.5.cloned.1.call-done = f32[96,768]{1,0:T(8,128)} async-done(((f32[768,768]{1,0:T(8,128)}), f32[96,768]{1,0:T(8,128)}) %reduce-scatter.5.cloned.1.call-update) | async-done | bytes 294928 | tf_op jit(solution)/shard_map/reduce_scatter | solution.py:315
  427.9 131.9 %reduce-scatter.3.cloned.1.call-done = f32[96,2304]{1,0:T(8,128)} async-done(((f32[768,2304]{1,0:T(8,128)}), f32[96,2304]{1,0:T(8,128)}) %reduce-scatter.3.cloned.1.call-update) | async-done | bytes 884752 | tf_op jit(solution)/shard_map/reduce_scatter | solution.py:314
  567.8 3.6 fusion.177
  571.5 3.5 fusion.86
  575.1 35.0 %all-reduce = f32[8,768]{1,0:T(8,128)S(1)} all-reduce(f32[8,768]{1,0:T(8,128)S(1)} %pad_maximum_fusion.4), channel_id=3, replica_groups=mesh['replica'=4,'fsdp'=8] {'fsdp'}, use_global_device_ids=true, to_apply=%region_38.39.clone | all-reduce | flops 6144 | bytes 49152
  610.8 6.5 psum.35
  621.5 129.9 %all-reduce.4.cloned.1.call-done = (f32[96,2304]{1,0:T(8,128)}, f32[96,768]{1,0:T(8,128)}, f32[1,768,1536]{2,1,0:T(8,128)}, f32[1,1536,768]{2,1,0:T(8,128)}) async-done(((f32[96,2304]{1,0:T(8,128)}, f32[96,768]{1,0:T(8,128)}, f32[1,768,1536]{2,1,0:T(8,128)}, f32[1,1536,768]{2,1,0:T(8,128)}), (f32[96,2304]{1,0:T(8,128)}, f32[96,768]{1,0:T(8,128)}, f32[1,768,1536]{2,1,0:T(8,128)}, ...) | async-done | bytes 10616848 | tf_op jit(solution)/shard_map/psum | solution.py:317
  755.3 5.0 copy.110
  (370 shorter events, 117.1 us)
Async XLA Ops:
  7.2 158.4 %copy-start = (bf16[1,768,1536]{2,1,0:T(8,128)(2,1)S(1)}, bf16[1,768,1536]{2,1,0:T(8,128)(2,1)}, u32[]{:S(2)}) copy-start(bf16[1,768,1536]{2,1,0:T(8,128)(2,1)} %param.24) | copy-start | bytes 7077892
  7.2 70.5 %copy-start.8 = (bf16[256,768]{1,0:T(8,128)(2,1)S(1)}, bf16[256,768]{1,0:T(8,128)(2,1)}, u32[]{:S(2)}) copy-start(bf16[256,768]{1,0:T(8,128)(2,1)} %param.13) | copy-start | bytes 1179652
  7.2 70.5 %all-gather.5.cloned.1.call-start = ((), (), s32[]{:S(2)}) async-start(), calls=%async_computation.10 | async-start | bytes 3981312 | tf_op jit(solution)/shard_map/all_gather | solution.py:56
  7.9 111.8 %all-gather.7.cloned.1.call-start = ((), (), s32[]{:S(2)}) async-start(), calls=%async_computation.11 | async-start | bytes 1327104 | tf_op jit(solution)/shard_map/all_gather | solution.py:57
  43.8 11.4 %copy-start.53 = (bf16[8,1,768]{2,0,1:T(8,128)(2,1)}, bf16[8,1,768]{2,0,1:T(8,128)(2,1)S(1)}, u32[]{:S(2)}) copy-start(bf16[8,1,768]{2,0,1:T(8,128)(2,1)S(1)} %copy.99) | copy-start | bytes 36868
  48.9 6.3 copy-start.92
  48.9 6.3 copy-start.94
  132.8 87.2 %copy-start.31 = (bf16[128,768]{1,0:T(8,128)(2,1)}, bf16[128,768]{1,0:T(8,128)(2,1)S(1)}, u32[]{:S(2)}) copy-start(bf16[128,768]{1,0:T(8,128)(2,1)S(1)} %get-tuple-element.87) | copy-start | bytes 589828
  134.7 6.6 copy-start.54
  134.8 7.1 copy-start.90
  137.1 23.5 %all-to-all-start = ((bf16[8,64,768]{2,1,0:T(8,128)(2,1)}), bf16[8,64,768]{2,1,0:T(8,128)(2,1)}, u32[]{:S(2)}, u32[]{:S(2)}) async-start(bf16[8,64,768]{2,1,0:T(8,128)(2,1)} %bitcast.14), calls=%async_computation | async-start | bytes 1572864 | tf_op jit(solution)/shard_map/all_to_all | solution.py:138
  141.8 78.2 %copy-start.19 = (bf16[768,4]{1,0:T(8,128)(2,1)}, bf16[768,4]{1,0:T(8,128)(2,1)S(1)}, u32[]{:S(2)}) copy-start(bf16[768,4]{1,0:T(8,128)(2,1)S(1)} %reshape.415) | copy-start | bytes 18436
  141.8 19.7 %copy-start.97 = (s32[128]{0:T(128)}, s32[128]{0:T(128)S(1)}, u32[]{:S(2)}) copy-start(s32[128]{0:T(128)S(1)} %get-tuple-element.102) | copy-start | bytes 1540
  141.9 19.7 %copy-start.102 = (s32[128]{0:T(128)}, s32[128]{0:T(128)S(1)}, u32[]{:S(2)}) copy-start(s32[128]{0:T(128)S(1)} %get-tuple-element.103) | copy-start | bytes 1540
  161.5 24.2 %all-to-all-start.2 = ((bf16[8,64,768]{2,1,0:T(8,128)(2,1)}), bf16[8,64,768]{2,1,0:T(8,128)(2,1)S(1)}, u32[]{:S(2)}, u32[]{:S(2)}) async-start(bf16[8,64,768]{2,1,0:T(8,128)(2,1)} %bitcast.269), calls=%async_computation.2 | async-start | bytes 1572864 | tf_op jit(solution)/shard_map/all_to_all | solution.py:138
  168.7 7.9 %copy-start.33 = (f32[8,64,1536]{2,1,0:T(8,128)}, f32[8,64,1536]{2,1,0:T(8,128)S(1)}, u32[]{:S(2)}) copy-start(f32[8,64,1536]{2,1,0:T(8,128)S(1)} %get-tuple-element.114) | copy-start | bytes 9437188
  168.7 9.1 %copy-start.103 = (bf16[1,1536,768]{2,1,0:T(8,128)(2,1)S(1)}, bf16[1,1536,768]{2,1,0:T(8,128)(2,1)}, u32[]{:S(2)}) copy-start(bf16[1,1536,768]{2,1,0:T(8,128)(2,1)} %param.25) | copy-start | bytes 7077892
  186.6 24.0 %all-to-all-start.1 = ((bf16[8,64,768]{2,1,0:T(8,128)(2,1)}), bf16[8,64,768]{2,1,0:T(8,128)(2,1)S(1)}, u32[]{:S(2)}, u32[]{:S(2)}) async-start(bf16[8,64,768]{2,1,0:T(8,128)(2,1)} %fusion.42), calls=%async_computation.1 | async-start | bytes 1572864 | tf_op jit(solution)/shard_map/all_to_all | solution.py:146
  193.4 7.9 %copy-start.34 = (f32[8,64,1536]{2,1,0:T(8,128)}, f32[8,64,1536]{2,1,0:T(8,128)S(1)}, u32[]{:S(2)}) copy-start(f32[8,64,1536]{2,1,0:T(8,128)S(1)} %get-tuple-element.115) | copy-start | bytes 9437188
  193.4 9.1 %copy-start.104 = (bf16[1,1536,768]{2,1,0:T(8,128)(2,1)S(1)}, bf16[1,1536,768]{2,1,0:T(8,128)(2,1)}, u32[]{:S(2)}) copy-start(bf16[1,1536,768]{2,1,0:T(8,128)(2,1)} %param.25) | copy-start | bytes 7077892
  210.6 9.5 %copy-start.27 = (bf16[8,64,768]{2,1,0:T(8,128)(2,1)}, bf16[8,64,768]{2,1,0:T(8,128)(2,1)S(1)}, u32[]{:S(2)}) copy-start(bf16[8,64,768]{2,1,0:T(8,128)(2,1)S(1)} %all-to-all-done.1) | copy-start | bytes 2359300
  210.6 24.1 %all-to-all-start.3 = ((bf16[8,64,768]{2,1,0:T(8,128)(2,1)}), bf16[8,64,768]{2,1,0:T(8,128)(2,1)}, u32[]{:S(2)}, u32[]{:S(2)}) async-start(bf16[8,64,768]{2,1,0:T(8,128)(2,1)} %fusion.45), calls=%async_computation.3 | async-start | bytes 1572864 | tf_op jit(solution)/shard_map/all_to_all | solution.py:146
  239.5 13.3 %copy-start.20 = (bf16[768,4]{1,0:T(8,128)(2,1)S(1)}, bf16[768,4]{1,0:T(8,128)(2,1)}, u32[]{:S(2)}) copy-start(bf16[768,4]{1,0:T(8,128)(2,1)} %copy-done.19) | copy-start | bytes 18436
  239.5 13.3 %copy-start.29 = (bf16[128,768]{1,0:T(8,128)(2,1)S(1)}, bf16[128,768]{1,0:T(8,128)(2,1)}, u32[]{:S(2)}) copy-start(bf16[128,768]{1,0:T(8,128)(2,1)} %copy-done.28) | copy-start | bytes 589828
  248.5 24.0 %all-to-all-start.6 = ((bf16[8,64,768]{2,1,0:T(8,128)(2,1)}), bf16[8,64,768]{2,1,0:T(8,128)(2,1)}, u32[]{:S(2)}, u32[]{:S(2)}) async-start(bf16[8,64,768]{2,1,0:T(8,128)(2,1)} %bitcast.268), calls=%async_computation.6 | async-start | bytes 1572864 | tf_op jit(solution)/shard_map/all_to_all | solution.py:211
  254.3 97.9 %copy-start.87 = (f32[128]{0:T(128)}, f32[128]{0:T(128)S(1)}, u32[]{:S(2)}) copy-start(f32[128]{0:T(128)S(1)} %get-tuple-element.64) | copy-start | bytes 1540
  273.5 24.0 %all-to-all-start.4 = ((bf16[8,64,768]{2,1,0:T(8,128)(2,1)}), bf16[8,64,768]{2,1,0:T(8,128)(2,1)}, u32[]{:S(2)}, u32[]{:S(2)}) async-start(bf16[8,64,768]{2,1,0:T(8,128)(2,1)} %bitcast.270), calls=%async_computation.4 | async-start | bytes 1572864 | tf_op jit(solution)/shard_map/all_to_all | solution.py:211
  297.5 24.0 %all-to-all-start.7 = ((bf16[8,64,768]{2,1,0:T(8,128)(2,1)}), bf16[8,64,768]{2,1,0:T(8,128)(2,1)}, u32[]{:S(2)}, u32[]{:S(2)}) async-start(bf16[8,64,768]{2,1,0:T(8,128)(2,1)} %fusion.39), calls=%async_computation.7 | async-start | bytes 1572864 | tf_op jit(solution)/shard_map/all_to_all | solution.py:229
  321.6 24.0 %all-to-all-start.5 = ((bf16[8,64,768]{2,1,0:T(8,128)(2,1)}), bf16[8,64,768]{2,1,0:T(8,128)(2,1)}, u32[]{:S(2)}, u32[]{:S(2)}) async-start(bf16[8,64,768]{2,1,0:T(8,128)(2,1)} %fusion.36), calls=%async_computation.5 | async-start | bytes 1572864 | tf_op jit(solution)/shard_map/all_to_all | solution.py:229
  325.8 102.1 %reduce-scatter.5.cloned.1.call-start = ((), (), s32[]{:S(2)}) async-start(), calls=%async_computation.13 | async-start | bytes 2654208 | tf_op jit(solution)/shard_map/reduce_scatter | solution.py:315
  350.6 4.8 copy-start.99
  350.6 4.8 copy-start.101
  350.6 4.9 copy-start.23
  350.6 4.9 copy-start.24
  350.6 4.9 copy-start.89
  350.6 4.9 copy-start.91
  359.2 200.6 %reduce-scatter.3.cloned.1.call-start = ((), (), s32[]{:S(2)}) async-start(), calls=%async_computation.12 | async-start | bytes 7962624 | tf_op jit(solution)/shard_map/reduce_scatter | solution.py:314
  371.5 379.8 %all-reduce.4.cloned.1.call-start = ((), (), s32[]{:S(2)}) async-start(), calls=%async_computation.14 | async-start | bytes 21233664 | tf_op jit(solution)/shard_map/psum | solution.py:317
  377.8 5.0 copy-start.38
  566.1 5.3 copy-start.68
  566.1 5.3 copy-start.70
  571.4 47.5 %copy-start.42 = (bf16[128,768]{1,0:T(8,128)(2,1)S(1)}, bf16[128,768]{1,0:T(8,128)(2,1)}, u32[]{:S(2)}) copy-start(bf16[128,768]{1,0:T(8,128)(2,1)} %get-tuple-element.80) | copy-start | bytes 589828
  571.4 47.5 %copy-start.46 = (bf16[128,768]{1,0:T(8,128)(2,1)S(1)}, bf16[128,768]{1,0:T(8,128)(2,1)}, u32[]{:S(2)}) copy-start(bf16[128,768]{1,0:T(8,128)(2,1)} %get-tuple-element.81) | copy-start | bytes 589828
  571.5 48.3 %copy-start.93 = (f32[128]{0:T(128)S(1)}, f32[128]{0:T(128)}, u32[]{:S(2)}) copy-start(f32[128]{0:T(128)} %copy-done.92) | copy-start | bytes 1540
  571.5 48.3 %copy-start.95 = (f32[128]{0:T(128)S(1)}, f32[128]{0:T(128)}, u32[]{:S(2)}) copy-start(f32[128]{0:T(128)} %copy-done.94) | copy-start | bytes 1540
  753.5 6.9 slice-start
  755.3 5.0 slice-start.1
  755.3 7.2 copy-start.1
  (76 other events, 171.4 us)
Sparse Core Ops, SparseCore 0:
  10.2 67.4 all-gather.4
  79.9 39.8 all-gather.6
  359.4 68.5 reduce-scatter.4
  431.5 128.3 reduce-scatter.2
  563.1 188.2 all-reduce.3

commit v2 on v1

--- a/solution.py
+++ b/solution.py
@@ -1,6 +1,10 @@
+import functools
+
 import jax
 import jax.numpy as jnp
 from jax import lax
+from jax.experimental import pallas as pl
+from jax.experimental.pallas import tpu as pltpu
 from jax.sharding import PartitionSpec as P
 
 D = 768
@@ -9,6 +13,750 @@
 FF = 3072
 SEQ = 128
 MB = 2
+MESH = pl.DeviceIdType.MESH
+F32 = jnp.float32
+BF16 = jnp.bfloat16
+NEG = -1e30
+HF = FF // 2
+TOK = MB * SEQ
+EXP = 4
+CAP = 64
+ROWS = MB * CAP
+LOWC = 1152
+EXTRA = D + 128
+WALL = 2 * LOWC + EXTRA
+SHARD = 96
+HALF = SHARD // 2
+PAIRS = HEADS // 2
+SCALE = HEAD ** (-0.5)
+
+
+def place():
+    replica = lax.axis_index("replica")
+    group = lax.axis_index("fsdp")
+    return replica // 2, replica % 2, group // 2, group % 2
+
+
+def device(x, c, z, y):
+    return (x * 2 + c, z * 2 + y)
+
+
+def remote(src, dst, send, recv, target):
+    return pltpu.make_async_remote_copy(
+        src_ref=src,
+        dst_ref=dst,
+        send_sem=send,
+        recv_sem=recv,
+        device_id=target,
+        device_id_type=MESH,
+    )
+
+
+def greet():
+    x, c, z, y = place()
+    barrier = pltpu.get_barrier_semaphore()
+    targets = [device(x, 1 - c, z, y), device(1 - x, c, z, y), device(x, c, z, 1 - y)]
+    targets += [device(x, c, (z + k) % 4, y) for k in (1, 2, 3)]
+    for target in targets:
+        pl.semaphore_signal(barrier, inc=1, device_id=target, device_id_type=MESH)
+    pl.semaphore_wait(barrier, len(targets))
+
+
+def dot(a, b, ca=1, cb=0):
+    return lax.dot_general(a, b, (((ca,), (cb,)), ((), ())), preferred_element_type=F32)
+
+
+GATHER_SEMS = 40
+
+
+def fill_own(wq, wp, sm, wall, local_sem):
+    x, c, z, y = place()
+    own = pl.ds(pl.multiple_of((z * 2 + y) * SHARD, 16), SHARD)
+    fills = [
+        pltpu.make_async_copy(wq.at[:, pl.ds(0, LOWC)], wall.at[own, pl.ds(0, LOWC)], local_sem.at[0]),
+        pltpu.make_async_copy(
+            wq.at[:, pl.ds(LOWC, LOWC)], wall.at[own, pl.ds(LOWC + EXTRA, LOWC)], local_sem.at[1]
+        ),
+        pltpu.make_async_copy(wp, wall.at[own, pl.ds(LOWC, D)], local_sem.at[2]),
+        pltpu.make_async_copy(sm, wall.at[own, pl.ds(LOWC + D, 128)], local_sem.at[3]),
+    ]
+    for fill in fills:
+        fill.start()
+    for fill in fills:
+        fill.wait()
+
+
+def gather_weights(wall, send_sem, recv_sem):
+    x, c, z, y = place()
+    plane = pl.ds(pl.multiple_of(x * LOWC, 128), LOWC + EXTRA)
+    share = pl.ds(pl.multiple_of(x * (LOWC + EXTRA), 128), LOWC)
+    gained = pl.ds(pl.multiple_of((1 - x) * (LOWC + EXTRA), 128), LOWC)
+    up, down = device(x, c, z + 1, y), device(x, c, z - 1, y)
+    across, facing, twin = device(x, c, z, 1 - y), device(1 - x, c, z, y), device(x, 1 - c, z, y)
+    started = []
+
+    def part(zs, ys, half, cols):
+        return wall.at[pl.ds(pl.multiple_of((zs * 2 + ys) * SHARD + half * HALF, 16), HALF), cols]
+
+    def run(cond, what):
+        if cond is None:
+            what()
+        else:
+            pl.when(cond)(what)
+
+    def go(cond, zs, ys, cols, send, recv, target):
+        piece = part(zs, ys, c, cols)
+        copy = remote(piece, piece, send_sem.at[send], recv_sem.at[recv], target)
+        run(cond, copy.start)
+        started.append((cond, copy))
+
+    def arrive(cond, zs, ys, half, cols, recv):
+        piece = part(zs, ys, half, cols)
+        copy = remote(piece, piece, send_sem.at[0], recv_sem.at[recv], twin)
+        run(cond, copy.wait_recv)
+
+    def spread(cond, zs, ys, k):
+        source = zs * 2 + ys
+        go(cond, zs, ys, share, 13 + source, 8 + source, facing)
+        go(cond, zs, ys, plane, 21 + source, 16 + source, twin)
+
+    go(z < 3, z, y, plane, 0, z, up)
+    go(z > 0, z, y, plane, 3, z, down)
+    go(None, z, y, plane, 6, 4 + z, across)
+    for k in (1, 2, 3):
+        below, above = z - k, z + k
+        for cond, zs, on, send, target in (
+            (below >= 0, below, z < 3, k, up),
+            (above <= 3, above, z > 0, 3 + k, down),
+        ):
+            arrive(cond, zs, y, c, plane, zs)
+            if k < 3:
+                go(cond & on, zs, y, plane, send, zs, target)
+            go(cond, zs, y, plane, 6 + (k if target is up else 3 + k), 4 + zs, across)
+            spread(cond, zs, y, k)
+        if k == 1:
+            arrive(None, z, 1 - y, c, plane, 4 + z)
+            spread(None, z, 1 - y, 0)
+        else:
+            for cond, zs in ((z - k + 1 >= 0, z - k + 1), (z + k - 1 <= 3, z + k - 1)):
+                arrive(cond, zs, 1 - y, c, plane, 4 + zs)
+                spread(cond, zs, 1 - y, 0)
+    for cond, zs in ((z == 3, z - 3), (z == 0, z + 3)):
+        arrive(cond, zs, 1 - y, c, plane, 4 + zs)
+        spread(cond, zs, 1 - y, 0)
+    for zs in range(4):
+        for ys in range(2):
+            source = zs * 2 + ys
+            other = (zs != z) | (ys != y)
+            arrive(other, zs, ys, c, gained, 8 + source)
+            go(other, zs, ys, gained, 29 + source, 24 + source, twin)
+    for zs in range(4):
+        for ys in range(2):
+            source = zs * 2 + ys
+            other = (zs != z) | (ys != y)
+            arrive(other, zs, ys, 1 - c, plane, 16 + source)
+            arrive(other, zs, ys, 1 - c, gained, 24 + source)
+    return started
+
+
+def finish(started):
+    for cond, copy in started:
+        if cond is None:
+            copy.wait_send()
+        else:
+            pl.when(cond)(copy.wait_send)
+
+
+def unit(values):
+    return lax.rsqrt(jnp.mean(values * values, axis=-1, keepdims=True) + 1e-06)
+
+
+def build_bias(wall, bias):
+    table = jnp.concatenate(
+        [wall[f * SHARD : f * SHARD + 16, LOWC + D : LOWC + EXTRA] for f in range(8)], axis=0
+    )
+    ahead = lax.broadcasted_iota(jnp.int32, (SEQ, SEQ), 0)
+    lane = lax.broadcasted_iota(jnp.int32, (SEQ, SEQ), 1)
+    turned = jnp.where(ahead + lane == SEQ, 1.0, jnp.where(ahead + lane == 0, 1.0, 0.0)).astype(BF16)
+    lines = dot(table, turned, 0, 0)
+    for h in range(HEADS):
+        line = jnp.broadcast_to(lines[HEAD + h : HEAD + h + 1, :], (SEQ, SEQ))
+        rolled = pltpu.roll(line, 0, 1, stride=1, stride_axis=0)
+        bias[(h // 2) * SEQ : (h // 2 + 1) * SEQ, (h % 2) * SEQ : (h % 2 + 1) * SEQ] = jnp.where(ahead >= lane, rolled, NEG)
+
+
+def routing(routes, slots, s):
+    rows = slice(s * SEQ, (s + 1) * SEQ)
+    lane = lax.broadcasted_iota(jnp.int32, (SEQ, EXP * CAP), 1)
+    spots = routes[rows, :] * CAP + slots[rows, :]
+    return spots[:, 0:1] == lane, spots[:, 1:2] == lane
+
+
+def live_column(lengths, s):
+    return lax.broadcasted_iota(jnp.int32, (SEQ, 1), 0) < lengths[s]
+
+
+def attention_forward(
+    x_ref, cot, lengths, routes, slots, wall, rows_t, board, normed, qkv, attended, hidden, normed2, gates,
+    out_f, out_g,
+):
+    rows_t[...] = jnp.transpose(wall[:, LOWC + D : LOWC + EXTRA].astype(F32))[0:8]
+    build_bias(wall, board)
+    x = x_ref[...].astype(F32)
+    normed[...] = (x * unit(x) * rows_t[0:1, :]).astype(BF16)
+    qkv[:, 0:LOWC] = dot(normed[...], wall[:, 0:LOWC]).astype(BF16)
+    qkv[:, LOWC : 2 * LOWC] = dot(normed[...], wall[:, LOWC + EXTRA : WALL]).astype(BF16)
+    lane = lax.broadcasted_iota(jnp.int32, (SEQ, 128), 1)
+
+    def pair(p, carry):
+        blocks = pl.ds(pl.multiple_of(p * SEQ, SEQ), SEQ)
+        for s in range(MB):
+            rows = slice(s * SEQ, (s + 1) * SEQ)
+            q = qkv[rows, pl.ds(pl.multiple_of(p * 128, 128), 128)]
+            k = qkv[rows, pl.ds(pl.multiple_of(D + p * 128, 128), 128)]
+            v = qkv[rows, pl.ds(pl.multiple_of(2 * D + p * 128, 128), 128)]
+            alive = lane < lengths[s]
+            got = []
+            for j in range(2):
+                mine = (lane < HEAD) if j == 0 else (lane >= HEAD)
+                raw = dot(jnp.where(mine, q, jnp.zeros_like(q)), k, 1, 1)
+                scores = jnp.where(alive, raw * SCALE + board[blocks, j * SEQ : (j + 1) * SEQ], NEG)
+                scores = jnp.exp(scores - jnp.max(scores, axis=-1, keepdims=True))
+                share = scores / jnp.sum(scores, axis=-1, keepdims=True)
+                board[blocks, (2 + 2 * s + j) * SEQ : (3 + 2 * s + j) * SEQ] = share
+                got.append(dot(share.astype(BF16), v))
+            attended[rows, pl.ds(pl.multiple_of(p * 128, 128), 128)] = jnp.where(
+                lane < HEAD, got[0], got[1]
+            ).astype(BF16)
+        return carry
+
+    lax.fori_loop(0, PAIRS, pair, 0)
+    branch = dot(attended[...], wall[:, LOWC : LOWC + D])
+    for s in range(MB):
+        rows = slice(s * SEQ, (s + 1) * SEQ)
+        live = live_column(lengths, s)
+        state = x_ref[rows, :].astype(F32) + jnp.where(live, branch[rows, :], 0.0)
+        hidden[rows, :] = state
+        low = (state * unit(state) * rows_t[1:2, :]).astype(BF16)
+        normed2[rows, :] = low
+        logits = dot(low, wall[:, LOWC + D : LOWC + EXTRA])
+        kind = lane - 2
+        picked = jnp.where(kind == routes[rows, 0:1], logits, 0.0) - jnp.where(
+            kind == routes[rows, 1:2], logits, 0.0
+        )
+        gate = jax.nn.sigmoid(jnp.sum(picked, axis=-1, keepdims=True))
+        gates[rows, :] = gate
+        grad = jnp.where(live, cot[rows, :].astype(F32), 0.0)
+        first, second = routing(routes, slots, s)
+        first = jnp.where(first & live, 1.0, 0.0).astype(BF16)
+        second = jnp.where(second & live, 1.0, 0.0).astype(BF16)
+        sent = dot(first + second, low, 0, 0).astype(BF16)
+        back = dot(first, (gate * grad).astype(BF16), 0, 0) + dot(
+            second, ((1.0 - gate) * grad).astype(BF16), 0, 0
+        )
+        back = back.astype(BF16)
+        for e in range(EXP):
+            out_f[e, s * CAP : (s + 1) * CAP, :] = sent[e * CAP : (e + 1) * CAP, :]
+            out_g[e, s * CAP : (s + 1) * CAP, :] = back[e * CAP : (e + 1) * CAP, :]
+
+
+class Links:
+    def __init__(self, send_sem, recv_sem):
+        self.send_sem, self.recv_sem = send_sem, recv_sem
+        self.started = []
+
+    def go(self, cond, src, dst, send, recv, target):
+        copy = remote(src, dst, self.send_sem.at[send], self.recv_sem.at[recv], target)
+        run(cond, copy.start)
+        self.started.append((cond, copy))
+        return copy
+
+    def arrive(self, cond, dst, recv, target):
+        run(cond, remote(dst, dst, self.send_sem.at[0], self.recv_sem.at[recv], target).wait_recv)
+
+    def leave(self, copy):
+        copy.wait_send()
+        self.started = [(cond, item) for cond, item in self.started if item is not copy]
+
+    def finish(self):
+        for cond, copy in self.started:
+            run(cond, copy.wait_send)
+        self.started = []
+
+
+def run(cond, what):
+    if cond is None:
+        what()
+    else:
+        pl.when(cond)(what)
+
+
+TILE = 512
+Z_ROWS, Y_ROWS, Y_PART, Z_BACK = 40, 48, 56, 64
+TWIN_W, FACE_W, TWIN_OUT = 72, 74, 76
+RS_TWIN, RS_Y, RS_Z, RS_FACE, RS_OUT = 78, 80, 84, 92, 93
+LINKS = 96
+
+
+def quarter(zs):
+    return pl.ds(pl.multiple_of(zs * 2 * ROWS, 2 * ROWS), 2 * ROWS)
+
+
+def half_rows(zs, ys):
+    return pl.ds(pl.multiple_of((zs * 2 + ys) * ROWS, ROWS), ROWS)
+
+
+def expert_forward(zs, recv, up, down, act, slope, part):
+    rows = quarter(zs)
+
+    def tile(i, carry):
+        cols = pl.ds(pl.multiple_of(i * TILE, TILE), TILE)
+        before = dot(recv[rows, :], up[:, cols])
+        below = 0.5 + 0.5 * lax.erf(before * 0.7071067811865476)
+        act[rows, cols] = (before * below).astype(BF16)
+        density = jnp.exp(before * before * -0.5) * 0.3989422804014327
+        slope[rows, cols] = (below + before * density).astype(BF16)
+        return carry
+
+    lax.fori_loop(0, HF // TILE, tile, 0)
+    got = dot(act[rows, 0:HF], down[...]).astype(BF16)
+    part[zs, 0] = got[0:ROWS]
+    part[zs, 1] = got[ROWS : 2 * ROWS]
+
+
+def expert_backward(zs, recv, up, down, slope, part):
+    rows = quarter(zs)
+
+    def tile(i, carry):
+        cols = pl.ds(pl.multiple_of(i * TILE, TILE), TILE)
+        grad = dot(recv[rows, :], down[cols, :], 1, 1)
+        slope[rows, cols] = (grad * slope[rows, cols].astype(F32)).astype(BF16)
+        return carry
+
+    lax.fori_loop(0, HF // TILE, tile, 0)
+    got = dot(slope[rows, :], up[...], 1, 1).astype(BF16)
+    part[zs, 0] = got[0:ROWS]
+    part[zs, 1] = got[ROWS : 2 * ROWS]
+
+
+def experts(links, out, recv, up, down, act, slope, part, take, back, w_down, w_up):
+    x, c, z, y = place()
+    across, facing, twin = device(x, c, z, 1 - y), device(1 - x, c, z, y), device(x, 1 - c, z, y)
+
+    for kind in range(2):
+        links.go(None, out[kind].at[z], recv[kind].at[half_rows(z, y), :], Y_ROWS + kind * 4, Y_ROWS + kind * 4 + z, across)
+        for d in (1, 2, 3):
+            to = (z + d) % 4
+            links.go(
+                None, out[kind].at[to], recv[kind].at[half_rows(z, y), :], Z_ROWS + kind * 4 + d,
+                Z_ROWS + kind * 4 + z, device(x, c, to, y),
+            )
+        recv[kind][half_rows(z, y), :] = out[kind][z]
+
+    def source(d):
+        return (z + 4 - d) % 4
+
+    def reach(kind, d):
+        zs = source(d)
+        rows = recv[kind].at[half_rows(zs, y), :]
+        links.arrive(None, rows, Z_ROWS + kind * 4 + zs, across)
+        links.go(None, rows, rows, Y_ROWS + kind * 4 + d, Y_ROWS + kind * 4 + zs, across)
+
+    def compute(kind, d):
+        zs = source(d)
+        links.arrive(None, recv[kind].at[half_rows(zs, 1 - y), :], Y_ROWS + kind * 4 + zs, across)
+        if kind == 0:
+            expert_forward(zs, recv[0], up, down, act, slope, part[0])
+        else:
+            expert_backward(zs, recv[1], up, down, slope, part[1])
+        links.go(
+            None, part[kind].at[zs, 1 - y], take[kind].at[zs], Y_PART + kind * 4 + d, Y_PART + kind * 4 + zs, across
+        )
+
+    def merge(kind, d):
+        zs = source(d)
+        links.arrive(None, take[kind].at[zs], Y_PART + kind * 4 + zs, across)
+        total = (part[kind][zs, y].astype(F32) + take[kind][zs].astype(F32)).astype(BF16)
+        if d == 0:
+            back[kind][z] = total
+        else:
+            part[kind][zs, y] = total
+            links.go(
+                None, part[kind].at[zs, y], back[kind].at[z], Z_BACK + kind * 4 + d, Z_BACK + kind * 4 + z,
+                device(x, c, zs, y),
+            )
+
+    compute(0, 0)
+    reach(0, 1)
+    compute(1, 0)
+    reach(0, 2)
+    compute(0, 1)
+    merge(0, 0)
+    reach(0, 3)
+    compute(0, 2)
+    merge(1, 0)
+    merge(0, 1)
+    reach(1, 1)
+    compute(0, 3)
+    merge(0, 2)
+    reach(1, 2)
+    compute(1, 1)
+    merge(0, 3)
+    reach(1, 3)
+    compute(1, 2)
+    merge(1, 1)
+    compute(1, 3)
+    merge(1, 2)
+
+    def down_tile(i, part_of, keep):
+        cols = pl.ds(pl.multiple_of(part_of * (HF // 2) + i * 256, 128), 256)
+        got = dot(act[:, cols], recv[1][...], 0, 0)
+        keep[pl.ds(pl.multiple_of(i * 256, 256), 256), :] = got.astype(keep.dtype)
+
+    def up_tile(i, part_of, keep):
+        cols = pl.ds(pl.multiple_of(part_of * (D // 2) + i * 128, 128), 128)
+        got = dot(recv[0][:, cols], slope[...], 0, 0)
+        keep[pl.ds(pl.multiple_of(i * 128, 128), 128), :] = got.astype(keep.dtype)
+
+    def tiles(one, part_of, keep):
+        def step(i, carry):
+            one(i, part_of, keep)
+            return carry
+
+        lax.fori_loop(0, 3, step, 0)
+
+    sent = []
+    for i, (one, w) in enumerate(((down_tile, w_down), (up_tile, w_up))):
+        own, give, got, face = w
+        tiles(one, 1 - c, give)
+        sent.append(links.go(None, give, got, TWIN_W + i, TWIN_W + i, twin))
+        if i == 0:
+            merge(1, 3)
+        tiles(one, c, own)
+        links.arrive(None, got, TWIN_W + i, twin)
+        links.leave(sent[i])
+        give[...] = (own[...] + got[...].astype(F32)).astype(BF16)
+        links.go(None, give, face, FACE_W + i, FACE_W + i, facing)
+    for kind in range(2):
+        for d in (1, 2, 3):
+            zs = source(d)
+            links.arrive(None, back[kind].at[zs], Z_BACK + kind * 4 + zs, across)
+
+
+def expert_grads_out(links, w_down, w_up, out_down, out_up, local_sem):
+    x, c, z, y = place()
+    facing, twin = device(1 - x, c, z, y), device(x, 1 - c, z, y)
+    pending = []
+    for i, (w, target) in enumerate(((w_down, out_down), (w_up, out_up))):
+        own, give, got, face = w
+        count = own.shape[0]
+        links.arrive(None, face, FACE_W + i, facing)
+        own[...] = give[...].astype(F32) + face[...].astype(F32)
+        rows = pl.ds(pl.multiple_of(c * count, 128), count)
+        links.go(None, own, target.at[rows, :], TWIN_OUT + i, TWIN_OUT + i, twin)
+        copy = pltpu.make_async_copy(own, target.at[rows, :], local_sem.at[i])
+        copy.start()
+        pending.append(copy)
+    for i, (w, target) in enumerate(((w_down, out_down), (w_up, out_up))):
+        count = w[0].shape[0]
+        rows = pl.ds(pl.multiple_of((1 - c) * count, 128), count)
+        links.arrive(None, target.at[rows, :], TWIN_OUT + i, twin)
+    return pending
+
+
+OWNC = 2 * D
+SENTC = OWNC + 128
+
+
+def combine(cot, lengths, routes, slots, rows_t, hidden, normed2, gates, back_f, back_g, mixed, rb, small_t):
+    lane = lax.broadcasted_iota(jnp.int32, (SEQ, 128), 1)
+    gain_grad = jnp.zeros((1, D), F32)
+    router_grad = jnp.zeros((128, D), F32)
+    for s in range(MB):
+        rows = slice(s * SEQ, (s + 1) * SEQ)
+        live = live_column(lengths, s)
+        first, second = routing(routes, slots, s)
+        first = jnp.where(first, 1.0, 0.0).astype(BF16)
+        second = jnp.where(second, 1.0, 0.0).astype(BF16)
+        given = jnp.concatenate([back_f[e, s * CAP : (s + 1) * CAP, :] for e in range(EXP)], axis=0)
+        first_out = dot(first, given)
+        second_out = dot(second, given)
+        gate = gates[rows, :]
+        grad = cot[rows, :].astype(F32)
+        grad_live = jnp.where(live, grad, 0.0)
+        state = hidden[rows, :]
+        moe = gate * first_out + (1.0 - gate) * second_out
+        mixed[rows, :] = (state + jnp.where(live, moe, 0.0)).astype(BF16)
+        tilt = jnp.sum(grad_live * first_out, axis=-1, keepdims=True) - jnp.sum(
+            grad_live * second_out, axis=-1, keepdims=True
+        )
+        tilt = tilt * gate * (1.0 - gate)
+        kind = lane - 2
+        hot = jnp.where(kind == routes[rows, 0:1], 1.0, 0.0) - jnp.where(kind == routes[rows, 1:2], 1.0, 0.0)
+        grad_logits = tilt * hot
+        high = grad_logits.astype(BF16)
+        low = (grad_logits - high.astype(F32)).astype(BF16)
+        router_grad = router_grad + dot(high, normed2[rows, :], 0, 0) + dot(low, normed2[rows, :], 0, 0)
+        given = jnp.concatenate([back_g[e, s * CAP : (s + 1) * CAP, :] for e in range(EXP)], axis=0)
+        grad_low = jnp.where(live, dot(first + second, given), 0.0)
+        for e in range(EXP):
+            grad_low = grad_low + grad_logits[:, 2 + e : 3 + e] * rows_t[2 + e : 3 + e, :]
+        factor = unit(state)
+        scaled = state * factor
+        gain_grad = gain_grad + jnp.sum(grad_low * scaled, axis=0, keepdims=True)
+        grad_low = grad_low * rows_t[1:2, :]
+        inner = jnp.mean(grad_low * scaled, axis=-1, keepdims=True)
+        grad_state = grad + factor * (grad_low - scaled * inner)
+        hidden[rows, :] = grad_state
+        rb[rows, 3 * D : 4 * D] = jnp.where(live, grad_state, 0.0).astype(BF16)
+    small_t[...] = router_grad
+    small_t[1:2, :] = gain_grad
+
+
+def attention_backward(x_ref, wall, rows_t, left, qkv, board, hidden, grad_att, rb, rel_rows, small_t, grad_tokens):
+    grad_att[...] = dot(rb[:, 3 * D : 4 * D], wall[:, LOWC : LOWC + D], 1, 1).astype(BF16)
+    lane = lax.broadcasted_iota(jnp.int32, (SEQ, 128), 1)
+    ahead = lax.broadcasted_iota(jnp.int32, (SEQ, 128), 0)
+    flip = jnp.where(ahead + lane == SEQ - 1, 1.0, 0.0).astype(BF16)
+    flip = jnp.concatenate([flip] * MB, axis=1)
+
+    def pair(p, carry):
+        blocks = pl.ds(pl.multiple_of(p * SEQ, SEQ), SEQ)
+        scores = [[None] * MB, [None] * MB]
+        for s in range(MB):
+            rows = slice(s * SEQ, (s + 1) * SEQ)
+            cols = [pl.ds(pl.multiple_of(i * D + p * 128, 128), 128) for i in range(3)]
+            q, k, v = (qkv[rows, cols[i]] for i in range(3))
+            grad = grad_att[rows, cols[0]]
+            grads = [[], [], []]
+            for j in range(2):
+                mine = (lane < HEAD) if j == 0 else (lane >= HEAD)
+                share = board[blocks, (2 + 2 * s + j) * SEQ : (3 + 2 * s + j) * SEQ]
+                grad_probs = dot(jnp.where(mine, grad, jnp.zeros_like(grad)), v, 1, 1)
+                inner = jnp.sum(share * grad_probs, axis=-1, keepdims=True)
+                grad_scores = (share * (grad_probs - inner)).astype(BF16)
+                scores[j][s] = grad_scores
+                grads[0].append(dot(grad_scores, k) * SCALE)
+                grads[1].append(dot(grad_scores, q, 0, 0) * SCALE)
+                grads[2].append(dot(share.astype(BF16), grad, 0, 0))
+            for i in range(3):
+                rb[rows, cols[i]] = jnp.where(lane < HEAD, grads[i][0], grads[i][1]).astype(BF16)
+        for j in range(2):
+            flipped = dot(flip, jnp.concatenate(scores[j], axis=0))
+            rolled = pltpu.roll(flipped, 1, 1, stride=1, stride_axis=0)
+            rel_rows[pl.ds(2 * p + j, 1), :] = jnp.sum(rolled, axis=0, keepdims=True)
+        return carry
+
+    lax.fori_loop(0, PAIRS, pair, 0)
+    grad_low = dot(rb[:, 0:LOWC], wall[:, 0:LOWC], 1, 1) + dot(
+        rb[:, LOWC : 2 * LOWC], wall[:, LOWC + EXTRA : WALL], 1, 1
+    )
+    state = x_ref[...].astype(F32)
+    factor = unit(state)
+    scaled = state * factor
+    small_t[0:1, :] = jnp.sum(grad_low * scaled, axis=0, keepdims=True)
+    grad_low = grad_low * rows_t[0:1, :]
+    inner = jnp.mean(grad_low * scaled, axis=-1, keepdims=True)
+    grad_tokens[...] = hidden[...] + factor * (grad_low - scaled * inner)
+
+    spot = lax.broadcasted_iota(jnp.int32, (SEQ, D), 0)
+    column = lax.broadcasted_iota(jnp.int32, (SEQ, D), 1)
+    distance = (SEQ - spot) & (SEQ - 1)
+    picks = jnp.where(column == (distance >> 4) * SHARD + (distance & 15), 1.0, 0.0).astype(BF16)
+    rest = rel_rows[...]
+    spread = jnp.zeros((16, D), F32)
+    for _ in range(3):
+        high = rest.astype(BF16)
+        spread = spread + dot(high, picks)
+        rest = rest - high.astype(F32)
+    small_t[HEAD : HEAD + 16, :] = spread
+
+
+def reduce_grads(links, left, rb, small_t, give, take, total, y_take, z_take, face_give, face_take, last, out_qkv, out_proj, out_small, local_sem):
+    x, c, z, y = place()
+    across, facing, twin = device(x, c, z, 1 - y), device(1 - x, c, z, y), device(x, 1 - c, z, y)
+    up, down = device(x, c, z + 1, y), device(x, c, z - 1, y)
+
+    def tile(core, i, keep):
+        def step(m, carry):
+            rows = pl.ds(pl.multiple_of(m * 256, 256), 256)
+            rhs = rb[:, pl.ds(pl.multiple_of((2 * core + i) * D, 128), D)]
+            keep[rows, i * D : (i + 1) * D] = dot(left[core * i, :, rows], rhs, 0, 0).astype(keep.dtype)
+            return carry
+
+        lax.fori_loop(0, 3, step, 0)
+
+    for i in range(2):
+        tile(1 - c, i, give)
+    small = jnp.transpose(small_t[...])
+    give[:, OWNC:SENTC] = small.astype(BF16)
+    first = links.go(None, give, take, RS_TWIN, RS_TWIN, twin)
+    for i in range(2):
+        tile(c, i, total)
+    total[:, OWNC:SENTC] = small.astype(BF16).astype(F32)
+    links.arrive(None, take, RS_TWIN, twin)
+    links.leave(first)
+    mirror = z // 2
+    near = z + mirror * (3 - 2 * z)
+    order = [o + mirror * (3 - 2 * o) for o in (3, 2, 1 - near, near)]
+
+    def shard(zs, ys):
+        return pl.ds(pl.multiple_of((zs * 2 + ys) * SHARD, 16), SHARD)
+
+    for zs in order:
+        rows = shard(zs, 1 - y)
+        give[rows, :] = (total[rows, :] + take[rows, :].astype(F32)).astype(BF16)
+        links.go(None, give.at[rows, :], y_take.at[zs], RS_Y + zs, RS_Y + zs, across)
+    for zs in order:
+        rows = shard(zs, y)
+        total[rows, :] = total[rows, :] + take[rows, :].astype(F32)
+    for k, zs in enumerate(order):
+        rows = shard(zs, y)
+        links.arrive(None, y_take.at[zs], RS_Y + zs, across)
+        total[rows, :] = total[rows, :] + y_take[zs].astype(F32)
+        if k < 3:
+            climbs, sinks = zs > z, zs < z
+            for cond, more, slot, target in ((climbs, z > 0, zs, up), (sinks, z < 3, 4 + zs, down)):
+
+                @pl.when(cond & more)
+                def _():
+                    links.arrive(None, z_take.at[slot], RS_Z + slot, across)
+                    total[rows, :] = total[rows, :] + z_take[slot].astype(F32)
+
+                @pl.when(cond)
+                def _():
+                    give[rows, :] = total[rows, :].astype(BF16)
+
+                links.go(cond, give.at[rows, :], z_take.at[slot], RS_Z + slot, RS_Z + slot, target)
+    rows = shard(z, y)
+    for cond, slot in ((z > 0, z), (z < 3, 4 + z)):
+
+        @pl.when(cond)
+        def _():
+            links.arrive(None, z_take.at[slot], RS_Z + slot, across)
+            total[rows, :] = total[rows, :] + z_take[slot].astype(F32)
+
+    face_give[...] = total[rows, :].astype(BF16)
+    links.go(None, face_give, face_take, RS_FACE, RS_FACE, facing)
+    links.arrive(None, face_take, RS_FACE, facing)
+    last[...] = face_give[...].astype(F32) + face_take[...].astype(F32)
+    pieces = (
+        (c == 0, slice(0, OWNC), out_qkv.at[:, 0:OWNC], 0),
+        (c == 1, slice(0, D), out_qkv.at[:, OWNC : 3 * D], 1),
+        (c == 1, slice(D, OWNC), out_proj, 2),
+    )
+    pending = []
+    for cond, cols, target, i in pieces:
+        links.go(cond, last.at[:, cols], target, RS_OUT + i, RS_OUT + i, twin)
+        copy = pltpu.make_async_copy(last.at[:, cols], target, local_sem.at[2 + i])
+        run(cond, copy.start)
+        pending.append((cond, copy))
+    copy = pltpu.make_async_copy(last.at[:, OWNC:SENTC], out_small, local_sem.at[5])
+    copy.start()
+    pending.append((None, copy))
+    for cond, cols, target, i in pieces:
+        links.arrive((c == 1) if i == 0 else (c == 0), target, RS_OUT + i, twin)
+    return pending
+
+
+def layer(
+    x_ref, cot, lengths, routes, slots, wq, wp, sm, w_up, w_down,
+    mixed, grad_tokens, out_qkv, out_proj, out_small, out_up, out_down,
+    wall, rows_t, left, qkv, hidden, normed2, gates, out_f, out_g, recv_f, recv_g, up, down, act, slope,
+    part_f, part_g, take_f, take_g, back_f, back_g, dn_own, dn_give, dn_take, dn_face, up_own, up_give, up_take, up_face,
+    rb, rel_rows, small_t, take, total, y_take, z_take, face_give, face_take, last,
+    local_sem, send_sem, recv_sem,
+):
+    fetch = [
+        pltpu.make_async_copy(w_up.at[0], up, local_sem.at[4]),
+        pltpu.make_async_copy(w_down.at[0], down, local_sem.at[5]),
+    ]
+    for copy in fetch:
+        copy.start()
+    greet()
+    fill_own(wq, wp, sm, wall, local_sem)
+    links = Links(send_sem, recv_sem)
+    links.started += gather_weights(wall, send_sem, recv_sem)
+    normed, attended = left.at[0], left.at[1]
+    attention_forward(
+        x_ref, cot, lengths, routes, slots, wall, rows_t, total, normed, qkv, attended, hidden, normed2, gates,
+        out_f, out_g,
+    )
+    for copy in fetch:
+        copy.wait()
+    downs, ups = (dn_own, dn_give, dn_take, dn_face), (up_own, up_give, up_take, up_face)
+    experts(
+        links, (out_f, out_g), (recv_f, recv_g), up, down, act, slope, (part_f, part_g), (take_f, take_g),
+        (back_f, back_g), downs, ups,
+    )
+    rel_rows[...] = jnp.zeros_like(rel_rows)
+    combine(cot, lengths, routes, slots, rows_t, hidden, normed2, gates, back_f, back_g, mixed, rb, small_t)
+    attention_backward(x_ref, wall, rows_t, left, qkv, total, hidden, normed2, rb, rel_rows, small_t, grad_tokens)
+    pending = reduce_grads(
+        links, left, rb, small_t, act.at[0:D, :], take, total, y_take, z_take, face_give, face_take, last, out_qkv, out_proj,
+        out_small, local_sem,
+    )
+    more = expert_grads_out(links, downs, ups, out_down, out_up, local_sem)
+    for cond, copy in pending + [(None, copy) for copy in more]:
+        run(cond, copy.wait)
+    links.finish()
+
+
+def pack_small(gain_attn, gain_moe, w_router, rel_table):
+    table = jnp.pad(rel_table, ((0, SHARD - rel_table.shape[0]), (0, 64 - HEADS)))
+    side = jnp.concatenate([gain_attn[:, None], gain_moe[:, None], w_router], axis=1)
+    return jnp.concatenate([jnp.pad(side, ((0, 0), (0, 64 - side.shape[1]))), table], axis=1)
+
+
+def body_fast(
+    tokens, cotangent, lengths, routes, slots, gain_attn, w_qkv, w_proj, rel_table, gain_moe, w_router, w_up, w_down
+):
+    small = pack_small(gain_attn, gain_moe, w_router, rel_table)
+    vm = pl.BlockSpec(memory_space=pltpu.VMEM)
+    hbm = pl.BlockSpec(memory_space=pl.ANY)
+    sds = jax.ShapeDtypeStruct
+    v = pltpu.VMEM
+    out = pl.pallas_call(
+        layer,
+        out_shape=(
+            sds((TOK, D), BF16), sds((TOK, D), F32), sds((SHARD, 3 * D), F32), sds((SHARD, D), F32),
+            sds((SHARD, 128), F32), sds((D, HF), F32), sds((HF, D), F32),
+        ),
+        in_specs=[vm, vm, pl.BlockSpec(memory_space=pltpu.SMEM), vm, vm, hbm, hbm, hbm, hbm, hbm],
+        out_specs=[vm, vm, hbm, hbm, hbm, hbm, hbm],
+        scratch_shapes=[
+            v((D, WALL), BF16), v((8, D), F32), v((2, TOK, D), BF16),
+            v((TOK, 3 * D), BF16), v((TOK, D), F32), v((TOK, D), BF16),
+            v((TOK, 1), F32), v((EXP, ROWS, D), BF16), v((EXP, ROWS, D), BF16),
+            v((8 * ROWS, D), BF16), v((8 * ROWS, D), BF16), v((D, HF), BF16), v((HF, D), BF16),
+            v((8 * ROWS, SENTC), BF16), v((8 * ROWS, HF), BF16),
+            v((EXP, 2, ROWS, D), BF16), v((EXP, 2, ROWS, D), BF16), v((EXP, ROWS, D), BF16), v((EXP, ROWS, D), BF16),
+            v((EXP, ROWS, D), BF16), v((EXP, ROWS, D), BF16),
+            v((HF // 2, D), F32), v((HF // 2, D), BF16), v((HF // 2, D), BF16), v((HF // 2, D), BF16),
+            v((D // 2, HF), F32), v((D // 2, HF), BF16), v((D // 2, HF), BF16), v((D // 2, HF), BF16),
+            v((TOK, 4 * D), BF16), v((16, SEQ), F32), v((128, D), F32),
+            v((D, SENTC), BF16), v((D, SENTC), F32), v((4, SHARD, SENTC), BF16), v((8, SHARD, SENTC), BF16),
+            v((SHARD, SENTC), BF16), v((SHARD, SENTC), BF16), v((SHARD, SENTC), F32),
+            pltpu.SemaphoreType.DMA((6,)), pltpu.SemaphoreType.DMA((LINKS,)), pltpu.SemaphoreType.DMA((LINKS,)),
+        ],
+        compiler_params=pltpu.CompilerParams(
+            collective_id=0, has_side_effects=True, vmem_limit_bytes=67043328
+        ),
+        name="layer",
+    )(tokens, cotangent, lengths, routes, slots, w_qkv, w_proj, small, w_up, w_down)
+    mixed, grad_tokens, grad_qkv, grad_proj, side, grad_up, grad_down = out
+    return (
+        mixed,
+        grad_tokens,
+        side[:, 0],
+        grad_qkv,
+        grad_proj,
+        side[: rel_table.shape[0], HEAD : HEAD + HEADS],
+        side[:, 1],
+        side[:, 2 : 2 + EXP],
+        grad_up[None],
+        grad_down[None],
+    )
 
 
 epsilon = 1e-06
@@ -371,4 +1119,5 @@
         P("fsdp", None, None),
         P("fsdp", None, None),
     )
-    return jax.shard_map(body, mesh=mesh, in_specs=in_specs, out_specs=out_specs, check_vma=False)
+    fast = dict(mesh.shape) == {"replica": 4, "fsdp": 8}
+    return jax.shard_map(body_fast if fast else body, mesh=mesh, in_specs=in_specs, out_specs=out_specs, check_vma=False)

time: 778 us -> 218 us (0.28)
  waiting for transfers between devices: 436 us -> 0 us
  Pallas kernels: 0 us -> 192 us
  matrix products: 93.8 us -> 0 us
  blocking collectives: 74.1 us -> 0 us
  other arithmetic: 55.4 us -> 2.08 us
  local copies, waits for them, and re-layouts: 60.6 us -> 22.5 us
  starting transfers between devices: 33.6 us -> 0 us
  between operations: 15.9 us -> 0.66 us
    pallas_call x0 -> x1, Pallas kernels: none -> 192 us  [body_fast(): pl.pallas_call(layer, out_shape=(sds((TOK, D), BF16), sds((TOK, D), F32),...]
    reduce_scatter x2 -> x0, waiting for transfers between devices: 172 us -> none  [the longest x1 132 us: body(): lax.psum_scatter(grad_qkv_w, 'fsdp', scatter_dimension=0, tiled=True)]
    psum x1 -> x0, waiting for transfers between devices: 130 us -> none  [body(): lax.psum((shards[0], shards[1], shards[2], grad_up[None], grad_down[None]...]
    dot_general x45 -> x0, matrix products: 93.8 us -> none  [the longest x2 11.7 us: body(): jnp.einsum('scd,fd->scf', grad_recv, down_weight, preferred_element_type=...]
    all_to_all x8 -> x0, waiting for transfers between devices: 87.1 us -> none  [the longest x2 25.5 us: body(): lax.all_to_all(grad_send, 'fsdp', split_axis=0, concat_axis=0, tiled=True)]
    all_gather x2 -> x0, waiting for transfers between devices: 45.6 us -> none  [the longest x1 31.7 us: fetch_weights(): lax.all_gather(w_proj, 'fsdp', axis=0, tiled=True)]
    unnamed x1 -> x0, blocking collectives: 35 us -> none
    all_to_all x8 -> x0, starting transfers between devices: 32.9 us -> none  [the longest x2 8.43 us: body(): lax.all_to_all(grad_send, 'fsdp', split_axis=0, concat_axis=0, tiled=True)]
  transfers between devices with their start and end apart: 13 -> 0, of which waited for: 13 -> 0; matrix products, arithmetic and copies ran while one was open for 19% -> 0% of each run, Pallas kernels for 0% -> 0%
where the time goes in v2:
time: 218 us; the launch traced here: 217 us
  Pallas kernels  192 us (88%)
  local copies, waits for them, and re-layouts  22.5 us (10%)
    pallas_call x1, Pallas kernels, body_fast(): pl.pallas_call(layer, out_shape=(sds((TOK, D), BF16), sds((TOK, D), F32),...  192 us
    unnamed x13, local copies, waits for them, and re-layouts  18.5 us

profile of v2, /device:TPU:0, one launch (start us, length us, event | category | flops | bytes accessed | tf_op | source)
XLA Modules:
  0.0 217.0 jit_solution(4586104040955454878)
XLA Ops:
  0.6 0.7 pad_maximum_fusion
  1.4 0.1 copy.35
  1.5 1.4 fusion.2.sm
  2.9 1.5 copy.36.routes
  4.3 1.5 copy.37.slots
  5.8 191.8 %layer.1 = (bf16[256,768]{1,0:T(8,128)(2,1)}, f32[256,768]{1,0:T(8,128)}, f32[96,2304]{1,0:T(8,128)}, f32[96,768]{1,0:T(8,128)}, f32[96,128]{1,0:T(8,128)}, /*index=5*/f32[768,1536]{1,0:T(8,128)}, f32[1536,768]{1,0:T(8,128)}) custom-call(bf16[256,768]{1,0:T(8,128)(2,1)} %x_ref.1, bf16[256,768]{1,0:T(8,128)(2,1)} %cot.1, s32[2]{0:T(128)} %lengths.1, ...), custom_call_target="tpu_custom_call" | custom-call | tf_op jit(solution)/shard_map/layer/pallas_call | solution.py:719
  197.6 1.6 slice_reduce_fusion
  199.2 1.4 slice.13
  200.6 0.9 slice.15
  201.5 0.7 copy.38
  202.1 1.8 copy.45
  203.9 2.1 copy.46
  205.9 2.1 copy.47
  208.1 0.0 slice-start
  208.1 1.8 copy.48
  209.9 0.0 slice-start.1
  209.9 4.9 %copy.49 = f32[1,768,1536]{2,1,0:T(8,128)} copy(f32[1,768,1536]{2,1,0:T(8,128)} %bitcast.7) | data formatting | bytes 9437184
  214.8 0.0 slice-done
  214.8 0.0 slice-done.1
  214.8 2.2 %copy.50 = f32[1,1536,768]{2,1,0:T(8,128)} copy(f32[1,1536,768]{2,1,0:T(8,128)S(1)} %bitcast.6) | data formatting | bytes 9437184
  (1 shorter events, 0.0 us)
Async XLA Ops:
  208.1 6.8 %slice-start = ((s8[4718592]{0:T(1024)(128)(4,1)}), s8[4194304]{0:T(1024)(128)(4,1)S(1)}, s32[]{:S(2)}) async-start(s8[4718592]{0:T(1024)(128)(4,1)} %bitcast.4), calls=%async_computation | async-start | bytes 8388608
  209.9 4.9 %slice-start.1 = ((s8[4718592]{0:T(1024)(128)(4,1)}), s8[524288]{0:T(1024)(128)(4,1)S(1)}, s32[]{:S(2)}) async-start(s8[4718592]{0:T(1024)(128)(4,1)} %bitcast.4), calls=%async_computation.1 | async-start | bytes 1048576

commit v3 on v2

--- a/solution.py
+++ b/solution.py
@@ -22,9 +22,14 @@
 EXP = 4
 CAP = 64
 ROWS = MB * CAP
-LOWC = 1152
-EXTRA = D + 128
-WALL = 2 * LOWC + EXTRA
+LOW = 896
+MID = 3 * D - 2 * LOW
+MORE = MID + 128
+SMALL = LOW + MID
+PROJ = LOW + MORE
+HIGH = PROJ + D
+WALL = HIGH + LOW
+LEFTC = LOW + MID
 SHARD = 96
 HALF = SHARD // 2
 PAIRS = HEADS // 2
@@ -66,105 +71,137 @@
     return lax.dot_general(a, b, (((ca,), (cb,)), ((), ())), preferred_element_type=F32)
 
 
-GATHER_SEMS = 40
-
-
-def fill_own(wq, wp, sm, wall, local_sem):
+def run(cond, what):
+    if cond is None:
+        what()
+    else:
+        pl.when(cond)(what)
+
+
+class Links:
+    def __init__(self, send_sem, recv_sem):
+        self.send_sem, self.recv_sem = send_sem, recv_sem
+        self.started = []
+
+    def go(self, cond, src, dst, send, recv, target):
+        copy = remote(src, dst, self.send_sem.at[send], self.recv_sem.at[recv], target)
+        run(cond, copy.start)
+        self.started.append((cond, copy))
+        return copy
+
+    def arrive(self, cond, dst, recv, target):
+        run(cond, remote(dst, dst, self.send_sem.at[0], self.recv_sem.at[recv], target).wait_recv)
+
+    def leave(self, copy):
+        copy.wait_send()
+        self.started = [(cond, item) for cond, item in self.started if item is not copy]
+
+    def finish(self):
+        for cond, copy in self.started:
+            run(cond, copy.wait_send)
+        self.started = []
+
+
+def gather_weights(links, wq, wp, sm, wall, local_sem):
     x, c, z, y = place()
     own = pl.ds(pl.multiple_of((z * 2 + y) * SHARD, 16), SHARD)
     fills = [
-        pltpu.make_async_copy(wq.at[:, pl.ds(0, LOWC)], wall.at[own, pl.ds(0, LOWC)], local_sem.at[0]),
-        pltpu.make_async_copy(
-            wq.at[:, pl.ds(LOWC, LOWC)], wall.at[own, pl.ds(LOWC + EXTRA, LOWC)], local_sem.at[1]
-        ),
-        pltpu.make_async_copy(wp, wall.at[own, pl.ds(LOWC, D)], local_sem.at[2]),
-        pltpu.make_async_copy(sm, wall.at[own, pl.ds(LOWC + D, 128)], local_sem.at[3]),
+        pltpu.make_async_copy(wq.at[:, pl.ds(0, LEFTC)], wall.at[own, pl.ds(0, LEFTC)], local_sem.at[0]),
+        pltpu.make_async_copy(wq.at[:, pl.ds(LEFTC, LOW)], wall.at[own, pl.ds(HIGH, LOW)], local_sem.at[1]),
+        pltpu.make_async_copy(wp, wall.at[own, pl.ds(PROJ, D)], local_sem.at[2]),
+        pltpu.make_async_copy(sm, wall.at[own, pl.ds(SMALL, 128)], local_sem.at[3]),
     ]
     for fill in fills:
         fill.start()
+    share = pl.ds(pl.multiple_of(x * HIGH, 128), LOW)
+    gained = pl.ds(pl.multiple_of((1 - x) * HIGH, 128), LOW)
+    columns = (share, pl.ds(LOW, MORE), pl.ds(PROJ, D))
+    up, down = device(x, c, z + 1, y), device(x, c, z - 1, y)
+    across, facing, twin = device(x, c, z, 1 - y), device(1 - x, c, z, y), device(x, 1 - c, z, y)
+
+    def part(zs, ys, half, cols):
+        return wall.at[pl.ds(pl.multiple_of((zs * 2 + ys) * SHARD + half * HALF, 16), HALF), cols]
+
+    def go(cond, zs, ys, cols, send, recv, target, src=None):
+        piece = part(zs, ys, c, cols)
+        links.go(cond, piece if src is None else src, piece, send, recv, target)
+
+    def arrive(cond, zs, ys, half, cols, recv):
+        links.arrive(cond, part(zs, ys, half, cols), recv, twin)
+
+    def spread(cond, sub, zs, ys):
+        source = zs * 2 + ys
+        if sub == 0:
+            go(cond, zs, ys, share, 39 + source, 24 + source, facing)
+        go(cond, zs, ys, columns[sub], 47 + sub * 8 + source, 32 + sub * 8 + source, twin)
+
+    def begin(sub, src):
+        go(z < 3, z, y, columns[sub], sub * 3, sub * 4 + z, up, src)
+        go(z > 0, z, y, columns[sub], 9 + sub * 3, sub * 4 + z, down, src)
+        go(None, z, y, columns[sub], 18 + sub * 7, 12 + sub * 4 + z, across, src)
+
+    def along(sub, k):
+        below, above = z - k, z + k
+        for cond, zs, on, first, target, place_of in (
+            (below >= 0, below, z < 3, 0, up, k),
+            (above <= 3, above, z > 0, 9, down, 3 + k),
+        ):
+            arrive(cond, zs, y, c, columns[sub], sub * 4 + zs)
+            if k < 3:
+                go(cond & on, zs, y, columns[sub], first + sub * 3 + k, sub * 4 + zs, target)
+            go(cond, zs, y, columns[sub], 18 + sub * 7 + place_of, 12 + sub * 4 + zs, across)
+            spread(cond, sub, zs, y)
+
+    def over(sub, k):
+        if k == 0:
+            arrive(None, z, 1 - y, c, columns[sub], 12 + sub * 4 + z)
+            spread(None, sub, z, 1 - y)
+            return
+        for cond, zs in ((z - k >= 0, z - k), (z + k <= 3, z + k)):
+            arrive(cond, zs, 1 - y, c, columns[sub], 12 + sub * 4 + zs)
+            spread(cond, sub, zs, 1 - y)
+
+    half = pl.ds(pl.multiple_of(c * HALF, 16), HALF)
+    begin(0, wq.at[half, pl.ds(pl.multiple_of(x * LEFTC, 128), LOW)])
     for fill in fills:
         fill.wait()
-
-
-def gather_weights(wall, send_sem, recv_sem):
-    x, c, z, y = place()
-    plane = pl.ds(pl.multiple_of(x * LOWC, 128), LOWC + EXTRA)
-    share = pl.ds(pl.multiple_of(x * (LOWC + EXTRA), 128), LOWC)
-    gained = pl.ds(pl.multiple_of((1 - x) * (LOWC + EXTRA), 128), LOWC)
-    up, down = device(x, c, z + 1, y), device(x, c, z - 1, y)
-    across, facing, twin = device(x, c, z, 1 - y), device(1 - x, c, z, y), device(x, 1 - c, z, y)
-    started = []
-
-    def part(zs, ys, half, cols):
-        return wall.at[pl.ds(pl.multiple_of((zs * 2 + ys) * SHARD + half * HALF, 16), HALF), cols]
-
-    def run(cond, what):
-        if cond is None:
-            what()
-        else:
-            pl.when(cond)(what)
-
-    def go(cond, zs, ys, cols, send, recv, target):
-        piece = part(zs, ys, c, cols)
-        copy = remote(piece, piece, send_sem.at[send], recv_sem.at[recv], target)
-        run(cond, copy.start)
-        started.append((cond, copy))
-
-    def arrive(cond, zs, ys, half, cols, recv):
-        piece = part(zs, ys, half, cols)
-        copy = remote(piece, piece, send_sem.at[0], recv_sem.at[recv], twin)
-        run(cond, copy.wait_recv)
-
-    def spread(cond, zs, ys, k):
-        source = zs * 2 + ys
-        go(cond, zs, ys, share, 13 + source, 8 + source, facing)
-        go(cond, zs, ys, plane, 21 + source, 16 + source, twin)
-
-    go(z < 3, z, y, plane, 0, z, up)
-    go(z > 0, z, y, plane, 3, z, down)
-    go(None, z, y, plane, 6, 4 + z, across)
+    begin(1, None)
+    begin(2, wp.at[half, :])
     for k in (1, 2, 3):
-        below, above = z - k, z + k
-        for cond, zs, on, send, target in (
-            (below >= 0, below, z < 3, k, up),
-            (above <= 3, above, z > 0, 3 + k, down),
-        ):
-            arrive(cond, zs, y, c, plane, zs)
-            if k < 3:
-                go(cond & on, zs, y, plane, send, zs, target)
-            go(cond, zs, y, plane, 6 + (k if target is up else 3 + k), 4 + zs, across)
-            spread(cond, zs, y, k)
+        for sub in range(3):
+            along(sub, k)
+            if k > 1 or sub < 2:
+                over(sub, k - 1)
         if k == 1:
-            arrive(None, z, 1 - y, c, plane, 4 + z)
-            spread(None, z, 1 - y, 0)
-        else:
-            for cond, zs in ((z - k + 1 >= 0, z - k + 1), (z + k - 1 <= 3, z + k - 1)):
-                arrive(cond, zs, 1 - y, c, plane, 4 + zs)
-                spread(cond, zs, 1 - y, 0)
-    for cond, zs in ((z == 3, z - 3), (z == 0, z + 3)):
-        arrive(cond, zs, 1 - y, c, plane, 4 + zs)
-        spread(cond, zs, 1 - y, 0)
-    for zs in range(4):
-        for ys in range(2):
-            source = zs * 2 + ys
-            other = (zs != z) | (ys != y)
-            arrive(other, zs, ys, c, gained, 8 + source)
-            go(other, zs, ys, gained, 29 + source, 24 + source, twin)
-    for zs in range(4):
-        for ys in range(2):
-            source = zs * 2 + ys
-            other = (zs != z) | (ys != y)
-            arrive(other, zs, ys, 1 - c, plane, 16 + source)
-            arrive(other, zs, ys, 1 - c, gained, 24 + source)
-    return started
-
-
-def finish(started):
-    for cond, copy in started:
-        if cond is None:
-            copy.wait_send()
-        else:
-            pl.when(cond)(copy.wait_send)
+            over(2, 0)
+    for sub in range(2):
+        over(sub, 3)
+
+    def each(what):
+        for zs in range(4):
+            for ys in range(2):
+                what((zs != z) | (ys != y), zs, ys, zs * 2 + ys)
+
+    def gain(other, zs, ys, source):
+        arrive(other, zs, ys, c, gained, 24 + source)
+        go(other, zs, ys, gained, 71 + source, 56 + source, twin)
+
+    def mostly(other, zs, ys, source):
+        for sub in range(2):
+            arrive(other, zs, ys, 1 - c, columns[sub], 32 + sub * 8 + source)
+        arrive(other, zs, ys, 1 - c, gained, 56 + source)
+
+    def rest(other, zs, ys, source):
+        arrive(other, zs, ys, 1 - c, columns[2], 32 + 16 + source)
+
+    each(gain)
+    each(mostly)
+
+    def later():
+        over(2, 3)
+        each(rest)
+
+    return later
 
 
 def unit(values):
@@ -173,7 +210,7 @@
 
 def build_bias(wall, bias):
     table = jnp.concatenate(
-        [wall[f * SHARD : f * SHARD + 16, LOWC + D : LOWC + EXTRA] for f in range(8)], axis=0
+        [wall[f * SHARD : f * SHARD + 16, SMALL : SMALL + 128] for f in range(8)], axis=0
     )
     ahead = lax.broadcasted_iota(jnp.int32, (SEQ, SEQ), 0)
     lane = lax.broadcasted_iota(jnp.int32, (SEQ, SEQ), 1)
@@ -185,11 +222,24 @@
         bias[(h // 2) * SEQ : (h // 2 + 1) * SEQ, (h % 2) * SEQ : (h % 2 + 1) * SEQ] = jnp.where(ahead >= lane, rolled, NEG)
 
 
-def routing(routes, slots, s):
-    rows = slice(s * SEQ, (s + 1) * SEQ)
-    lane = lax.broadcasted_iota(jnp.int32, (SEQ, EXP * CAP), 1)
-    spots = routes[rows, :] * CAP + slots[rows, :]
+def stand(routes, slots, lines, columns):
+    chosen = routes[...]
+    lines[...] = jnp.zeros_like(lines)
+    lines[0:2, :] = (chosen * CAP + slots[...]).astype(F32)
+    lines[2:4, :] = chosen.astype(F32)
+    columns[...] = jnp.transpose(lines[...])
+
+
+def routing(columns, s):
+    spots = columns[s * SEQ : (s + 1) * SEQ, :]
+    lane = lax.broadcasted_iota(jnp.int32, (SEQ, EXP * CAP), 1).astype(F32)
     return spots[:, 0:1] == lane, spots[:, 1:2] == lane
+
+
+def named(columns, s):
+    spots = columns[s * SEQ : (s + 1) * SEQ, :]
+    lane = lax.broadcasted_iota(jnp.int32, (SEQ, 128), 1).astype(F32) - 2.0
+    return spots[:, 2:3] == lane, spots[:, 3:4] == lane
 
 
 def live_column(lengths, s):
@@ -197,15 +247,14 @@
 
 
 def attention_forward(
-    x_ref, cot, lengths, routes, slots, wall, rows_t, board, normed, qkv, attended, hidden, normed2, gates,
-    out_f, out_g,
+    later, x_ref, cot, lengths, columns, wall, rows_t, board, normed, qkv, attended, hidden, normed2, gates, out_f, out_g
 ):
-    rows_t[...] = jnp.transpose(wall[:, LOWC + D : LOWC + EXTRA].astype(F32))[0:8]
+    rows_t[...] = jnp.transpose(wall[:, SMALL : SMALL + 128].astype(F32))[0:8]
     build_bias(wall, board)
     x = x_ref[...].astype(F32)
     normed[...] = (x * unit(x) * rows_t[0:1, :]).astype(BF16)
-    qkv[:, 0:LOWC] = dot(normed[...], wall[:, 0:LOWC]).astype(BF16)
-    qkv[:, LOWC : 2 * LOWC] = dot(normed[...], wall[:, LOWC + EXTRA : WALL]).astype(BF16)
+    qkv[:, 0:LEFTC] = dot(normed[...], wall[:, 0:LEFTC]).astype(BF16)
+    qkv[:, LEFTC : 3 * D] = dot(normed[...], wall[:, HIGH:WALL]).astype(BF16)
     lane = lax.broadcasted_iota(jnp.int32, (SEQ, 128), 1)
 
     def pair(p, carry):
@@ -222,7 +271,7 @@
                 raw = dot(jnp.where(mine, q, jnp.zeros_like(q)), k, 1, 1)
                 scores = jnp.where(alive, raw * SCALE + board[blocks, j * SEQ : (j + 1) * SEQ], NEG)
                 scores = jnp.exp(scores - jnp.max(scores, axis=-1, keepdims=True))
-                share = scores / jnp.sum(scores, axis=-1, keepdims=True)
+                share = scores * (1.0 / jnp.sum(scores, axis=-1, keepdims=True))
                 board[blocks, (2 + 2 * s + j) * SEQ : (3 + 2 * s + j) * SEQ] = share
                 got.append(dot(share.astype(BF16), v))
             attended[rows, pl.ds(pl.multiple_of(p * 128, 128), 128)] = jnp.where(
@@ -231,7 +280,8 @@
         return carry
 
     lax.fori_loop(0, PAIRS, pair, 0)
-    branch = dot(attended[...], wall[:, LOWC : LOWC + D])
+    later()
+    branch = dot(attended[...], wall[:, PROJ:HIGH])
     for s in range(MB):
         rows = slice(s * SEQ, (s + 1) * SEQ)
         live = live_column(lengths, s)
@@ -239,15 +289,13 @@
         hidden[rows, :] = state
         low = (state * unit(state) * rows_t[1:2, :]).astype(BF16)
         normed2[rows, :] = low
-        logits = dot(low, wall[:, LOWC + D : LOWC + EXTRA])
-        kind = lane - 2
-        picked = jnp.where(kind == routes[rows, 0:1], logits, 0.0) - jnp.where(
-            kind == routes[rows, 1:2], logits, 0.0
-        )
+        logits = dot(low, wall[:, SMALL : SMALL + 128])
+        one, two = named(columns, s)
+        picked = jnp.where(one, logits, 0.0) - jnp.where(two, logits, 0.0)
         gate = jax.nn.sigmoid(jnp.sum(picked, axis=-1, keepdims=True))
         gates[rows, :] = gate
         grad = jnp.where(live, cot[rows, :].astype(F32), 0.0)
-        first, second = routing(routes, slots, s)
+        first, second = routing(columns, s)
         first = jnp.where(first & live, 1.0, 0.0).astype(BF16)
         second = jnp.where(second & live, 1.0, 0.0).astype(BF16)
         sent = dot(first + second, low, 0, 0).astype(BF16)
@@ -260,42 +308,11 @@
             out_g[e, s * CAP : (s + 1) * CAP, :] = back[e * CAP : (e + 1) * CAP, :]
 
 
-class Links:
-    def __init__(self, send_sem, recv_sem):
-        self.send_sem, self.recv_sem = send_sem, recv_sem
-        self.started = []
-
-    def go(self, cond, src, dst, send, recv, target):
-        copy = remote(src, dst, self.send_sem.at[send], self.recv_sem.at[recv], target)
-        run(cond, copy.start)
-        self.started.append((cond, copy))
-        return copy
-
-    def arrive(self, cond, dst, recv, target):
-        run(cond, remote(dst, dst, self.send_sem.at[0], self.recv_sem.at[recv], target).wait_recv)
-
-    def leave(self, copy):
-        copy.wait_send()
-        self.started = [(cond, item) for cond, item in self.started if item is not copy]
-
-    def finish(self):
-        for cond, copy in self.started:
-            run(cond, copy.wait_send)
-        self.started = []
-
-
-def run(cond, what):
-    if cond is None:
-        what()
-    else:
-        pl.when(cond)(what)
-
-
 TILE = 512
-Z_ROWS, Y_ROWS, Y_PART, Z_BACK = 40, 48, 56, 64
-TWIN_W, FACE_W, TWIN_OUT = 72, 74, 76
-RS_TWIN, RS_Y, RS_Z, RS_FACE, RS_OUT = 78, 80, 84, 92, 93
-LINKS = 96
+Z_ROWS, Y_ROWS, Y_PART, Z_BACK = 80, 88, 96, 104
+TWIN_W, FACE_W, TWIN_OUT = 112, 114, 120
+RS_TWIN, RS_Y, RS_Z, RS_FACE, RS_OUT = 126, 130, 146, 178, 182
+LINKS = 186
 
 
 def quarter(zs):
@@ -369,6 +386,9 @@
             expert_forward(zs, recv[0], up, down, act, slope, part[0])
         else:
             expert_backward(zs, recv[1], up, down, slope, part[1])
+
+    def give_part(kind, d):
+        zs = source(d)
         links.go(
             None, part[kind].at[zs, 1 - y], take[kind].at[zs], Y_PART + kind * 4 + d, Y_PART + kind * 4 + zs, across
         )
@@ -386,27 +406,31 @@
                 device(x, c, zs, y),
             )
 
+    reach(0, 1)
     compute(0, 0)
-    reach(0, 1)
+    reach(0, 2)
     compute(1, 0)
-    reach(0, 2)
+    reach(0, 3)
     compute(0, 1)
-    merge(0, 0)
-    reach(0, 3)
+    reach(1, 1)
+    give_part(0, 1)
     compute(0, 2)
-    merge(1, 0)
+    reach(1, 2)
+    give_part(0, 2)
+    compute(1, 1)
+    reach(1, 3)
+    give_part(1, 1)
     merge(0, 1)
-    reach(1, 1)
     compute(0, 3)
+    give_part(0, 3)
     merge(0, 2)
-    reach(1, 2)
-    compute(1, 1)
-    merge(0, 3)
-    reach(1, 3)
     compute(1, 2)
+    give_part(1, 2)
     merge(1, 1)
     compute(1, 3)
-    merge(1, 2)
+    give_part(1, 3)
+    give_part(0, 0)
+    give_part(1, 0)
 
     def down_tile(i, part_of, keep):
         cols = pl.ds(pl.multiple_of(part_of * (HF // 2) + i * 256, 128), 256)
@@ -425,57 +449,63 @@
 
         lax.fori_loop(0, 3, step, 0)
 
-    sent = []
+    pairs = ((0, 3), (1, 2), (1, 3))
     for i, (one, w) in enumerate(((down_tile, w_down), (up_tile, w_up))):
         own, give, got, face = w
         tiles(one, 1 - c, give)
-        sent.append(links.go(None, give, got, TWIN_W + i, TWIN_W + i, twin))
-        if i == 0:
-            merge(1, 3)
+        sent = links.go(None, give, got, TWIN_W + i, TWIN_W + i, twin)
         tiles(one, c, own)
         links.arrive(None, got, TWIN_W + i, twin)
-        links.leave(sent[i])
-        give[...] = (own[...] + got[...].astype(F32)).astype(BF16)
-        links.go(None, give, face, FACE_W + i, FACE_W + i, facing)
+        links.leave(sent)
+        count = own.shape[0] // 3
+        for m in range(3):
+            rows = slice(m * count, (m + 1) * count)
+            give[rows, :] = (own[rows, :] + got[rows, :].astype(F32)).astype(BF16)
+            links.go(None, give.at[rows, :], face.at[rows, :], FACE_W + i * 3 + m, FACE_W + i * 3 + m, facing)
+        merge(*pairs[i])
+    merge(*pairs[2])
+    merge(0, 0)
+    merge(1, 0)
     for kind in range(2):
         for d in (1, 2, 3):
             zs = source(d)
             links.arrive(None, back[kind].at[zs], Z_BACK + kind * 4 + zs, across)
 
 
-def expert_grads_out(links, w_down, w_up, out_down, out_up, local_sem):
+def expert_grad_out(links, piece, w_down, w_up, out_down, out_up, local_sem):
     x, c, z, y = place()
     facing, twin = device(1 - x, c, z, y), device(x, 1 - c, z, y)
-    pending = []
-    for i, (w, target) in enumerate(((w_down, out_down), (w_up, out_up))):
-        own, give, got, face = w
-        count = own.shape[0]
-        links.arrive(None, face, FACE_W + i, facing)
-        own[...] = give[...].astype(F32) + face[...].astype(F32)
-        rows = pl.ds(pl.multiple_of(c * count, 128), count)
-        links.go(None, own, target.at[rows, :], TWIN_OUT + i, TWIN_OUT + i, twin)
-        copy = pltpu.make_async_copy(own, target.at[rows, :], local_sem.at[i])
-        copy.start()
-        pending.append(copy)
-    for i, (w, target) in enumerate(((w_down, out_down), (w_up, out_up))):
-        count = w[0].shape[0]
-        rows = pl.ds(pl.multiple_of((1 - c) * count, 128), count)
-        links.arrive(None, target.at[rows, :], TWIN_OUT + i, twin)
-    return pending
-
-
-OWNC = 2 * D
-SENTC = OWNC + 128
-
-
-def combine(cot, lengths, routes, slots, rows_t, hidden, normed2, gates, back_f, back_g, mixed, rb, small_t):
-    lane = lax.broadcasted_iota(jnp.int32, (SEQ, 128), 1)
+    (own, give, got, face), target = ((w_down, out_down), (w_up, out_up))[piece // 3]
+    count = own.shape[0] // 3
+    rows = slice((piece % 3) * count, (piece % 3 + 1) * count)
+    links.arrive(None, face.at[rows, :], FACE_W + piece, facing)
+    face[rows, :] = (give[rows, :].astype(F32) + face[rows, :].astype(F32)).astype(BF16)
+    there = target.at[pl.ds(pl.multiple_of((c * 3 + piece % 3) * count, 128), count), :]
+    links.go(None, face.at[rows, :], there, TWIN_OUT + piece, TWIN_OUT + piece, twin)
+    copy = pltpu.make_async_copy(face.at[rows, :], there, local_sem.at[8 + piece])
+    copy.start()
+    return copy
+
+
+def expert_grads_arrive(links, out_down, out_up):
+    x, c, z, y = place()
+    for piece in range(6):
+        target = (out_down, out_up)[piece // 3]
+        count = target.shape[0] // 6
+        there = target.at[pl.ds(pl.multiple_of(((1 - c) * 3 + piece % 3) * count, 128), count), :]
+        links.arrive(None, there, TWIN_OUT + piece, device(x, 1 - c, z, y))
+
+
+SENTC = 2 * D + 128
+
+
+def combine(cot, lengths, columns, rows_t, hidden, normed2, gates, back_f, back_g, mixed, rb, small_t):
     gain_grad = jnp.zeros((1, D), F32)
     router_grad = jnp.zeros((128, D), F32)
     for s in range(MB):
         rows = slice(s * SEQ, (s + 1) * SEQ)
         live = live_column(lengths, s)
-        first, second = routing(routes, slots, s)
+        first, second = routing(columns, s)
         first = jnp.where(first, 1.0, 0.0).astype(BF16)
         second = jnp.where(second, 1.0, 0.0).astype(BF16)
         given = jnp.concatenate([back_f[e, s * CAP : (s + 1) * CAP, :] for e in range(EXP)], axis=0)
@@ -491,8 +521,8 @@
             grad_live * second_out, axis=-1, keepdims=True
         )
         tilt = tilt * gate * (1.0 - gate)
-        kind = lane - 2
-        hot = jnp.where(kind == routes[rows, 0:1], 1.0, 0.0) - jnp.where(kind == routes[rows, 1:2], 1.0, 0.0)
+        one, two = named(columns, s)
+        hot = jnp.where(one, 1.0, 0.0) - jnp.where(two, 1.0, 0.0)
         grad_logits = tilt * hot
         high = grad_logits.astype(BF16)
         low = (grad_logits - high.astype(F32)).astype(BF16)
@@ -513,8 +543,9 @@
     small_t[1:2, :] = gain_grad
 
 
-def attention_backward(x_ref, wall, rows_t, left, qkv, board, hidden, grad_att, rb, rel_rows, small_t, grad_tokens):
-    grad_att[...] = dot(rb[:, 3 * D : 4 * D], wall[:, LOWC : LOWC + D], 1, 1).astype(BF16)
+def attention_backward(x_ref, wall, rows_t, qkv, board, hidden, grad_att, rb, rel_rows, small_t, grad_tokens, midway):
+    grad_att[...] = dot(rb[:, 3 * D : 4 * D], wall[:, PROJ:HIGH], 1, 1).astype(BF16)
+    midway()
     lane = lax.broadcasted_iota(jnp.int32, (SEQ, 128), 1)
     ahead = lax.broadcasted_iota(jnp.int32, (SEQ, 128), 0)
     flip = jnp.where(ahead + lane == SEQ - 1, 1.0, 0.0).astype(BF16)
@@ -548,8 +579,8 @@
         return carry
 
     lax.fori_loop(0, PAIRS, pair, 0)
-    grad_low = dot(rb[:, 0:LOWC], wall[:, 0:LOWC], 1, 1) + dot(
-        rb[:, LOWC : 2 * LOWC], wall[:, LOWC + EXTRA : WALL], 1, 1
+    grad_low = dot(rb[:, 0:LEFTC], wall[:, 0:LEFTC], 1, 1) + dot(
+        rb[:, LEFTC : 3 * D], wall[:, HIGH:WALL], 1, 1
     )
     state = x_ref[...].astype(F32)
     factor = unit(state)
@@ -572,97 +603,136 @@
     small_t[HEAD : HEAD + 16, :] = spread
 
 
-def reduce_grads(links, left, rb, small_t, give, take, total, y_take, z_take, face_give, face_take, last, out_qkv, out_proj, out_small, local_sem):
-    x, c, z, y = place()
-    across, facing, twin = device(x, c, z, 1 - y), device(1 - x, c, z, y), device(x, 1 - c, z, y)
-    up, down = device(x, c, z + 1, y), device(x, c, z - 1, y)
-
-    def tile(core, i, keep):
+HC = D // 2
+GROUPS = (
+    (1, 2 * HC, HC, lambda core: 3 * D + core * HC, lambda core: core * HC),
+    (0, HC, HC, lambda core: 2 * D + core * HC, lambda core: 2 * D + core * HC),
+    (0, 0, HC, lambda core: core * D, lambda core: core * D),
+    (0, 3 * HC, HC + 128, lambda core: core * D + HC, lambda core: core * D + HC),
+)
+
+
+class Reduction:
+    def __init__(self, links, group, left, rb, small_t, give, take, total, y_take, z_take, face_give, face_take, last):
+        self.links, self.group = links, group
+        which, first, self.width, self.rhs, self.target = GROUPS[group]
+        self.cols = slice(first, first + self.width)
+        self.core_cols = slice(first, first + HC)
+        self.small_cols = slice(first + HC, first + self.width)
+        self.lhs, self.rb, self.small_t = left.at[which], rb, small_t
+        self.give, self.take, self.total = give, take, total
+        self.y_take, self.z_take, self.face_give, self.face_take, self.last = y_take, z_take, face_give, face_take, last
+        x, c, z, y = self.place = place()
+        self.across, self.facing, self.twin = device(x, c, z, 1 - y), device(1 - x, c, z, y), device(x, 1 - c, z, y)
+        mirror = z // 2
+        near = z + mirror * (3 - 2 * z)
+        self.order = [o + mirror * (3 - 2 * o) for o in (3, 2, 1 - near, near)]
+
+    def tile(self, core, keep):
         def step(m, carry):
             rows = pl.ds(pl.multiple_of(m * 256, 256), 256)
-            rhs = rb[:, pl.ds(pl.multiple_of((2 * core + i) * D, 128), D)]
-            keep[rows, i * D : (i + 1) * D] = dot(left[core * i, :, rows], rhs, 0, 0).astype(keep.dtype)
+            rhs = self.rb[:, pl.ds(pl.multiple_of(self.rhs(core), 128), HC)]
+            keep[rows, self.core_cols] = dot(self.lhs[:, rows], rhs, 0, 0).astype(keep.dtype)
             return carry
 
         lax.fori_loop(0, 3, step, 0)
 
-    for i in range(2):
-        tile(1 - c, i, give)
-    small = jnp.transpose(small_t[...])
-    give[:, OWNC:SENTC] = small.astype(BF16)
-    first = links.go(None, give, take, RS_TWIN, RS_TWIN, twin)
-    for i in range(2):
-        tile(c, i, total)
-    total[:, OWNC:SENTC] = small.astype(BF16).astype(F32)
-    links.arrive(None, take, RS_TWIN, twin)
-    links.leave(first)
-    mirror = z // 2
-    near = z + mirror * (3 - 2 * z)
-    order = [o + mirror * (3 - 2 * o) for o in (3, 2, 1 - near, near)]
-
-    def shard(zs, ys):
+    def form(self):
+        x, c, z, y = self.place
+        self.tile(1 - c, self.give)
+        if self.group == 3:
+            small = jnp.transpose(self.small_t[...]).astype(BF16)
+            self.give[:, self.small_cols] = small
+            self.total[:, self.small_cols] = small.astype(F32)
+        slot = RS_TWIN + self.group
+        self.sent = self.links.go(None, self.give.at[:, self.cols], self.take.at[:, self.cols], slot, slot, self.twin)
+        self.tile(c, self.total)
+
+    def shard(self, zs, ys):
         return pl.ds(pl.multiple_of((zs * 2 + ys) * SHARD, 16), SHARD)
 
-    for zs in order:
-        rows = shard(zs, 1 - y)
-        give[rows, :] = (total[rows, :] + take[rows, :].astype(F32)).astype(BF16)
-        links.go(None, give.at[rows, :], y_take.at[zs], RS_Y + zs, RS_Y + zs, across)
-    for zs in order:
-        rows = shard(zs, y)
-        total[rows, :] = total[rows, :] + take[rows, :].astype(F32)
-    for k, zs in enumerate(order):
-        rows = shard(zs, y)
-        links.arrive(None, y_take.at[zs], RS_Y + zs, across)
-        total[rows, :] = total[rows, :] + y_take[zs].astype(F32)
-        if k < 3:
-            climbs, sinks = zs > z, zs < z
-            for cond, more, slot, target in ((climbs, z > 0, zs, up), (sinks, z < 3, 4 + zs, down)):
-
-                @pl.when(cond & more)
-                def _():
-                    links.arrive(None, z_take.at[slot], RS_Z + slot, across)
-                    total[rows, :] = total[rows, :] + z_take[slot].astype(F32)
-
-                @pl.when(cond)
-                def _():
-                    give[rows, :] = total[rows, :].astype(BF16)
-
-                links.go(cond, give.at[rows, :], z_take.at[slot], RS_Z + slot, RS_Z + slot, target)
-    rows = shard(z, y)
-    for cond, slot in ((z > 0, z), (z < 3, 4 + z)):
+    def halve(self):
+        x, c, z, y = self.place
+        links, cols = self.links, self.cols
+        links.arrive(None, self.take.at[:, cols], RS_TWIN + self.group, self.twin)
+        links.leave(self.sent)
+        for zs in self.order:
+            rows = self.shard(zs, 1 - y)
+            self.give[rows, cols] = (self.total[rows, cols] + self.take[rows, cols].astype(F32)).astype(BF16)
+            slot = RS_Y + self.group * 4 + zs
+            links.go(None, self.give.at[rows, cols], self.y_take.at[zs, :, cols], slot, slot, self.across)
+        for zs in self.order:
+            rows = self.shard(zs, y)
+            self.total[rows, cols] = self.total[rows, cols] + self.take[rows, cols].astype(F32)
+
+    def chain(self, k):
+        x, c, z, y = self.place
+        links, cols, zs = self.links, self.cols, self.order[k]
+        total, z_take = self.total, self.z_take
+        rows = self.shard(zs, y)
+        links.arrive(None, self.y_take.at[zs, :, cols], RS_Y + self.group * 4 + zs, self.across)
+        total[rows, cols] = total[rows, cols] + self.y_take[zs, :, cols].astype(F32)
+        if k == 3:
+            return
+        for cond, more, slot, target in (
+            (zs > z, z > 0, zs, device(x, c, z + 1, y)),
+            (zs < z, z < 3, 4 + zs, device(x, c, z - 1, y)),
+        ):
+            self.add_from_z(cond & more, slot, rows)
+
+            @pl.when(cond)
+            def _():
+                self.give[rows, cols] = total[rows, cols].astype(BF16)
+
+            index = RS_Z + self.group * 8 + slot
+            links.go(cond, self.give.at[rows, cols], z_take.at[slot, :, cols], index, index, target)
+
+    def add_from_z(self, cond, slot, rows):
+        cols = self.cols
 
         @pl.when(cond)
         def _():
-            links.arrive(None, z_take.at[slot], RS_Z + slot, across)
-            total[rows, :] = total[rows, :] + z_take[slot].astype(F32)
-
-    face_give[...] = total[rows, :].astype(BF16)
-    links.go(None, face_give, face_take, RS_FACE, RS_FACE, facing)
-    links.arrive(None, face_take, RS_FACE, facing)
-    last[...] = face_give[...].astype(F32) + face_take[...].astype(F32)
-    pieces = (
-        (c == 0, slice(0, OWNC), out_qkv.at[:, 0:OWNC], 0),
-        (c == 1, slice(0, D), out_qkv.at[:, OWNC : 3 * D], 1),
-        (c == 1, slice(D, OWNC), out_proj, 2),
-    )
-    pending = []
-    for cond, cols, target, i in pieces:
-        links.go(cond, last.at[:, cols], target, RS_OUT + i, RS_OUT + i, twin)
-        copy = pltpu.make_async_copy(last.at[:, cols], target, local_sem.at[2 + i])
-        run(cond, copy.start)
-        pending.append((cond, copy))
-    copy = pltpu.make_async_copy(last.at[:, OWNC:SENTC], out_small, local_sem.at[5])
-    copy.start()
-    pending.append((None, copy))
-    for cond, cols, target, i in pieces:
-        links.arrive((c == 1) if i == 0 else (c == 0), target, RS_OUT + i, twin)
-    return pending
+            part = self.z_take.at[slot, :, cols]
+            self.links.arrive(None, part, RS_Z + self.group * 8 + slot, self.across)
+            self.total[rows, cols] = self.total[rows, cols] + part[...].astype(F32)
+
+    def face(self):
+        x, c, z, y = self.place
+        rows, cols = self.shard(z, y), self.cols
+        self.add_from_z(z > 0, z, rows)
+        self.add_from_z(z < 3, 4 + z, rows)
+        self.face_give[:, cols] = self.total[rows, cols].astype(BF16)
+        slot = RS_FACE + self.group
+        self.links.go(None, self.face_give.at[:, cols], self.face_take.at[:, cols], slot, slot, self.facing)
+
+    def publish(self, out_qkv, out_proj, out_small, local_sem):
+        x, c, z, y = self.place
+        cols = self.cols
+        self.links.arrive(None, self.face_take.at[:, cols], RS_FACE + self.group, self.facing)
+        self.last[:, cols] = self.face_give[:, cols].astype(F32) + self.face_take[:, cols].astype(F32)
+        self.out = out_proj if self.group == 0 else out_qkv
+        slot = RS_OUT + self.group
+        part, there = self.last.at[:, self.core_cols], self.landing(c)
+        self.links.go(None, part, there, slot, slot, self.twin)
+        copies = [pltpu.make_async_copy(part, there, local_sem.at[self.group])]
+        if self.group == 3:
+            copies.append(pltpu.make_async_copy(self.last.at[:, self.small_cols], out_small, local_sem.at[6]))
+        for copy in copies:
+            copy.start()
+        return copies
+
+    def landing(self, core):
+        return self.out.at[:, pl.ds(pl.multiple_of(self.target(core), 128), HC)]
+
+    def landed(self):
+        x, c, z, y = self.place
+        self.links.arrive(None, self.landing(1 - c), RS_OUT + self.group, self.twin)
 
 
 def layer(
     x_ref, cot, lengths, routes, slots, wq, wp, sm, w_up, w_down,
     mixed, grad_tokens, out_qkv, out_proj, out_small, out_up, out_down,
-    wall, rows_t, left, qkv, hidden, normed2, gates, out_f, out_g, recv_f, recv_g, up, down, act, slope,
+    wall, rows_t, lines, columns, left, qkv, hidden, normed2, gates, out_f, out_g, recv_f, recv_g, up, down, act, slope,
     part_f, part_g, take_f, take_g, back_f, back_g, dn_own, dn_give, dn_take, dn_face, up_own, up_give, up_take, up_face,
     rb, rel_rows, small_t, take, total, y_take, z_take, face_give, face_take, last,
     local_sem, send_sem, recv_sem,
@@ -671,16 +741,16 @@
         pltpu.make_async_copy(w_up.at[0], up, local_sem.at[4]),
         pltpu.make_async_copy(w_down.at[0], down, local_sem.at[5]),
     ]
+    greet()
+    links = Links(send_sem, recv_sem)
     for copy in fetch:
         copy.start()
-    greet()
-    fill_own(wq, wp, sm, wall, local_sem)
-    links = Links(send_sem, recv_sem)
-    links.started += gather_weights(wall, send_sem, recv_sem)
+    stand(routes, slots, lines, columns)
+    rel_rows[...] = jnp.zeros_like(rel_rows)
+    later = gather_weights(links, wq, wp, sm, wall, local_sem)
     normed, attended = left.at[0], left.at[1]
     attention_forward(
-        x_ref, cot, lengths, routes, slots, wall, rows_t, total, normed, qkv, attended, hidden, normed2, gates,
-        out_f, out_g,
+        later, x_ref, cot, lengths, columns, wall, rows_t, total, normed, qkv, attended, hidden, normed2, gates, out_f, out_g
     )
     for copy in fetch:
         copy.wait()
@@ -689,16 +759,60 @@
         links, (out_f, out_g), (recv_f, recv_g), up, down, act, slope, (part_f, part_g), (take_f, take_g),
         (back_f, back_g), downs, ups,
     )
-    rel_rows[...] = jnp.zeros_like(rel_rows)
-    combine(cot, lengths, routes, slots, rows_t, hidden, normed2, gates, back_f, back_g, mixed, rb, small_t)
-    attention_backward(x_ref, wall, rows_t, left, qkv, total, hidden, normed2, rb, rel_rows, small_t, grad_tokens)
-    pending = reduce_grads(
-        links, left, rb, small_t, act.at[0:D, :], take, total, y_take, z_take, face_give, face_take, last, out_qkv, out_proj,
-        out_small, local_sem,
-    )
-    more = expert_grads_out(links, downs, ups, out_down, out_up, local_sem)
-    for cond, copy in pending + [(None, copy) for copy in more]:
-        run(cond, copy.wait)
+    combine(cot, lengths, columns, rows_t, hidden, normed2, gates, back_f, back_g, mixed, rb, small_t)
+    proj, values, first, second = (
+        Reduction(
+            links, group, left, rb, small_t, act.at[0:D, :], take, total, y_take, z_take, face_give, face_take, last
+        )
+        for group in range(4)
+    )
+    pending = []
+
+    def grads(piece):
+        pending.append(expert_grad_out(links, piece, downs, ups, out_down, out_up, local_sem))
+
+    def publish(item):
+        pending.extend(item.publish(out_qkv, out_proj, out_small, local_sem))
+
+    proj.form()
+    attention_backward(
+        x_ref, wall, rows_t, qkv, total, hidden, normed2, rb, rel_rows, small_t, grad_tokens, proj.halve
+    )
+    values.form()
+    proj.chain(0)
+    values.halve()
+    proj.chain(1)
+    first.form()
+    proj.chain(2)
+    proj.chain(3)
+    first.halve()
+    values.chain(0)
+    second.form()
+    values.chain(1)
+    second.halve()
+    values.chain(2)
+    values.chain(3)
+    grads(0)
+    grads(1)
+    proj.face()
+    for k in range(4):
+        first.chain(k)
+    values.face()
+    grads(2)
+    for k in range(4):
+        second.chain(k)
+    first.face()
+    grads(3)
+    second.face()
+    grads(4)
+    grads(5)
+    for item in (proj, values, first, second):
+        publish(item)
+    for item in (proj, values, first, second):
+        item.landed()
+    expert_grads_arrive(links, out_down, out_up)
+    for copy in pending:
+        copy.wait()
     links.finish()
 
 
@@ -706,6 +820,23 @@
     table = jnp.pad(rel_table, ((0, SHARD - rel_table.shape[0]), (0, 64 - HEADS)))
     side = jnp.concatenate([gain_attn[:, None], gain_moe[:, None], w_router], axis=1)
     return jnp.concatenate([jnp.pad(side, ((0, 0), (0, 64 - side.shape[1]))), table], axis=1)
+
+
+def hand_out(mixed, tokens, qkv, proj, small, up, down, to_mixed, to_tokens, to_qkv, to_proj, to_small, to_up, to_down):
+    to_mixed[...] = mixed[...]
+    to_tokens[...] = tokens[...]
+    to_qkv[...] = qkv[...]
+    to_proj[...] = proj[...]
+    to_up[...] = up[...].astype(F32)
+    to_down[...] = down[...].astype(F32)
+
+    @pl.when(pl.program_id(0) == 0)
+    def _():
+        to_small[...] = jnp.transpose(small[...])
+
+
+def rows_of(shape, steps):
+    return pl.BlockSpec((shape[0] // steps, shape[1]), lambda i: (i, 0))
 
 
 def body_fast(
@@ -716,16 +847,17 @@
     hbm = pl.BlockSpec(memory_space=pl.ANY)
     sds = jax.ShapeDtypeStruct
     v = pltpu.VMEM
+    shapes = (
+        sds((TOK, D), BF16), sds((TOK, D), F32), sds((SHARD, 3 * D), F32), sds((SHARD, D), F32),
+        sds((SHARD, 128), F32), sds((D, HF), BF16), sds((HF, D), BF16),
+    )
     out = pl.pallas_call(
         layer,
-        out_shape=(
-            sds((TOK, D), BF16), sds((TOK, D), F32), sds((SHARD, 3 * D), F32), sds((SHARD, D), F32),
-            sds((SHARD, 128), F32), sds((D, HF), F32), sds((HF, D), F32),
-        ),
+        out_shape=shapes,
         in_specs=[vm, vm, pl.BlockSpec(memory_space=pltpu.SMEM), vm, vm, hbm, hbm, hbm, hbm, hbm],
         out_specs=[vm, vm, hbm, hbm, hbm, hbm, hbm],
         scratch_shapes=[
-            v((D, WALL), BF16), v((8, D), F32), v((2, TOK, D), BF16),
+            v((D, WALL), BF16), v((8, D), F32), v((8, TOK), F32), v((TOK, 8), F32), v((2, TOK, D), BF16),
             v((TOK, 3 * D), BF16), v((TOK, D), F32), v((TOK, D), BF16),
             v((TOK, 1), F32), v((EXP, ROWS, D), BF16), v((EXP, ROWS, D), BF16),
             v((8 * ROWS, D), BF16), v((8 * ROWS, D), BF16), v((D, HF), BF16), v((HF, D), BF16),
@@ -737,23 +869,37 @@
             v((TOK, 4 * D), BF16), v((16, SEQ), F32), v((128, D), F32),
             v((D, SENTC), BF16), v((D, SENTC), F32), v((4, SHARD, SENTC), BF16), v((8, SHARD, SENTC), BF16),
             v((SHARD, SENTC), BF16), v((SHARD, SENTC), BF16), v((SHARD, SENTC), F32),
-            pltpu.SemaphoreType.DMA((6,)), pltpu.SemaphoreType.DMA((LINKS,)), pltpu.SemaphoreType.DMA((LINKS,)),
+            pltpu.SemaphoreType.DMA((14,)), pltpu.SemaphoreType.DMA((LINKS,)), pltpu.SemaphoreType.DMA((LINKS,)),
         ],
         compiler_params=pltpu.CompilerParams(
             collective_id=0, has_side_effects=True, vmem_limit_bytes=67043328
         ),
         name="layer",
-    )(tokens, cotangent, lengths, routes, slots, w_qkv, w_proj, small, w_up, w_down)
-    mixed, grad_tokens, grad_qkv, grad_proj, side, grad_up, grad_down = out
+    )(tokens, cotangent, lengths, routes.T, slots.T, w_qkv, w_proj, small, w_up, w_down)
+    steps = 4
+    final = list(shapes)
+    final[5], final[6] = sds((D, HF), F32), sds((HF, D), F32)
+    specs = [rows_of(item.shape, steps) for item in shapes]
+    whole_in = pl.BlockSpec((SHARD, 128), lambda i: (0, 0))
+    whole_out = pl.BlockSpec((128, SHARD), lambda i: (0, 0))
+    final[4] = sds((128, SHARD), F32)
+    mixed, grad_tokens, grad_qkv, grad_proj, side, grad_up, grad_down = pl.pallas_call(
+        hand_out,
+        out_shape=tuple(final),
+        grid=(steps,),
+        in_specs=specs[:4] + [whole_in] + specs[5:],
+        out_specs=specs[:4] + [whole_out] + specs[5:],
+        name="hand_out",
+    )(*out)
     return (
         mixed,
         grad_tokens,
-        side[:, 0],
+        side[0],
         grad_qkv,
         grad_proj,
-        side[: rel_table.shape[0], HEAD : HEAD + HEADS],
-        side[:, 1],
-        side[:, 2 : 2 + EXP],
+        side[HEAD : HEAD + HEADS, : rel_table.shape[0]].T,
+        side[1],
+        side[2 : 2 + EXP].T,
         grad_up[None],
         grad_down[None],
     )

time: 218 us -> 197 us (0.904)
  local copies, waits for them, and re-layouts: 22.5 us -> 4.04 us
    unnamed x13 -> x1, local copies, waits for them, and re-layouts: 18.5 us -> 0.68 us
    slice x3 -> x0, local copies, waits for them, and re-layouts: 3.82 us -> none  [the longest x1 1.58 us: body_fast(): side[:, 1]]
    pallas_call x1 -> x2, Pallas kernels: 192 us -> 190 us  [the longest x1 182 us: body_fast(): pl.pallas_call(layer, out_shape=shapes, in_specs=[vm, vm, pl.BlockSpec(me...]
where the time goes in v3:
time: 197 us
  Pallas kernels  190 us (96%)
  local copies, waits for them, and re-layouts  4.04 us (2%)
  other arithmetic  2.08 us (1%)
    pallas_call x1, Pallas kernels, body_fast(): pl.pallas_call(layer, out_shape=shapes, in_specs=[vm, vm, pl.BlockSpec(me...  182 us
    pallas_call x1, Pallas kernels, body_fast(): pl.pallas_call(hand_out, out_shape=tuple(final), grid=(steps,), in_specs=...  8.08 us

profile of v3, /device:TPU:0, one launch (start us, length us, event | category | flops | bytes accessed | tf_op | source)
XLA Modules:
  0.0 196.6 jit_solution(12194675613463223493)
XLA Ops:
  0.6 0.7 pad_maximum_fusion
  1.4 0.1 copy.27
  1.5 1.4 fusion.2.sm
  2.9 181.8 %layer.1 = (bf16[256,768]{1,0:T(8,128)(2,1)}, f32[256,768]{1,0:T(8,128)}, f32[96,2304]{1,0:T(8,128)}, f32[96,768]{1,0:T(8,128)}, f32[96,128]{1,0:T(8,128)}, /*in...) custom-call(bf16[256,768]{1,0:T(8,128)(2,1)} %x_ref.1, bf16[256,768]{1,0:T(8,128)(2,1)} %cot.1, s32[2]{0:T(128)} %lengths.1, ...), custom_call_target="tpu_custom_call" | custom-call | tf_op jit(solution)/shard_map/layer/pallas_call | solution.py:854
  184.6 8.1 %hand_out.1 = (bf16[256,768]{1,0:T(8,128)(2,1)}, f32[256,768]{1,0:T(8,128)}, f32[96,2304]{1,0:T(8,128)}, f32[96,768]{1,0:T(8,128)}, f32[128,96]{1,0:T(8,128)}, /*index=5*/f32[768,1536]{1,0:T(8,128)}, f32[1536,768]{1,0:T(8,128)}) custom-call(bf16[256,768]{1,0:T(8,128)(2,1)} %get-tuple-element.24.mixed, f32[256,768]{1,0:T(8,128)} %get-tuple-element.25.tokens, ...), custom_call_target="tpu_custom_call" | custom-call | tf_op jit(solution)/shard_map/hand_out/pallas_call | solution.py:886
  192.7 1.3 slice_bitcast_fusion.2
  194.0 1.3 slice_bitcast_fusion.1
  195.3 0.7 slice_bitcast_fusion
  196.0 0.7 copy.28

commit v4 on v3

--- a/solution.py
+++ b/solution.py
@@ -102,14 +102,13 @@
         self.started = []
 
 
-def gather_weights(links, wq, wp, sm, wall, local_sem):
+def gather_weights(links, wq, wp, wall, local_sem, others):
     x, c, z, y = place()
     own = pl.ds(pl.multiple_of((z * 2 + y) * SHARD, 16), SHARD)
     fills = [
         pltpu.make_async_copy(wq.at[:, pl.ds(0, LEFTC)], wall.at[own, pl.ds(0, LEFTC)], local_sem.at[0]),
         pltpu.make_async_copy(wq.at[:, pl.ds(LEFTC, LOW)], wall.at[own, pl.ds(HIGH, LOW)], local_sem.at[1]),
         pltpu.make_async_copy(wp, wall.at[own, pl.ds(PROJ, D)], local_sem.at[2]),
-        pltpu.make_async_copy(sm, wall.at[own, pl.ds(SMALL, 128)], local_sem.at[3]),
     ]
     for fill in fills:
         fill.start()
@@ -163,17 +162,18 @@
 
     half = pl.ds(pl.multiple_of(c * HALF, 16), HALF)
     begin(0, wq.at[half, pl.ds(pl.multiple_of(x * LEFTC, 128), LOW)])
+    for copy in others:
+        copy.start()
     for fill in fills:
         fill.wait()
     begin(1, None)
-    begin(2, wp.at[half, :])
     for k in (1, 2, 3):
-        for sub in range(3):
+        for sub in range(2):
             along(sub, k)
-            if k > 1 or sub < 2:
-                over(sub, k - 1)
-        if k == 1:
-            over(2, 0)
+            over(sub, k - 1)
+        if k == 2:
+            begin(2, wp.at[half, :])
+    along(2, 1)
     for sub in range(2):
         over(sub, 3)
 
@@ -197,11 +197,16 @@
     each(gain)
     each(mostly)
 
-    def later():
-        over(2, 3)
-        each(rest)
-
-    return later
+    def first():
+        along(2, 2)
+        over(2, 0)
+
+    def second():
+        along(2, 3)
+        over(2, 1)
+        over(2, 2)
+
+    return first, second, lambda: over(2, 3), lambda: each(rest)
 
 
 def unit(values):
@@ -220,6 +225,19 @@
         line = jnp.broadcast_to(lines[HEAD + h : HEAD + h + 1, :], (SEQ, SEQ))
         rolled = pltpu.roll(line, 0, 1, stride=1, stride_axis=0)
         bias[(h // 2) * SEQ : (h // 2 + 1) * SEQ, (h % 2) * SEQ : (h % 2 + 1) * SEQ] = jnp.where(ahead >= lane, rolled, NEG)
+
+
+def pack(gain_attn, gain_moe, router_t, rel, board, wall):
+    x, c, z, y = place()
+    board[0:SEQ, 0:SEQ] = jnp.zeros((SEQ, SEQ), F32)
+    board[0:1, 0:SHARD] = gain_attn[...].astype(F32)
+    board[1:2, 0:SHARD] = gain_moe[...].astype(F32)
+    board[2 : 2 + EXP, 0:SHARD] = router_t[...].astype(F32)
+    turned = jnp.transpose(board[0:SEQ, 0:SEQ])
+    board[0:SEQ, 0:SEQ] = turned
+    board[0:16, HEAD : HEAD + HEADS] = rel[...].astype(F32)
+    own = pl.ds(pl.multiple_of((z * 2 + y) * SHARD, 16), SHARD)
+    wall[own, SMALL : SMALL + 128] = board[0:SHARD, 0:SEQ].astype(BF16)
 
 
 def stand(routes, slots, lines, columns):
@@ -279,8 +297,10 @@
             ).astype(BF16)
         return carry
 
-    lax.fori_loop(0, PAIRS, pair, 0)
-    later()
+    for t in range(3):
+        later[t]()
+        lax.fori_loop(2 * t, 2 * t + 2, pair, 0)
+    later[3]()
     branch = dot(attended[...], wall[:, PROJ:HIGH])
     for s in range(MB):
         rows = slice(s * SEQ, (s + 1) * SEQ)
@@ -311,8 +331,8 @@
 TILE = 512
 Z_ROWS, Y_ROWS, Y_PART, Z_BACK = 80, 88, 96, 104
 TWIN_W, FACE_W, TWIN_OUT = 112, 114, 120
-RS_TWIN, RS_Y, RS_Z, RS_FACE, RS_OUT = 126, 130, 146, 178, 182
-LINKS = 186
+RS_TWIN, RS_Y, RS_Z, RS_FACE, RS_OUT = 126, 131, 147, 179, 183
+LINKS = 191
 
 
 def quarter(zs):
@@ -543,7 +563,7 @@
     small_t[1:2, :] = gain_grad
 
 
-def attention_backward(x_ref, wall, rows_t, qkv, board, hidden, grad_att, rb, rel_rows, small_t, grad_tokens, midway):
+def attention_backward(x_ref, wall, rows_t, qkv, board, hidden, grad_att, rb, rel_rows, small_t, grad_tokens, midway, formed):
     grad_att[...] = dot(rb[:, 3 * D : 4 * D], wall[:, PROJ:HIGH], 1, 1).astype(BF16)
     midway()
     lane = lax.broadcasted_iota(jnp.int32, (SEQ, 128), 1)
@@ -578,7 +598,9 @@
             rel_rows[pl.ds(2 * p + j, 1), :] = jnp.sum(rolled, axis=0, keepdims=True)
         return carry
 
-    lax.fori_loop(0, PAIRS, pair, 0)
+    for t in range(3):
+        lax.fori_loop(2 * t, 2 * t + 2, pair, 0)
+        formed[t]()
     grad_low = dot(rb[:, 0:LEFTC], wall[:, 0:LEFTC], 1, 1) + dot(
         rb[:, LEFTC : 3 * D], wall[:, HIGH:WALL], 1, 1
     )
@@ -604,21 +626,27 @@
 
 
 HC = D // 2
-GROUPS = (
-    (1, 2 * HC, HC, lambda core: 3 * D + core * HC, lambda core: core * HC),
-    (0, HC, HC, lambda core: 2 * D + core * HC, lambda core: 2 * D + core * HC),
-    (0, 0, HC, lambda core: core * D, lambda core: core * D),
-    (0, 3 * HC, HC + 128, lambda core: core * D + HC, lambda core: core * D + HC),
-)
+SMALLS = SENTC - 128
+
+
+def portions(group):
+    if group == 0:
+        return 1, 2 * HC, HC, ((0, HC, lambda core: 3 * D + core * HC, lambda core: core * HC),)
+    t = group - 1
+    both = (
+        (0, 256, lambda core: core * D + 256 * t, lambda core: core * D + 256 * t),
+        (256, 128, lambda core: 2 * D + 256 * t + 128 * core, lambda core: 2 * D + 256 * t + 128 * core),
+    )
+    return 0, (0, HC, 3 * HC)[t], HC + 128 * (t == 2), both
 
 
 class Reduction:
     def __init__(self, links, group, left, rb, small_t, give, take, total, y_take, z_take, face_give, face_take, last):
         self.links, self.group = links, group
-        which, first, self.width, self.rhs, self.target = GROUPS[group]
-        self.cols = slice(first, first + self.width)
+        which, first, width, portion = portions(group)
+        self.cols = slice(first, first + width)
         self.core_cols = slice(first, first + HC)
-        self.small_cols = slice(first + HC, first + self.width)
+        self.portion = [(slice(first + at, first + at + wide), wide, rhs, target) for at, wide, rhs, target in portion]
         self.lhs, self.rb, self.small_t = left.at[which], rb, small_t
         self.give, self.take, self.total = give, take, total
         self.y_take, self.z_take, self.face_give, self.face_take, self.last = y_take, z_take, face_give, face_take, last
@@ -631,8 +659,9 @@
     def tile(self, core, keep):
         def step(m, carry):
             rows = pl.ds(pl.multiple_of(m * 256, 256), 256)
-            rhs = self.rb[:, pl.ds(pl.multiple_of(self.rhs(core), 128), HC)]
-            keep[rows, self.core_cols] = dot(self.lhs[:, rows], rhs, 0, 0).astype(keep.dtype)
+            for cols, wide, rhs, target in self.portion:
+                right = self.rb[:, pl.ds(pl.multiple_of(rhs(core), 128), wide)]
+                keep[rows, cols] = dot(self.lhs[:, rows], right, 0, 0).astype(keep.dtype)
             return carry
 
         lax.fori_loop(0, 3, step, 0)
@@ -640,13 +669,17 @@
     def form(self):
         x, c, z, y = self.place
         self.tile(1 - c, self.give)
-        if self.group == 3:
-            small = jnp.transpose(self.small_t[...]).astype(BF16)
-            self.give[:, self.small_cols] = small
-            self.total[:, self.small_cols] = small.astype(F32)
-        slot = RS_TWIN + self.group
-        self.sent = self.links.go(None, self.give.at[:, self.cols], self.take.at[:, self.cols], slot, slot, self.twin)
+        self.sent = [self.to_twin(self.core_cols, RS_TWIN + self.group)]
         self.tile(c, self.total)
+
+    def to_twin(self, cols, slot):
+        return self.links.go(None, self.give.at[:, cols], self.take.at[:, cols], slot, slot, self.twin)
+
+    def form_small(self):
+        small = jnp.transpose(self.small_t[...])
+        self.give[:, SMALLS:SENTC] = small.astype(BF16)
+        self.total[:, SMALLS:SENTC] = small.astype(BF16).astype(F32)
+        self.sent.append(self.to_twin(slice(SMALLS, SENTC), RS_TWIN + 4))
 
     def shard(self, zs, ys):
         return pl.ds(pl.multiple_of((zs * 2 + ys) * SHARD, 16), SHARD)
@@ -654,8 +687,11 @@
     def halve(self):
         x, c, z, y = self.place
         links, cols = self.links, self.cols
-        links.arrive(None, self.take.at[:, cols], RS_TWIN + self.group, self.twin)
-        links.leave(self.sent)
+        links.arrive(None, self.take.at[:, self.core_cols], RS_TWIN + self.group, self.twin)
+        if self.group == 3:
+            links.arrive(None, self.take.at[:, SMALLS:SENTC], RS_TWIN + 4, self.twin)
+        for copy in self.sent:
+            links.leave(copy)
         for zs in self.order:
             rows = self.shard(zs, 1 - y)
             self.give[rows, cols] = (self.total[rows, cols] + self.take[rows, cols].astype(F32)).astype(BF16)
@@ -711,46 +747,57 @@
         self.links.arrive(None, self.face_take.at[:, cols], RS_FACE + self.group, self.facing)
         self.last[:, cols] = self.face_give[:, cols].astype(F32) + self.face_take[:, cols].astype(F32)
         self.out = out_proj if self.group == 0 else out_qkv
-        slot = RS_OUT + self.group
-        part, there = self.last.at[:, self.core_cols], self.landing(c)
-        self.links.go(None, part, there, slot, slot, self.twin)
-        copies = [pltpu.make_async_copy(part, there, local_sem.at[self.group])]
+        copies = []
+        for i, (part, there) in enumerate(self.landing(c)):
+            slot = RS_OUT + self.group * 2 + i
+            self.links.go(None, part, there, slot, slot, self.twin)
+            copies.append(pltpu.make_async_copy(part, there, local_sem.at[16 + self.group * 2 + i]))
         if self.group == 3:
-            copies.append(pltpu.make_async_copy(self.last.at[:, self.small_cols], out_small, local_sem.at[6]))
+            copies.append(pltpu.make_async_copy(self.last.at[:, SMALLS:SENTC], out_small, local_sem.at[6]))
         for copy in copies:
             copy.start()
         return copies
 
     def landing(self, core):
-        return self.out.at[:, pl.ds(pl.multiple_of(self.target(core), 128), HC)]
+        return [
+            (self.last.at[:, cols], self.out.at[:, pl.ds(pl.multiple_of(target(core), 128), wide)])
+            for cols, wide, rhs, target in self.portion
+        ]
 
     def landed(self):
         x, c, z, y = self.place
-        self.links.arrive(None, self.landing(1 - c), RS_OUT + self.group, self.twin)
+        for i, (part, there) in enumerate(self.landing(1 - c)):
+            self.links.arrive(None, there, RS_OUT + self.group * 2 + i, self.twin)
 
 
 def layer(
-    x_ref, cot, lengths, routes, slots, wq, wp, sm, w_up, w_down,
-    mixed, grad_tokens, out_qkv, out_proj, out_small, out_up, out_down,
+    x_in, cot_in, lengths, routes, slots, gain_attn, gain_moe, router_t, rel, wq, wp, w_up, w_down,
+    mixed_out, tokens_out, out_qkv, out_proj, out_small, out_up, out_down,
+    x_ref, cot, mixed, grad_tokens, board,
     wall, rows_t, lines, columns, left, qkv, hidden, normed2, gates, out_f, out_g, recv_f, recv_g, up, down, act, slope,
     part_f, part_g, take_f, take_g, back_f, back_g, dn_own, dn_give, dn_take, dn_face, up_own, up_give, up_take, up_face,
     rb, rel_rows, small_t, take, total, y_take, z_take, face_give, face_take, last,
     local_sem, send_sem, recv_sem,
 ):
+    inputs = [
+        pltpu.make_async_copy(x_in, x_ref, local_sem.at[24]),
+        pltpu.make_async_copy(cot_in, cot, local_sem.at[25]),
+    ]
     fetch = [
         pltpu.make_async_copy(w_up.at[0], up, local_sem.at[4]),
         pltpu.make_async_copy(w_down.at[0], down, local_sem.at[5]),
     ]
+    pack(gain_attn, gain_moe, router_t, rel, board, wall)
     greet()
     links = Links(send_sem, recv_sem)
-    for copy in fetch:
-        copy.start()
+    later = gather_weights(links, wq, wp, wall, local_sem, inputs + fetch)
     stand(routes, slots, lines, columns)
     rel_rows[...] = jnp.zeros_like(rel_rows)
-    later = gather_weights(links, wq, wp, sm, wall, local_sem)
+    for copy in inputs:
+        copy.wait()
     normed, attended = left.at[0], left.at[1]
     attention_forward(
-        later, x_ref, cot, lengths, columns, wall, rows_t, total, normed, qkv, attended, hidden, normed2, gates, out_f, out_g
+        later, x_ref, cot, lengths, columns, wall, rows_t, board, normed, qkv, attended, hidden, normed2, gates, out_f, out_g
     )
     for copy in fetch:
         copy.wait()
@@ -760,13 +807,20 @@
         (back_f, back_g), downs, ups,
     )
     combine(cot, lengths, columns, rows_t, hidden, normed2, gates, back_f, back_g, mixed, rb, small_t)
-    proj, values, first, second = (
+    pending = []
+
+    def put(src, dst, i):
+        copy = pltpu.make_async_copy(src, dst, local_sem.at[i])
+        copy.start()
+        pending.append(copy)
+
+    put(mixed, mixed_out, 26)
+    proj, one, two, three = (
         Reduction(
             links, group, left, rb, small_t, act.at[0:D, :], take, total, y_take, z_take, face_give, face_take, last
         )
         for group in range(4)
     )
-    pending = []
 
     def grads(piece):
         pending.append(expert_grad_out(links, piece, downs, ups, out_down, out_up, local_sem))
@@ -774,41 +828,55 @@
     def publish(item):
         pending.extend(item.publish(out_qkv, out_proj, out_small, local_sem))
 
+    def early():
+        one.form()
+        proj.chain(0)
+
+    def middle():
+        one.halve()
+        two.form()
+        proj.chain(1)
+
+    def late():
+        two.halve()
+        three.form()
+        proj.chain(2)
+        one.chain(0)
+
     proj.form()
     attention_backward(
-        x_ref, wall, rows_t, qkv, total, hidden, normed2, rb, rel_rows, small_t, grad_tokens, proj.halve
-    )
-    values.form()
-    proj.chain(0)
-    values.halve()
-    proj.chain(1)
-    first.form()
-    proj.chain(2)
+        x_ref, wall, rows_t, qkv, board, hidden, normed2, rb, rel_rows, small_t, grad_tokens, proj.halve,
+        (early, middle, late),
+    )
+    three.form_small()
+    put(grad_tokens, tokens_out, 27)
     proj.chain(3)
-    first.halve()
-    values.chain(0)
-    second.form()
-    values.chain(1)
-    second.halve()
-    values.chain(2)
-    values.chain(3)
+    one.chain(1)
+    three.halve()
+    two.chain(0)
+    one.chain(2)
     grads(0)
+    proj.face()
+    two.chain(1)
+    one.chain(3)
     grads(1)
-    proj.face()
-    for k in range(4):
-        first.chain(k)
-    values.face()
+    three.chain(0)
+    two.chain(2)
     grads(2)
-    for k in range(4):
-        second.chain(k)
-    first.face()
+    one.face()
+    three.chain(1)
+    two.chain(3)
     grads(3)
-    second.face()
+    three.chain(2)
+    two.face()
     grads(4)
+    three.chain(3)
     grads(5)
-    for item in (proj, values, first, second):
+    three.face()
+    items = (proj, one, two, three)
+    for item in items:
         publish(item)
-    for item in (proj, values, first, second):
+    for item in items:
         item.landed()
     expert_grads_arrive(links, out_down, out_up)
     for copy in pending:
@@ -816,13 +884,10 @@
     links.finish()
 
 
-def pack_small(gain_attn, gain_moe, w_router, rel_table):
-    table = jnp.pad(rel_table, ((0, SHARD - rel_table.shape[0]), (0, 64 - HEADS)))
-    side = jnp.concatenate([gain_attn[:, None], gain_moe[:, None], w_router], axis=1)
-    return jnp.concatenate([jnp.pad(side, ((0, 0), (0, 64 - side.shape[1]))), table], axis=1)
-
-
-def hand_out(mixed, tokens, qkv, proj, small, up, down, to_mixed, to_tokens, to_qkv, to_proj, to_small, to_up, to_down):
+def hand_out(
+    mixed, tokens, qkv, proj, small, up, down,
+    to_mixed, to_tokens, to_qkv, to_proj, to_gain_attn, to_gain_moe, to_router, to_rel, to_up, to_down,
+):
     to_mixed[...] = mixed[...]
     to_tokens[...] = tokens[...]
     to_qkv[...] = qkv[...]
@@ -832,7 +897,11 @@
 
     @pl.when(pl.program_id(0) == 0)
     def _():
-        to_small[...] = jnp.transpose(small[...])
+        turned = jnp.transpose(small[...])
+        to_gain_attn[...] = turned[0]
+        to_gain_moe[...] = turned[1]
+        to_router[...] = turned[2 : 2 + EXP]
+        to_rel[...] = small[0:16, HEAD : HEAD + HEADS]
 
 
 def rows_of(shape, steps):
@@ -842,7 +911,6 @@
 def body_fast(
     tokens, cotangent, lengths, routes, slots, gain_attn, w_qkv, w_proj, rel_table, gain_moe, w_router, w_up, w_down
 ):
-    small = pack_small(gain_attn, gain_moe, w_router, rel_table)
     vm = pl.BlockSpec(memory_space=pltpu.VMEM)
     hbm = pl.BlockSpec(memory_space=pl.ANY)
     sds = jax.ShapeDtypeStruct
@@ -854,9 +922,10 @@
     out = pl.pallas_call(
         layer,
         out_shape=shapes,
-        in_specs=[vm, vm, pl.BlockSpec(memory_space=pltpu.SMEM), vm, vm, hbm, hbm, hbm, hbm, hbm],
-        out_specs=[vm, vm, hbm, hbm, hbm, hbm, hbm],
+        in_specs=[hbm, hbm, pl.BlockSpec(memory_space=pltpu.SMEM), vm, vm, vm, vm, vm, vm, hbm, hbm, hbm, hbm],
+        out_specs=[hbm, hbm, hbm, hbm, hbm, hbm, hbm],
         scratch_shapes=[
+            v((TOK, D), BF16), v((TOK, D), BF16), v((TOK, D), BF16), v((TOK, D), F32), v((D, D), F32),
             v((D, WALL), BF16), v((8, D), F32), v((8, TOK), F32), v((TOK, 8), F32), v((2, TOK, D), BF16),
             v((TOK, 3 * D), BF16), v((TOK, D), F32), v((TOK, D), BF16),
             v((TOK, 1), F32), v((EXP, ROWS, D), BF16), v((EXP, ROWS, D), BF16),
@@ -869,37 +938,43 @@
             v((TOK, 4 * D), BF16), v((16, SEQ), F32), v((128, D), F32),
             v((D, SENTC), BF16), v((D, SENTC), F32), v((4, SHARD, SENTC), BF16), v((8, SHARD, SENTC), BF16),
             v((SHARD, SENTC), BF16), v((SHARD, SENTC), BF16), v((SHARD, SENTC), F32),
-            pltpu.SemaphoreType.DMA((14,)), pltpu.SemaphoreType.DMA((LINKS,)), pltpu.SemaphoreType.DMA((LINKS,)),
+            pltpu.SemaphoreType.DMA((28,)), pltpu.SemaphoreType.DMA((LINKS,)), pltpu.SemaphoreType.DMA((LINKS,)),
         ],
         compiler_params=pltpu.CompilerParams(
             collective_id=0, has_side_effects=True, vmem_limit_bytes=67043328
         ),
         name="layer",
-    )(tokens, cotangent, lengths, routes.T, slots.T, w_qkv, w_proj, small, w_up, w_down)
+    )(
+        tokens, cotangent, lengths, routes.T, slots.T, gain_attn[None], gain_moe[None], w_router.T, rel_table, w_qkv, w_proj,
+        w_up, w_down,
+    )
     steps = 4
-    final = list(shapes)
-    final[5], final[6] = sds((D, HF), F32), sds((HF, D), F32)
-    specs = [rows_of(item.shape, steps) for item in shapes]
-    whole_in = pl.BlockSpec((SHARD, 128), lambda i: (0, 0))
-    whole_out = pl.BlockSpec((128, SHARD), lambda i: (0, 0))
-    final[4] = sds((128, SHARD), F32)
-    mixed, grad_tokens, grad_qkv, grad_proj, side, grad_up, grad_down = pl.pallas_call(
-        hand_out,
-        out_shape=tuple(final),
-        grid=(steps,),
-        in_specs=specs[:4] + [whole_in] + specs[5:],
-        out_specs=specs[:4] + [whole_out] + specs[5:],
-        name="hand_out",
-    )(*out)
+    tall = [rows_of(item.shape, steps) for item in shapes]
+    small_in = pl.BlockSpec((SHARD, 128), lambda i: (0, 0))
+    small_out = [
+        pl.BlockSpec((SHARD,), lambda i: (0,)), pl.BlockSpec((SHARD,), lambda i: (0,)),
+        pl.BlockSpec((EXP, SHARD), lambda i: (0, 0)), pl.BlockSpec((16, HEADS), lambda i: (0, 0)),
+    ]
+    small = (sds((SHARD,), F32), sds((SHARD,), F32), sds((EXP, SHARD), F32), sds((16, HEADS), F32))
+    mixed, grad_tokens, grad_qkv, grad_proj, grad_gain_attn, grad_gain_moe, grad_router, grad_rel, grad_up, grad_down = (
+        pl.pallas_call(
+            hand_out,
+            out_shape=shapes[:4] + small + (sds((D, HF), F32), sds((HF, D), F32)),
+            grid=(steps,),
+            in_specs=tall[:4] + [small_in] + tall[5:],
+            out_specs=tall[:4] + small_out + tall[5:],
+            name="hand_out",
+        )(*out)
+    )
     return (
         mixed,
         grad_tokens,
-        side[0],
+        grad_gain_attn,
         grad_qkv,
         grad_proj,
-        side[HEAD : HEAD + HEADS, : rel_table.shape[0]].T,
-        side[1],
-        side[2 : 2 + EXP].T,
+        grad_rel,
+        grad_gain_moe,
+        grad_router.T,
         grad_up[None],
         grad_down[None],
     )

time: 197 us -> 180 us (0.914)
  Pallas kernels: 190 us -> 179 us
  local copies, waits for them, and re-layouts: 4.04 us -> 0 us
  other arithmetic: 2.08 us -> 0 us
    pallas_call x2, Pallas kernels: 190 us -> 179 us  [the longest x1 171 us: body_fast(): pl.pallas_call(layer, out_shape=shapes, in_specs=[hbm, hbm, pl.BlockSpec(...]
    concatenate x2 -> x0, other arithmetic: 2.08 us -> none  [the longest x1 1.37 us: pack_small(): jnp.concatenate([jnp.pad(side, ((0, 0), (0, 64 - side.shape[1]))), table]...]
where the time goes in v4:
time: 180 us
  Pallas kernels  179 us (99%)
    pallas_call x1, Pallas kernels, body_fast(): pl.pallas_call(layer, out_shape=shapes, in_specs=[hbm, hbm, pl.BlockSpec(...  171 us
    pallas_call x1, Pallas kernels, body_fast(): pl.pallas_call(hand_out, out_shape=shapes[:4] + small + (sds((D, HF), F32...  8.12 us

profile of v4, /device:TPU:0, one launch (start us, length us, event | category | flops | bytes accessed | tf_op | source)
XLA Modules:
  0.0 179.7 jit_solution(18256938424963884827)
XLA Ops:
  0.6 170.7 %layer.1 = (bf16[256,768]{1,0:T(8,128)(2,1)}, f32[256,768]{1,0:T(8,128)}, f32[96,2304]{1,0:T(8,128)}, f32[96,768]{1,0:T(8,128)}, f32[96,128]{1,0:T(8,128)}, /*in...) custom-call(bf16[256,768]{1,0:T(8,128)(2,1)} %x_in.1, bf16[256,768]{1,0:T(8,128)(2,1)} %cot_in.1, s32[2]{0:T(128)} %lengths.1, ...), custom_call_target="tpu_custom_call" | custom-call | tf_op jit(solution)/shard_map/layer/pallas_call | solution.py:922
  171.4 8.1 %hand_out.1 = (bf16[256,768]{1,0:T(8,128)(2,1)}, f32[256,768]{1,0:T(8,128)}, f32[96,2304]{1,0:T(8,128)}, f32[96,768]{1,0:T(8,128)}, f32[96]{0:T(128)}, /*index=5...) custom-call(bf16[256,768]{1,0:T(8,128)(2,1)} %get-tuple-element.27.mixed, ...), custom_call_target="tpu_custom_call" | custom-call | tf_op jit(solution)/shard_map/hand_out/pallas_call | solution.py:960

commit v5 on v4

--- a/solution.py
+++ b/solution.py
@@ -64,7 +64,7 @@
     targets += [device(x, c, (z + k) % 4, y) for k in (1, 2, 3)]
     for target in targets:
         pl.semaphore_signal(barrier, inc=1, device_id=target, device_id_type=MESH)
-    pl.semaphore_wait(barrier, len(targets))
+    return lambda: pl.semaphore_wait(barrier, len(targets))
 
 
 def dot(a, b, ca=1, cb=0):
@@ -102,7 +102,7 @@
         self.started = []
 
 
-def gather_weights(links, wq, wp, wall, local_sem, others):
+def gather_weights(links, wq, wp, wall, local_sem, others, ready):
     x, c, z, y = place()
     own = pl.ds(pl.multiple_of((z * 2 + y) * SHARD, 16), SHARD)
     fills = [
@@ -110,8 +110,9 @@
         pltpu.make_async_copy(wq.at[:, pl.ds(LEFTC, LOW)], wall.at[own, pl.ds(HIGH, LOW)], local_sem.at[1]),
         pltpu.make_async_copy(wp, wall.at[own, pl.ds(PROJ, D)], local_sem.at[2]),
     ]
-    for fill in fills:
-        fill.start()
+    for copy in fills + others:
+        copy.start()
+    ready()
     share = pl.ds(pl.multiple_of(x * HIGH, 128), LOW)
     gained = pl.ds(pl.multiple_of((1 - x) * HIGH, 128), LOW)
     columns = (share, pl.ds(LOW, MORE), pl.ds(PROJ, D))
@@ -162,8 +163,6 @@
 
     half = pl.ds(pl.multiple_of(c * HALF, 16), HALF)
     begin(0, wq.at[half, pl.ds(pl.multiple_of(x * LEFTC, 128), LOW)])
-    for copy in others:
-        copy.start()
     for fill in fills:
         fill.wait()
     begin(1, None)
@@ -213,6 +212,16 @@
     return lax.rsqrt(jnp.mean(values * values, axis=-1, keepdims=True) + 1e-06)
 
 
+def heads(rows):
+    lane = lax.broadcasted_iota(jnp.int32, rows.shape, 1)
+    none = jnp.zeros_like(rows)
+    return jnp.concatenate([jnp.where(lane < HEAD, rows, none), jnp.where(lane < HEAD, none, rows)], axis=0)
+
+
+def beside(blocks):
+    return jnp.concatenate([blocks[0:SEQ], blocks[SEQ : 2 * SEQ]], axis=1)
+
+
 def build_bias(wall, bias):
     table = jnp.concatenate(
         [wall[f * SHARD : f * SHARD + 16, SMALL : SMALL + 128] for f in range(8)], axis=0
@@ -224,7 +233,7 @@
     for h in range(HEADS):
         line = jnp.broadcast_to(lines[HEAD + h : HEAD + h + 1, :], (SEQ, SEQ))
         rolled = pltpu.roll(line, 0, 1, stride=1, stride_axis=0)
-        bias[(h // 2) * SEQ : (h // 2 + 1) * SEQ, (h % 2) * SEQ : (h % 2 + 1) * SEQ] = jnp.where(ahead >= lane, rolled, NEG)
+        bias[h * SEQ : (h + 1) * SEQ, 0:SEQ] = jnp.where(ahead >= lane, rolled, NEG)
 
 
 def pack(gain_attn, gain_moe, router_t, rel, board, wall):
@@ -273,27 +282,21 @@
     normed[...] = (x * unit(x) * rows_t[0:1, :]).astype(BF16)
     qkv[:, 0:LEFTC] = dot(normed[...], wall[:, 0:LEFTC]).astype(BF16)
     qkv[:, LEFTC : 3 * D] = dot(normed[...], wall[:, HIGH:WALL]).astype(BF16)
-    lane = lax.broadcasted_iota(jnp.int32, (SEQ, 128), 1)
+    lane = lax.broadcasted_iota(jnp.int32, (2 * SEQ, 128), 1)
 
     def pair(p, carry):
-        blocks = pl.ds(pl.multiple_of(p * SEQ, SEQ), SEQ)
+        blocks = pl.ds(pl.multiple_of(p * 2 * SEQ, SEQ), 2 * SEQ)
         for s in range(MB):
             rows = slice(s * SEQ, (s + 1) * SEQ)
             q = qkv[rows, pl.ds(pl.multiple_of(p * 128, 128), 128)]
             k = qkv[rows, pl.ds(pl.multiple_of(D + p * 128, 128), 128)]
             v = qkv[rows, pl.ds(pl.multiple_of(2 * D + p * 128, 128), 128)]
-            alive = lane < lengths[s]
-            got = []
-            for j in range(2):
-                mine = (lane < HEAD) if j == 0 else (lane >= HEAD)
-                raw = dot(jnp.where(mine, q, jnp.zeros_like(q)), k, 1, 1)
-                scores = jnp.where(alive, raw * SCALE + board[blocks, j * SEQ : (j + 1) * SEQ], NEG)
-                scores = jnp.exp(scores - jnp.max(scores, axis=-1, keepdims=True))
-                share = scores * (1.0 / jnp.sum(scores, axis=-1, keepdims=True))
-                board[blocks, (2 + 2 * s + j) * SEQ : (3 + 2 * s + j) * SEQ] = share
-                got.append(dot(share.astype(BF16), v))
-            attended[rows, pl.ds(pl.multiple_of(p * 128, 128), 128)] = jnp.where(
-                lane < HEAD, got[0], got[1]
+            scores = jnp.where(lane < lengths[s], dot(heads(q), k, 1, 1) * SCALE + board[blocks, 0:SEQ], NEG)
+            scores = jnp.exp(scores - jnp.max(scores, axis=-1, keepdims=True))
+            share = scores * (1.0 / jnp.sum(scores, axis=-1, keepdims=True))
+            board[blocks, (1 + s) * SEQ : (2 + s) * SEQ] = share
+            attended[rows, pl.ds(pl.multiple_of(p * 128, 128), 128)] = dot(
+                beside(share.astype(BF16)), heads(v)
             ).astype(BF16)
         return carry
 
@@ -469,12 +472,8 @@
 
         lax.fori_loop(0, 3, step, 0)
 
-    pairs = ((0, 3), (1, 2), (1, 3))
-    for i, (one, w) in enumerate(((down_tile, w_down), (up_tile, w_up))):
-        own, give, got, face = w
-        tiles(one, 1 - c, give)
-        sent = links.go(None, give, got, TWIN_W + i, TWIN_W + i, twin)
-        tiles(one, c, own)
+    def spread(i, sent):
+        own, give, got, face = (w_down, w_up)[i]
         links.arrive(None, got, TWIN_W + i, twin)
         links.leave(sent)
         count = own.shape[0] // 3
@@ -482,8 +481,18 @@
             rows = slice(m * count, (m + 1) * count)
             give[rows, :] = (own[rows, :] + got[rows, :].astype(F32)).astype(BF16)
             links.go(None, give.at[rows, :], face.at[rows, :], FACE_W + i * 3 + m, FACE_W + i * 3 + m, facing)
-        merge(*pairs[i])
-    merge(*pairs[2])
+
+    tiles(down_tile, 1 - c, w_down[1])
+    sent = links.go(None, w_down[1], w_down[2], TWIN_W, TWIN_W, twin)
+    merge(0, 3)
+    tiles(down_tile, c, w_down[0])
+    spread(0, sent)
+    merge(1, 2)
+    tiles(up_tile, 1 - c, w_up[1])
+    sent = links.go(None, w_up[1], w_up[2], TWIN_W + 1, TWIN_W + 1, twin)
+    merge(1, 3)
+    tiles(up_tile, c, w_up[0])
+    spread(1, sent)
     merge(0, 0)
     merge(1, 0)
     for kind in range(2):
@@ -572,29 +581,24 @@
     flip = jnp.concatenate([flip] * MB, axis=1)
 
     def pair(p, carry):
-        blocks = pl.ds(pl.multiple_of(p * SEQ, SEQ), SEQ)
-        scores = [[None] * MB, [None] * MB]
+        blocks = pl.ds(pl.multiple_of(p * 2 * SEQ, SEQ), 2 * SEQ)
+        scores = []
         for s in range(MB):
             rows = slice(s * SEQ, (s + 1) * SEQ)
             cols = [pl.ds(pl.multiple_of(i * D + p * 128, 128), 128) for i in range(3)]
             q, k, v = (qkv[rows, cols[i]] for i in range(3))
-            grad = grad_att[rows, cols[0]]
-            grads = [[], [], []]
-            for j in range(2):
-                mine = (lane < HEAD) if j == 0 else (lane >= HEAD)
-                share = board[blocks, (2 + 2 * s + j) * SEQ : (3 + 2 * s + j) * SEQ]
-                grad_probs = dot(jnp.where(mine, grad, jnp.zeros_like(grad)), v, 1, 1)
-                inner = jnp.sum(share * grad_probs, axis=-1, keepdims=True)
-                grad_scores = (share * (grad_probs - inner)).astype(BF16)
-                scores[j][s] = grad_scores
-                grads[0].append(dot(grad_scores, k) * SCALE)
-                grads[1].append(dot(grad_scores, q, 0, 0) * SCALE)
-                grads[2].append(dot(share.astype(BF16), grad, 0, 0))
-            for i in range(3):
-                rb[rows, cols[i]] = jnp.where(lane < HEAD, grads[i][0], grads[i][1]).astype(BF16)
+            grad = heads(grad_att[rows, cols[0]])
+            share = board[blocks, (1 + s) * SEQ : (2 + s) * SEQ]
+            grad_probs = dot(grad, v, 1, 1)
+            inner = jnp.sum(share * grad_probs, axis=-1, keepdims=True)
+            grad_scores = (share * (grad_probs - inner)).astype(BF16)
+            scores.append(beside(grad_scores))
+            rb[rows, cols[0]] = (dot(scores[s], heads(k)) * SCALE).astype(BF16)
+            rb[rows, cols[1]] = (dot(grad_scores, heads(q), 0, 0) * SCALE).astype(BF16)
+            rb[rows, cols[2]] = dot(share.astype(BF16), grad, 0, 0).astype(BF16)
+        flipped = dot(flip, jnp.concatenate(scores, axis=0))
         for j in range(2):
-            flipped = dot(flip, jnp.concatenate(scores[j], axis=0))
-            rolled = pltpu.roll(flipped, 1, 1, stride=1, stride_axis=0)
+            rolled = pltpu.roll(flipped[:, j * SEQ : (j + 1) * SEQ], 1, 1, stride=1, stride_axis=0)
             rel_rows[pl.ds(2 * p + j, 1), :] = jnp.sum(rolled, axis=0, keepdims=True)
         return carry
 
@@ -787,12 +791,16 @@
         pltpu.make_async_copy(w_up.at[0], up, local_sem.at[4]),
         pltpu.make_async_copy(w_down.at[0], down, local_sem.at[5]),
     ]
-    pack(gain_attn, gain_moe, router_t, rel, board, wall)
-    greet()
+    met = greet()
     links = Links(send_sem, recv_sem)
-    later = gather_weights(links, wq, wp, wall, local_sem, inputs + fetch)
-    stand(routes, slots, lines, columns)
-    rel_rows[...] = jnp.zeros_like(rel_rows)
+
+    def ready():
+        pack(gain_attn, gain_moe, router_t, rel, board, wall)
+        stand(routes, slots, lines, columns)
+        rel_rows[...] = jnp.zeros_like(rel_rows)
+        met()
+
+    later = gather_weights(links, wq, wp, wall, local_sem, inputs + fetch, ready)
     for copy in inputs:
         copy.wait()
     normed, attended = left.at[0], left.at[1]
@@ -884,28 +892,58 @@
     links.finish()
 
 
+PARTS = 6
+
+
 def hand_out(
     mixed, tokens, qkv, proj, small, up, down,
     to_mixed, to_tokens, to_qkv, to_proj, to_gain_attn, to_gain_moe, to_router, to_rel, to_up, to_down,
+    v_mixed, v_tokens, v_qkv, v_proj, v_small, v_up, v_down,
+    v_gain_attn, v_gain_moe, v_router, v_rel, wide_up, wide_down, in_sem, out_sem,
 ):
-    to_mixed[...] = mixed[...]
-    to_tokens[...] = tokens[...]
-    to_qkv[...] = qkv[...]
-    to_proj[...] = proj[...]
-    to_up[...] = up[...].astype(F32)
-    to_down[...] = down[...].astype(F32)
-
-    @pl.when(pl.program_id(0) == 0)
-    def _():
-        turned = jnp.transpose(small[...])
-        to_gain_attn[...] = turned[0]
-        to_gain_moe[...] = turned[1]
-        to_router[...] = turned[2 : 2 + EXP]
-        to_rel[...] = small[0:16, HEAD : HEAD + HEADS]
-
-
-def rows_of(shape, steps):
-    return pl.BlockSpec((shape[0] // steps, shape[1]), lambda i: (i, 0))
+    def rows(array, i):
+        count = array.shape[0] // PARTS
+        return pl.ds(i * count, count)
+
+    def copy(src, dst, sem, i):
+        item = pltpu.make_async_copy(src, dst, sem.at[i])
+        item.start()
+        return item
+
+    halves = [
+        (source, held, wide, out, rows(source, i))
+        for i in range(PARTS)
+        for source, held, wide, out in ((up, v_up, wide_up, to_up), (down, v_down, wide_down, to_down))
+    ]
+    coming = [copy(source.at[at], held.at[at], in_sem, i) for i, (source, held, _, _, at) in enumerate(halves)]
+    plain = ((tokens, v_tokens, to_tokens), (qkv, v_qkv, to_qkv), (mixed, v_mixed, to_mixed), (proj, v_proj, to_proj))
+    first = len(halves)
+    little = copy(small, v_small, in_sem, first + len(plain))
+    others = [copy(source, held, in_sem, first + i) for i, (source, held, _) in enumerate(plain)]
+    going = []
+
+    def put(src, dst):
+        going.append(copy(src, dst, out_sem, len(going)))
+
+    for item, (source, held, wide, out, at) in zip(coming, halves):
+        item.wait()
+        wide[at] = held[at].astype(F32)
+        put(wide.at[at], out.at[at])
+    little.wait()
+    turned = jnp.transpose(v_small[...])
+    v_gain_attn[...] = turned[0]
+    v_gain_moe[...] = turned[1]
+    v_router[...] = turned[2 : 2 + EXP]
+    v_rel[...] = v_small[0:16, HEAD : HEAD + HEADS]
+    put(v_gain_attn, to_gain_attn)
+    put(v_gain_moe, to_gain_moe)
+    put(v_router, to_router)
+    put(v_rel, to_rel)
+    for item, (_, held, out) in zip(others, plain):
+        item.wait()
+        put(held, out)
+    for item in going:
+        item.wait()
 
 
 def body_fast(
@@ -925,7 +963,7 @@
         in_specs=[hbm, hbm, pl.BlockSpec(memory_space=pltpu.SMEM), vm, vm, vm, vm, vm, vm, hbm, hbm, hbm, hbm],
         out_specs=[hbm, hbm, hbm, hbm, hbm, hbm, hbm],
         scratch_shapes=[
-            v((TOK, D), BF16), v((TOK, D), BF16), v((TOK, D), BF16), v((TOK, D), F32), v((D, D), F32),
+            v((TOK, D), BF16), v((TOK, D), BF16), v((TOK, D), BF16), v((TOK, D), F32), v((HEADS * SEQ, 3 * SEQ), F32),
             v((D, WALL), BF16), v((8, D), F32), v((8, TOK), F32), v((TOK, 8), F32), v((2, TOK, D), BF16),
             v((TOK, 3 * D), BF16), v((TOK, D), F32), v((TOK, D), BF16),
             v((TOK, 1), F32), v((EXP, ROWS, D), BF16), v((EXP, ROWS, D), BF16),
@@ -948,21 +986,16 @@
         tokens, cotangent, lengths, routes.T, slots.T, gain_attn[None], gain_moe[None], w_router.T, rel_table, w_qkv, w_proj,
         w_up, w_down,
     )
-    steps = 4
-    tall = [rows_of(item.shape, steps) for item in shapes]
-    small_in = pl.BlockSpec((SHARD, 128), lambda i: (0, 0))
-    small_out = [
-        pl.BlockSpec((SHARD,), lambda i: (0,)), pl.BlockSpec((SHARD,), lambda i: (0,)),
-        pl.BlockSpec((EXP, SHARD), lambda i: (0, 0)), pl.BlockSpec((16, HEADS), lambda i: (0, 0)),
-    ]
     small = (sds((SHARD,), F32), sds((SHARD,), F32), sds((EXP, SHARD), F32), sds((16, HEADS), F32))
+    final = shapes[:4] + small + (sds((D, HF), F32), sds((HF, D), F32))
     mixed, grad_tokens, grad_qkv, grad_proj, grad_gain_attn, grad_gain_moe, grad_router, grad_rel, grad_up, grad_down = (
         pl.pallas_call(
             hand_out,
-            out_shape=shapes[:4] + small + (sds((D, HF), F32), sds((HF, D), F32)),
-            grid=(steps,),
-            in_specs=tall[:4] + [small_in] + tall[5:],
-            out_specs=tall[:4] + small_out + tall[5:],
+            out_shape=final,
+            in_specs=[hbm] * len(shapes),
+            out_specs=[hbm] * len(final),
+            scratch_shapes=[v(item.shape, item.dtype) for item in shapes + small + final[-2:]]
+            + [pltpu.SemaphoreType.DMA((2 * PARTS + 5,)), pltpu.SemaphoreType.DMA((2 * PARTS + 8,))],
             name="hand_out",
         )(*out)
     )

time: 180 us -> 173 us (0.961)
  Pallas kernels: 179 us -> 172 us
    pallas_call x1, Pallas kernels: 171 us -> 165 us  [body_fast(): pl.pallas_call(layer, out_shape=shapes, in_specs=[hbm, hbm, pl.BlockSpec(...]
where the time goes in v5:
time: 173 us
  Pallas kernels  172 us (99%)
    pallas_call x1, Pallas kernels, body_fast(): pl.pallas_call(layer, out_shape=shapes, in_specs=[hbm, hbm, pl.BlockSpec(...  165 us
    pallas_call x1, Pallas kernels, body_fast(): pl.pallas_call(hand_out, out_shape=final, in_specs=[hbm] * len(shapes), o...  6.59 us

profile of v5, /device:TPU:0, one launch (start us, length us, event | category | flops | bytes accessed | tf_op | source)
XLA Modules:
  0.0 172.6 jit_solution(13123572822315542532)
XLA Ops:
  0.6 165.1 %layer.1 = (bf16[256,768]{1,0:T(8,128)(2,1)}, f32[256,768]{1,0:T(8,128)}, f32[96,2304]{1,0:T(8,128)}, f32[96,768]{1,0:T(8,128)}, f32[96,128]{1,0:T(8,128)}, /*in...) custom-call(bf16[256,768]{1,0:T(8,128)(2,1)} %x_in.1, bf16[256,768]{1,0:T(8,128)(2,1)} %cot_in.1, s32[2]{0:T(128)} %lengths.1, ...), custom_call_target="tpu_custom_call" | custom-call | tf_op jit(solution)/shard_map/layer/pallas_call | solution.py:960
  165.8 6.6 %hand_out.1 = (bf16[256,768]{1,0:T(8,128)(2,1)}, f32[256,768]{1,0:T(8,128)}, f32[96,2304]{1,0:T(8,128)}, f32[96,768]{1,0:T(8,128)}, f32[96]{0:T(128)}, /*index=5...) custom-call(bf16[256,768]{1,0:T(8,128)(2,1)} %get-tuple-element.27.mixed, ...), custom_call_target="tpu_custom_call" | custom-call | tf_op jit(solution)/shard_map/hand_out/pallas_call | solution.py:992

commit v6 on v5

--- a/solution.py
+++ b/solution.py
@@ -334,8 +334,8 @@
 TILE = 512
 Z_ROWS, Y_ROWS, Y_PART, Z_BACK = 80, 88, 96, 104
 TWIN_W, FACE_W, TWIN_OUT = 112, 114, 120
-RS_TWIN, RS_Y, RS_Z, RS_FACE, RS_OUT = 126, 131, 147, 179, 183
-LINKS = 191
+RS_TWIN, RS_Y, RS_Z, RS_FACE, RS_OUT = 126, 131, 151, 191, 196
+LINKS = 206
 
 
 def quarter(zs):
@@ -449,7 +449,6 @@
     merge(0, 2)
     compute(1, 2)
     give_part(1, 2)
-    merge(1, 1)
     compute(1, 3)
     give_part(1, 3)
     give_part(0, 0)
@@ -484,15 +483,16 @@
 
     tiles(down_tile, 1 - c, w_down[1])
     sent = links.go(None, w_down[1], w_down[2], TWIN_W, TWIN_W, twin)
-    merge(0, 3)
+    merge(1, 1)
     tiles(down_tile, c, w_down[0])
     spread(0, sent)
-    merge(1, 2)
+    merge(0, 3)
     tiles(up_tile, 1 - c, w_up[1])
     sent = links.go(None, w_up[1], w_up[2], TWIN_W + 1, TWIN_W + 1, twin)
-    merge(1, 3)
+    merge(1, 2)
     tiles(up_tile, c, w_up[0])
     spread(1, sent)
+    merge(1, 3)
     merge(0, 0)
     merge(1, 0)
     for kind in range(2):
@@ -631,17 +631,20 @@
 
 HC = D // 2
 SMALLS = SENTC - 128
+STRAIGHT = (0, 1, 2, 3, 4)
 
 
 def portions(group):
     if group == 0:
         return 1, 2 * HC, HC, ((0, HC, lambda core: 3 * D + core * HC, lambda core: core * HC),)
+    if group == 4:
+        return 0, SMALLS, 128, ()
     t = group - 1
     both = (
         (0, 256, lambda core: core * D + 256 * t, lambda core: core * D + 256 * t),
         (256, 128, lambda core: 2 * D + 256 * t + 128 * core, lambda core: 2 * D + 256 * t + 128 * core),
     )
-    return 0, (0, HC, 3 * HC)[t], HC + 128 * (t == 2), both
+    return 0, (0, HC, 3 * HC)[t], HC, both
 
 
 class Reduction:
@@ -649,7 +652,6 @@
         self.links, self.group = links, group
         which, first, width, portion = portions(group)
         self.cols = slice(first, first + width)
-        self.core_cols = slice(first, first + HC)
         self.portion = [(slice(first + at, first + at + wide), wide, rhs, target) for at, wide, rhs, target in portion]
         self.lhs, self.rb, self.small_t = left.at[which], rb, small_t
         self.give, self.take, self.total = give, take, total
@@ -673,17 +675,18 @@
     def form(self):
         x, c, z, y = self.place
         self.tile(1 - c, self.give)
-        self.sent = [self.to_twin(self.core_cols, RS_TWIN + self.group)]
+        self.to_twin()
         self.tile(c, self.total)
 
-    def to_twin(self, cols, slot):
-        return self.links.go(None, self.give.at[:, cols], self.take.at[:, cols], slot, slot, self.twin)
+    def to_twin(self):
+        slot, cols = RS_TWIN + self.group, self.cols
+        self.sent = self.links.go(None, self.give.at[:, cols], self.take.at[:, cols], slot, slot, self.twin)
 
     def form_small(self):
-        small = jnp.transpose(self.small_t[...])
-        self.give[:, SMALLS:SENTC] = small.astype(BF16)
-        self.total[:, SMALLS:SENTC] = small.astype(BF16).astype(F32)
-        self.sent.append(self.to_twin(slice(SMALLS, SENTC), RS_TWIN + 4))
+        small = jnp.transpose(self.small_t[...]).astype(BF16)
+        self.give[:, self.cols] = small
+        self.to_twin()
+        self.total[:, self.cols] = small.astype(F32)
 
     def shard(self, zs, ys):
         return pl.ds(pl.multiple_of((zs * 2 + ys) * SHARD, 16), SHARD)
@@ -691,11 +694,8 @@
     def halve(self):
         x, c, z, y = self.place
         links, cols = self.links, self.cols
-        links.arrive(None, self.take.at[:, self.core_cols], RS_TWIN + self.group, self.twin)
-        if self.group == 3:
-            links.arrive(None, self.take.at[:, SMALLS:SENTC], RS_TWIN + 4, self.twin)
-        for copy in self.sent:
-            links.leave(copy)
+        links.arrive(None, self.take.at[:, cols], RS_TWIN + self.group, self.twin)
+        links.leave(self.sent)
         for zs in self.order:
             rows = self.shard(zs, 1 - y)
             self.give[rows, cols] = (self.total[rows, cols] + self.take[rows, cols].astype(F32)).astype(BF16)
@@ -714,6 +714,11 @@
         total[rows, cols] = total[rows, cols] + self.y_take[zs, :, cols].astype(F32)
         if k == 3:
             return
+        if self.group in STRAIGHT:
+            self.give[rows, cols] = total[rows, cols].astype(BF16)
+            base = RS_Z + self.group * 8
+            links.go(None, self.give.at[rows, cols], z_take.at[z, :, cols], base + k, base + z, device(x, c, zs, y))
+            return
         for cond, more, slot, target in (
             (zs > z, z > 0, zs, device(x, c, z + 1, y)),
             (zs < z, z < 3, 4 + zs, device(x, c, z - 1, y)),
@@ -739,8 +744,14 @@
     def face(self):
         x, c, z, y = self.place
         rows, cols = self.shard(z, y), self.cols
-        self.add_from_z(z > 0, z, rows)
-        self.add_from_z(z < 3, 4 + z, rows)
+        if self.group in STRAIGHT:
+            for d in (1, 2, 3):
+                zs = (z + d) % 4
+                self.links.arrive(None, self.z_take.at[zs, :, cols], RS_Z + self.group * 8 + zs, self.across)
+                self.total[rows, cols] = self.total[rows, cols] + self.z_take[zs, :, cols].astype(F32)
+        else:
+            self.add_from_z(z > 0, z, rows)
+            self.add_from_z(z < 3, 4 + z, rows)
         self.face_give[:, cols] = self.total[rows, cols].astype(BF16)
         slot = RS_FACE + self.group
         self.links.go(None, self.face_give.at[:, cols], self.face_take.at[:, cols], slot, slot, self.facing)
@@ -756,8 +767,8 @@
             slot = RS_OUT + self.group * 2 + i
             self.links.go(None, part, there, slot, slot, self.twin)
             copies.append(pltpu.make_async_copy(part, there, local_sem.at[16 + self.group * 2 + i]))
-        if self.group == 3:
-            copies.append(pltpu.make_async_copy(self.last.at[:, SMALLS:SENTC], out_small, local_sem.at[6]))
+        if self.group == 4:
+            copies.append(pltpu.make_async_copy(self.last.at[:, cols], out_small, local_sem.at[6]))
         for copy in copies:
             copy.start()
         return copies
@@ -823,11 +834,11 @@
         pending.append(copy)
 
     put(mixed, mixed_out, 26)
-    proj, one, two, three = (
+    proj, one, two, three, small = (
         Reduction(
             links, group, left, rb, small_t, act.at[0:D, :], take, total, y_take, z_take, face_give, face_take, last
         )
-        for group in range(4)
+        for group in range(5)
     )
 
     def grads(piece):
@@ -850,17 +861,18 @@
         three.form()
         proj.chain(2)
         one.chain(0)
+        three.halve()
 
     proj.form()
     attention_backward(
         x_ref, wall, rows_t, qkv, board, hidden, normed2, rb, rel_rows, small_t, grad_tokens, proj.halve,
         (early, middle, late),
     )
-    three.form_small()
+    small.form_small()
     put(grad_tokens, tokens_out, 27)
     proj.chain(3)
     one.chain(1)
-    three.halve()
+    small.halve()
     two.chain(0)
     one.chain(2)
     grads(0)
@@ -870,21 +882,28 @@
     grads(1)
     three.chain(0)
     two.chain(2)
+    three.chain(1)
     grads(2)
     one.face()
-    three.chain(1)
+    three.chain(2)
+    small.chain(0)
     two.chain(3)
+    small.chain(1)
+    small.chain(2)
     grads(3)
-    three.chain(2)
+    publish(proj)
     two.face()
     grads(4)
     three.chain(3)
+    small.chain(3)
     grads(5)
+    publish(one)
     three.face()
-    items = (proj, one, two, three)
-    for item in items:
-        publish(item)
-    for item in items:
+    small.face()
+    publish(two)
+    publish(three)
+    publish(small)
+    for item in (proj, one, two, three):
         item.landed()
     expert_grads_arrive(links, out_down, out_up)
     for copy in pending:

time: 173 us -> 169 us (0.977)
  Pallas kernels: 172 us -> 168 us
    pallas_call x1, Pallas kernels: 165 us -> 162 us  [body_fast(): pl.pallas_call(layer, out_shape=shapes, in_specs=[hbm, hbm, pl.BlockSpec(...]
where the time goes in v6:
time: 169 us
  Pallas kernels  168 us (99%)
    pallas_call x1, Pallas kernels, body_fast(): pl.pallas_call(layer, out_shape=shapes, in_specs=[hbm, hbm, pl.BlockSpec(...  162 us
    pallas_call x1, Pallas kernels, body_fast(): pl.pallas_call(hand_out, out_shape=final, in_specs=[hbm] * len(shapes), o...  6.59 us

profile of v6, /device:TPU:0, one launch (start us, length us, event | category | flops | bytes accessed | tf_op | source)
XLA Modules:
  0.0 169.2 jit_solution(5858961924022914883)
XLA Ops:
  0.6 161.8 %layer.1 = (bf16[256,768]{1,0:T(8,128)(2,1)}, f32[256,768]{1,0:T(8,128)}, f32[96,2304]{1,0:T(8,128)}, f32[96,768]{1,0:T(8,128)}, f32[96,128]{1,0:T(8,128)}, /*in...) custom-call(bf16[256,768]{1,0:T(8,128)(2,1)} %x_in.1, bf16[256,768]{1,0:T(8,128)(2,1)} %cot_in.1, s32[2]{0:T(128)} %lengths.1, ...), custom_call_target="tpu_custom_call" | custom-call | tf_op jit(solution)/shard_map/layer/pallas_call | solution.py:979
  162.5 6.6 %hand_out.1 = (bf16[256,768]{1,0:T(8,128)(2,1)}, f32[256,768]{1,0:T(8,128)}, f32[96,2304]{1,0:T(8,128)}, f32[96,768]{1,0:T(8,128)}, f32[96]{0:T(128)}, /*index=5...) custom-call(bf16[256,768]{1,0:T(8,128)(2,1)} %get-tuple-element.27.mixed, ...), custom_call_target="tpu_custom_call" | custom-call | tf_op jit(solution)/shard_map/hand_out/pallas_call | solution.py:1011

commit v7 on v6

--- a/solution.py
+++ b/solution.py
@@ -274,7 +274,8 @@
 
 
 def attention_forward(
-    later, x_ref, cot, lengths, columns, wall, rows_t, board, normed, qkv, attended, hidden, normed2, gates, out_f, out_g
+    later, dispatch, x_ref, cot, lengths, columns, wall, rows_t, board, normed, qkv, attended, hidden, normed2, gates,
+    out_f, out_g,
 ):
     rows_t[...] = jnp.transpose(wall[:, SMALL : SMALL + 128].astype(F32))[0:8]
     build_bias(wall, board)
@@ -284,58 +285,71 @@
     qkv[:, LEFTC : 3 * D] = dot(normed[...], wall[:, HIGH:WALL]).astype(BF16)
     lane = lax.broadcasted_iota(jnp.int32, (2 * SEQ, 128), 1)
 
-    def pair(p, carry):
+    def pair(s, p):
         blocks = pl.ds(pl.multiple_of(p * 2 * SEQ, SEQ), 2 * SEQ)
-        for s in range(MB):
-            rows = slice(s * SEQ, (s + 1) * SEQ)
-            q = qkv[rows, pl.ds(pl.multiple_of(p * 128, 128), 128)]
-            k = qkv[rows, pl.ds(pl.multiple_of(D + p * 128, 128), 128)]
-            v = qkv[rows, pl.ds(pl.multiple_of(2 * D + p * 128, 128), 128)]
-            scores = jnp.where(lane < lengths[s], dot(heads(q), k, 1, 1) * SCALE + board[blocks, 0:SEQ], NEG)
-            scores = jnp.exp(scores - jnp.max(scores, axis=-1, keepdims=True))
-            share = scores * (1.0 / jnp.sum(scores, axis=-1, keepdims=True))
-            board[blocks, (1 + s) * SEQ : (2 + s) * SEQ] = share
-            attended[rows, pl.ds(pl.multiple_of(p * 128, 128), 128)] = dot(
-                beside(share.astype(BF16)), heads(v)
-            ).astype(BF16)
-        return carry
-
-    for t in range(3):
-        later[t]()
-        lax.fori_loop(2 * t, 2 * t + 2, pair, 0)
-    later[3]()
-    branch = dot(attended[...], wall[:, PROJ:HIGH])
-    for s in range(MB):
+        rows = slice(s * SEQ, (s + 1) * SEQ)
+        q = qkv[rows, pl.ds(pl.multiple_of(p * 128, 128), 128)]
+        k = qkv[rows, pl.ds(pl.multiple_of(D + p * 128, 128), 128)]
+        v = qkv[rows, pl.ds(pl.multiple_of(2 * D + p * 128, 128), 128)]
+        scores = jnp.where(lane < lengths[s], dot(heads(q), k, 1, 1) * SCALE + board[blocks, 0:SEQ], NEG)
+        scores = jnp.exp(scores - jnp.max(scores, axis=-1, keepdims=True))
+        share = scores * (1.0 / jnp.sum(scores, axis=-1, keepdims=True))
+        board[blocks, (1 + s) * SEQ : (2 + s) * SEQ] = share
+        attended[rows, pl.ds(pl.multiple_of(p * 128, 128), 128)] = dot(
+            beside(share.astype(BF16)), heads(v)
+        ).astype(BF16)
+
+    def pairs(s, first, last):
+        def step(i, carry):
+            pair(s, 2 * i)
+            pair(s, 2 * i + 1)
+            return carry
+
+        lax.fori_loop(first, last, step, 0)
+
+    def finish(s):
         rows = slice(s * SEQ, (s + 1) * SEQ)
         live = live_column(lengths, s)
-        state = x_ref[rows, :].astype(F32) + jnp.where(live, branch[rows, :], 0.0)
+        branch = dot(attended[rows, :], wall[:, PROJ:HIGH])
+        state = x_ref[rows, :].astype(F32) + jnp.where(live, branch, 0.0)
         hidden[rows, :] = state
         low = (state * unit(state) * rows_t[1:2, :]).astype(BF16)
         normed2[rows, :] = low
+        first, second = routing(columns, s)
+        first = jnp.where(first & live, 1.0, 0.0).astype(BF16)
+        second = jnp.where(second & live, 1.0, 0.0).astype(BF16)
+        sent = dot(first + second, low, 0, 0).astype(BF16)
+        for e in range(EXP):
+            out_f[e, s * CAP : (s + 1) * CAP, :] = sent[e * CAP : (e + 1) * CAP, :]
+        dispatch(s)
         logits = dot(low, wall[:, SMALL : SMALL + 128])
         one, two = named(columns, s)
         picked = jnp.where(one, logits, 0.0) - jnp.where(two, logits, 0.0)
         gate = jax.nn.sigmoid(jnp.sum(picked, axis=-1, keepdims=True))
         gates[rows, :] = gate
         grad = jnp.where(live, cot[rows, :].astype(F32), 0.0)
-        first, second = routing(columns, s)
-        first = jnp.where(first & live, 1.0, 0.0).astype(BF16)
-        second = jnp.where(second & live, 1.0, 0.0).astype(BF16)
-        sent = dot(first + second, low, 0, 0).astype(BF16)
         back = dot(first, (gate * grad).astype(BF16), 0, 0) + dot(
             second, ((1.0 - gate) * grad).astype(BF16), 0, 0
         )
         back = back.astype(BF16)
         for e in range(EXP):
-            out_f[e, s * CAP : (s + 1) * CAP, :] = sent[e * CAP : (e + 1) * CAP, :]
             out_g[e, s * CAP : (s + 1) * CAP, :] = back[e * CAP : (e + 1) * CAP, :]
+
+    for t in range(3):
+        later[t]()
+        pairs(0, t, t + 1)
+    later[3]()
+    finish(0)
+    pairs(1, 0, 3)
+    finish(1)
 
 
 TILE = 512
 Z_ROWS, Y_ROWS, Y_PART, Z_BACK = 80, 88, 96, 104
 TWIN_W, FACE_W, TWIN_OUT = 112, 114, 120
 RS_TWIN, RS_Y, RS_Z, RS_FACE, RS_OUT = 126, 131, 151, 191, 196
-LINKS = 206
+Z_FIRST, Y_FIRST = 206, 214
+LINKS = 216
 
 
 def quarter(zs):
@@ -379,11 +393,27 @@
     part[zs, 1] = got[ROWS : 2 * ROWS]
 
 
+def one_sequence(zs, ys, s):
+    return pl.ds(pl.multiple_of((zs * 2 + ys) * ROWS + s * CAP, CAP), CAP)
+
+
+def dispatch_forward(links, out, recv, s):
+    x, c, z, y = place()
+    rows = slice(s * CAP, (s + 1) * CAP)
+    there = recv.at[one_sequence(z, y, s), :]
+    links.go(None, out.at[z, rows, :], there, Y_FIRST + s, Y_FIRST + s, device(x, c, z, 1 - y))
+    for d in (1, 2, 3):
+        to = (z + d) % 4
+        slot = Z_FIRST + s * 4
+        links.go(None, out.at[to, rows, :], there, slot + d, slot + z, device(x, c, to, y))
+    recv[one_sequence(z, y, s), :] = out[z, rows, :]
+
+
 def experts(links, out, recv, up, down, act, slope, part, take, back, w_down, w_up):
     x, c, z, y = place()
     across, facing, twin = device(x, c, z, 1 - y), device(1 - x, c, z, y), device(x, 1 - c, z, y)
 
-    for kind in range(2):
+    for kind in (1,):
         links.go(None, out[kind].at[z], recv[kind].at[half_rows(z, y), :], Y_ROWS + kind * 4, Y_ROWS + kind * 4 + z, across)
         for d in (1, 2, 3):
             to = (z + d) % 4
@@ -399,12 +429,20 @@
     def reach(kind, d):
         zs = source(d)
         rows = recv[kind].at[half_rows(zs, y), :]
-        links.arrive(None, rows, Z_ROWS + kind * 4 + zs, across)
+        if kind == 0:
+            for s in range(MB):
+                links.arrive(None, recv[0].at[one_sequence(zs, y, s), :], Z_FIRST + s * 4 + zs, across)
+        else:
+            links.arrive(None, rows, Z_ROWS + kind * 4 + zs, across)
         links.go(None, rows, rows, Y_ROWS + kind * 4 + d, Y_ROWS + kind * 4 + zs, across)
 
     def compute(kind, d):
         zs = source(d)
-        links.arrive(None, recv[kind].at[half_rows(zs, 1 - y), :], Y_ROWS + kind * 4 + zs, across)
+        if kind == 0 and d == 0:
+            for s in range(MB):
+                links.arrive(None, recv[0].at[one_sequence(z, 1 - y, s), :], Y_FIRST + s, across)
+        else:
+            links.arrive(None, recv[kind].at[half_rows(zs, 1 - y), :], Y_ROWS + kind * 4 + zs, across)
         if kind == 0:
             expert_forward(zs, recv[0], up, down, act, slope, part[0])
         else:
@@ -816,7 +854,8 @@
         copy.wait()
     normed, attended = left.at[0], left.at[1]
     attention_forward(
-        later, x_ref, cot, lengths, columns, wall, rows_t, board, normed, qkv, attended, hidden, normed2, gates, out_f, out_g
+        later, functools.partial(dispatch_forward, links, out_f, recv_f), x_ref, cot, lengths, columns, wall, rows_t, board, normed, qkv, attended, hidden, normed2, gates,
+        out_f, out_g,
     )
     for copy in fetch:
         copy.wait()

time: 169 us -> 167 us (0.988)
  Pallas kernels: 168 us -> 166 us
    pallas_call x1, Pallas kernels: 162 us -> 160 us  [body_fast(): pl.pallas_call(layer, out_shape=shapes, in_specs=[hbm, hbm, pl.BlockSpec(...]
where the time goes in v7:
time: 167 us
  Pallas kernels  166 us (99%)
    pallas_call x1, Pallas kernels, body_fast(): pl.pallas_call(layer, out_shape=shapes, in_specs=[hbm, hbm, pl.BlockSpec(...  160 us
    pallas_call x1, Pallas kernels, body_fast(): pl.pallas_call(hand_out, out_shape=final, in_specs=[hbm] * len(shapes), o...  6.59 us

profile of v7, /device:TPU:0, one launch (start us, length us, event | category | flops | bytes accessed | tf_op | source)
XLA Modules:
  0.0 167.1 jit_solution(17974879343215580022)
XLA Ops:
  0.6 159.7 %layer.1 = (bf16[256,768]{1,0:T(8,128)(2,1)}, f32[256,768]{1,0:T(8,128)}, f32[96,2304]{1,0:T(8,128)}, f32[96,768]{1,0:T(8,128)}, f32[96,128]{1,0:T(8,128)}, /*in...) custom-call(bf16[256,768]{1,0:T(8,128)(2,1)} %x_in.1, bf16[256,768]{1,0:T(8,128)(2,1)} %cot_in.1, s32[2]{0:T(128)} %lengths.1, ...), custom_call_target="tpu_custom_call" | custom-call | tf_op jit(solution)/shard_map/layer/pallas_call | solution.py:1018
  160.3 6.6 %hand_out.1 = (bf16[256,768]{1,0:T(8,128)(2,1)}, f32[256,768]{1,0:T(8,128)}, f32[96,2304]{1,0:T(8,128)}, f32[96,768]{1,0:T(8,128)}, f32[96]{0:T(128)}, /*index=5...) custom-call(bf16[256,768]{1,0:T(8,128)(2,1)} %get-tuple-element.27.mixed, ...), custom_call_target="tpu_custom_call" | custom-call | tf_op jit(solution)/shard_map/hand_out/pallas_call | solution.py:1050

commit v8 on v7

--- a/solution.py
+++ b/solution.py
@@ -349,7 +349,8 @@
 TWIN_W, FACE_W, TWIN_OUT = 112, 114, 120
 RS_TWIN, RS_Y, RS_Z, RS_FACE, RS_OUT = 126, 131, 151, 191, 196
 Z_FIRST, Y_FIRST = 206, 214
-LINKS = 216
+RS_PART = 216
+LINKS = 226
 
 
 def quarter(zs):
@@ -532,11 +533,15 @@
     spread(1, sent)
     merge(1, 3)
     merge(0, 0)
-    merge(1, 0)
-    for kind in range(2):
+
+    def returned(kind):
+        if kind == 1:
+            merge(1, 0)
         for d in (1, 2, 3):
             zs = source(d)
             links.arrive(None, back[kind].at[zs], Z_BACK + kind * 4 + zs, across)
+
+    return returned
 
 
 def expert_grad_out(links, piece, w_down, w_up, out_down, out_up, local_sem):
@@ -566,9 +571,11 @@
 SENTC = 2 * D + 128
 
 
-def combine(cot, lengths, columns, rows_t, hidden, normed2, gates, back_f, back_g, mixed, rb, small_t):
+def combine(returned, cot, lengths, columns, rows_t, hidden, normed2, gates, back_f, back_g, mixed, rb, small_t):
     gain_grad = jnp.zeros((1, D), F32)
     router_grad = jnp.zeros((128, D), F32)
+    kept = []
+    returned(0)
     for s in range(MB):
         rows = slice(s * SEQ, (s + 1) * SEQ)
         live = live_column(lengths, s)
@@ -579,11 +586,9 @@
         first_out = dot(first, given)
         second_out = dot(second, given)
         gate = gates[rows, :]
-        grad = cot[rows, :].astype(F32)
-        grad_live = jnp.where(live, grad, 0.0)
-        state = hidden[rows, :]
+        grad_live = jnp.where(live, cot[rows, :].astype(F32), 0.0)
         moe = gate * first_out + (1.0 - gate) * second_out
-        mixed[rows, :] = (state + jnp.where(live, moe, 0.0)).astype(BF16)
+        mixed[rows, :] = (hidden[rows, :] + jnp.where(live, moe, 0.0)).astype(BF16)
         tilt = jnp.sum(grad_live * first_out, axis=-1, keepdims=True) - jnp.sum(
             grad_live * second_out, axis=-1, keepdims=True
         )
@@ -594,16 +599,22 @@
         high = grad_logits.astype(BF16)
         low = (grad_logits - high.astype(F32)).astype(BF16)
         router_grad = router_grad + dot(high, normed2[rows, :], 0, 0) + dot(low, normed2[rows, :], 0, 0)
+        kept.append((live, first + second, grad_logits))
+    returned(1)
+    for s in range(MB):
+        rows = slice(s * SEQ, (s + 1) * SEQ)
+        live, either, grad_logits = kept[s]
         given = jnp.concatenate([back_g[e, s * CAP : (s + 1) * CAP, :] for e in range(EXP)], axis=0)
-        grad_low = jnp.where(live, dot(first + second, given), 0.0)
+        grad_low = jnp.where(live, dot(either, given), 0.0)
         for e in range(EXP):
             grad_low = grad_low + grad_logits[:, 2 + e : 3 + e] * rows_t[2 + e : 3 + e, :]
+        state = hidden[rows, :]
         factor = unit(state)
         scaled = state * factor
         gain_grad = gain_grad + jnp.sum(grad_low * scaled, axis=0, keepdims=True)
         grad_low = grad_low * rows_t[1:2, :]
         inner = jnp.mean(grad_low * scaled, axis=-1, keepdims=True)
-        grad_state = grad + factor * (grad_low - scaled * inner)
+        grad_state = cot[rows, :].astype(F32) + factor * (grad_low - scaled * inner)
         hidden[rows, :] = grad_state
         rb[rows, 3 * D : 4 * D] = jnp.where(live, grad_state, 0.0).astype(BF16)
     small_t[...] = router_grad
@@ -700,30 +711,40 @@
         near = z + mirror * (3 - 2 * z)
         self.order = [o + mirror * (3 - 2 * o) for o in (3, 2, 1 - near, near)]
 
-    def tile(self, core, keep):
-        def step(m, carry):
-            rows = pl.ds(pl.multiple_of(m * 256, 256), 256)
-            for cols, wide, rhs, target in self.portion:
-                right = self.rb[:, pl.ds(pl.multiple_of(rhs(core), 128), wide)]
-                keep[rows, cols] = dot(self.lhs[:, rows], right, 0, 0).astype(keep.dtype)
-            return carry
-
-        lax.fori_loop(0, 3, step, 0)
+    def tile(self, core, keep, rows):
+        for cols, wide, rhs, target in self.portion:
+            right = self.rb[:, pl.ds(pl.multiple_of(rhs(core), 128), wide)]
+            keep[rows, cols] = dot(self.lhs[:, rows], right, 0, 0).astype(keep.dtype)
 
     def form(self):
         x, c, z, y = self.place
-        self.tile(1 - c, self.give)
-        self.to_twin()
-        self.tile(c, self.total)
-
-    def to_twin(self):
-        slot, cols = RS_TWIN + self.group, self.cols
-        self.sent = self.links.go(None, self.give.at[:, cols], self.take.at[:, cols], slot, slot, self.twin)
+        self.sent = []
+        for m in range(3):
+            self.tile(1 - c, self.give, self.third(m))
+            self.to_twin(self.third(m), self.slots()[m])
+
+        def own(m, carry):
+            self.tile(c, self.total, pl.ds(pl.multiple_of(m * 256, 256), 256))
+            return carry
+
+        lax.fori_loop(0, 3, own, 0)
+
+    def third(self, m):
+        return slice(m * 256, (m + 1) * 256)
+
+    def slots(self):
+        return RS_TWIN + self.group, RS_PART + self.group * 2, RS_PART + self.group * 2 + 1
+
+    def to_twin(self, rows, slot):
+        cols = self.cols
+        self.sent.append(self.links.go(None, self.give.at[rows, cols], self.take.at[rows, cols], slot, slot, self.twin))
 
     def form_small(self):
         small = jnp.transpose(self.small_t[...]).astype(BF16)
         self.give[:, self.cols] = small
-        self.to_twin()
+        self.sent = []
+        for m in range(3):
+            self.to_twin(self.third(m), self.slots()[m])
         self.total[:, self.cols] = small.astype(F32)
 
     def shard(self, zs, ys):
@@ -732,8 +753,10 @@
     def halve(self):
         x, c, z, y = self.place
         links, cols = self.links, self.cols
-        links.arrive(None, self.take.at[:, cols], RS_TWIN + self.group, self.twin)
-        links.leave(self.sent)
+        for m in range(3):
+            links.arrive(None, self.take.at[self.third(m), cols], self.slots()[m], self.twin)
+        for copy in self.sent:
+            links.leave(copy)
         for zs in self.order:
             rows = self.shard(zs, 1 - y)
             self.give[rows, cols] = (self.total[rows, cols] + self.take[rows, cols].astype(F32)).astype(BF16)
@@ -860,11 +883,11 @@
     for copy in fetch:
         copy.wait()
     downs, ups = (dn_own, dn_give, dn_take, dn_face), (up_own, up_give, up_take, up_face)
-    experts(
+    returned = experts(
         links, (out_f, out_g), (recv_f, recv_g), up, down, act, slope, (part_f, part_g), (take_f, take_g),
         (back_f, back_g), downs, ups,
     )
-    combine(cot, lengths, columns, rows_t, hidden, normed2, gates, back_f, back_g, mixed, rb, small_t)
+    combine(returned, cot, lengths, columns, rows_t, hidden, normed2, gates, back_f, back_g, mixed, rb, small_t)
     pending = []
 
     def put(src, dst, i):

time: 167 us -> 166 us (level)
  no operation moved by 1% of the time
where the time goes in v8:
time: 166 us
  Pallas kernels  165 us (99%)
    pallas_call x1, Pallas kernels, body_fast(): pl.pallas_call(layer, out_shape=shapes, in_specs=[hbm, hbm, pl.BlockSpec(...  158 us
    pallas_call x1, Pallas kernels, body_fast(): pl.pallas_call(hand_out, out_shape=final, in_specs=[hbm] * len(shapes), o...  6.59 us

profile of v8, /device:TPU:0, one launch (start us, length us, event | category | flops | bytes accessed | tf_op | source)
XLA Modules:
  0.0 165.9 jit_solution(11603295727866291280)
XLA Ops:
  0.6 158.4 %layer.1 = (bf16[256,768]{1,0:T(8,128)(2,1)}, f32[256,768]{1,0:T(8,128)}, f32[96,2304]{1,0:T(8,128)}, f32[96,768]{1,0:T(8,128)}, f32[96,128]{1,0:T(8,128)}, /*in...) custom-call(bf16[256,768]{1,0:T(8,128)(2,1)} %x_in.1, bf16[256,768]{1,0:T(8,128)(2,1)} %cot_in.1, s32[2]{0:T(128)} %lengths.1, ...), custom_call_target="tpu_custom_call" | custom-call | tf_op jit(solution)/shard_map/layer/pallas_call | solution.py:1041
  159.1 6.6 %hand_out.1 = (bf16[256,768]{1,0:T(8,128)(2,1)}, f32[256,768]{1,0:T(8,128)}, f32[96,2304]{1,0:T(8,128)}, f32[96,768]{1,0:T(8,128)}, f32[96]{0:T(128)}, /*index=5...) custom-call(bf16[256,768]{1,0:T(8,128)(2,1)} %get-tuple-element.27.mixed, ...), custom_call_target="tpu_custom_call" | custom-call | tf_op jit(solution)/shard_map/hand_out/pallas_call | solution.py:1073
